TPU v7x, 128 devices: a whole 4x4x4 slice. The times are simulated.
128 devices in a mesh: inline: 16 (over x, y), crosslin: 8 (over z, core).
Axes of the slice: x: 4, y: 4, z: 4, core: 2. Of those that a mesh axis runs over, the one named last changes fastest.
Arguments:
- traces: float32 [16384, 4, 1024], P(('inline', 'crosslin')), may hold values from -6 to 6
- destination: int32 [16384, 1], P(('inline', 'crosslin')), may hold values from 0 to 127; in each aligned block of 128 rows (0 to 127, 128 to 255, ...) at most 2 rows name the same one
- bin_index: int32 [16384, 4], P(('inline', 'crosslin')), may hold values from 0 to 1023
- dip_inline: int32 [512, 256], P('inline', 'crosslin'), may hold values from -2 to 2
- dip_cross: int32 [512, 256], P('inline', 'crosslin'), may hold values from -2 to 2
Outputs:
- smoothed: float32 [512, 256, 1024], P('inline', 'crosslin')
Inputs may be any that keep to these rules, and one draw needn't show every extreme that they name: `destination`: at most 2 of one device's blocks name the same tile, and that many are reached.
All inputs are finite; a program needn't handle non-finite values.
Results may differ from a plain program's by a relative error of at most 0.00009.
Values sent between devices are 32-bit elements; how exact they have to be, the bound alone decides.
A program may use at most 64 MiB of HBM per device.

v0:
```python
import jax
import jax.numpy as jnp
from jax import lax
from jax.sharding import PartitionSpec as P

HALF = 7
DMAX = 2


def padded_2(cells, sides, width):
    for axis, dim in sides:
        count = lax.axis_size(axis)
        ends = count - 1
        head = lax.slice_in_dim(cells, 0, width, axis=dim)
        tail = lax.slice_in_dim(cells, cells.shape[dim] - width, cells.shape[dim], axis=dim)
        cells = jnp.concatenate(
            [
                lax.ppermute(tail, axis, [(i, (i + 1) % count) for i in range(ends)]),
                cells,
                lax.ppermute(head, axis, [((i + 1) % count, i) for i in range(ends)]),
            ],
            axis=dim,
        )
    return cells


def steer(padded, dip_index, along_dim):
    margin = HALF * DMAX
    samples = padded.shape[-1] - 2 * margin
    extent = padded.shape[along_dim] - 2 * HALF
    result = jnp.zeros(dip_index.shape + (samples,), jnp.float32)
    for dip_value in range(-DMAX, DMAX + 1):
        running = jnp.zeros(dip_index.shape + (samples,), jnp.float32)
        for offset in range(-HALF, HALF + 1):
            weight = (HALF + 1 - abs(offset)) / float((HALF + 1) ** 2)
            shifted = lax.slice_in_dim(
                padded, HALF + offset, HALF + offset + extent, axis=along_dim
            )
            begin = margin + dip_value * offset
            shifted = shifted[..., begin : begin + samples]
            running = running + weight * shifted
        result = jnp.where((dip_index == dip_value)[..., None], running, result)
    return result


def pad_time(gridded):
    margin = HALF * DMAX
    return jnp.pad(gridded, ((0, 0), (0, 0), (margin, margin)))


def smooth_inline(gridded, dip_index):
    padded = padded_2(pad_time(gridded), (("inline", 0),), HALF)
    return steer(padded, dip_index, 0)


def smooth_cross(gridded, dip_index):
    padded = padded_2(pad_time(gridded), (("crosslin", 1),), HALF)
    return steer(padded, dip_index, 1)


def on_device(traces, destination, bin_index, dip_inline, dip_cross):
    held_blocks, block_rows, samples = traces.shape
    rows_inline = lax.axis_size("inline")
    cols_cross = lax.axis_size("crosslin")
    devices = rows_inline * cols_cross
    capacity = 2 * held_blocks // devices
    tile_rows, tile_cols = dip_inline.shape
    bin_total = tile_rows * tile_cols
    target = destination[:, 0]
    positions = jnp.arange(held_blocks, dtype=jnp.int32)
    earlier = (target[:, None] == target[None, :]) & (positions[None, :] < positions[:, None])
    ranking = jnp.sum(earlier.astype(jnp.int32), axis=1)
    slot_index = target * capacity + ranking
    slot_range = jnp.arange(devices * capacity, dtype=jnp.int32)
    matches = slot_range[:, None] == slot_index[None, :]
    source = jnp.sum(jnp.where(matches, positions[None, :], 0), axis=1)
    filled = jnp.any(matches, axis=1)
    outgoing = jnp.where(filled[:, None, None], traces[source], 0.0)
    outgoing_bins = jnp.where(filled[:, None], bin_index[source], bin_total)
    outgoing = outgoing.reshape(devices, capacity, block_rows, samples)
    outgoing_bins = outgoing_bins.reshape(devices, capacity, block_rows)
    arrived, arrived_bins = (
        lax.all_to_all(outgoing, ("inline", "crosslin"), split_axis=0, concat_axis=0, tiled=True),
        lax.all_to_all(
            outgoing_bins, ("inline", "crosslin"), split_axis=0, concat_axis=0, tiled=True
        ),
    )
    arrived_rows = arrived.reshape(-1, samples)
    arrived_bins = arrived_bins.reshape(-1)
    member = (jnp.arange(bin_total, dtype=jnp.int32)[:, None] == arrived_bins[None, :]).astype(
        jnp.float32
    )
    summed = jnp.dot(
        member, arrived_rows, precision=lax.Precision.HIGHEST, preferred_element_type=jnp.float32
    )
    fold_count = jnp.sum(member, axis=1)
    stacked = (summed / jnp.maximum(fold_count, 1.0)[:, None]).reshape(
        tile_rows, tile_cols, samples
    )
    first_pass = smooth_inline(stacked, dip_inline)
    second_pass = smooth_cross(first_pass, dip_cross)
    return smooth_inline(second_pass, dip_inline)


def solution(mesh):
    return jax.shard_map(
        on_device,
        mesh=mesh,
        in_specs=(
            P(("inline", "crosslin"), None, None),
            P(("inline", "crosslin"), None),
            P(("inline", "crosslin"), None),
            P("inline", "crosslin"),
            P("inline", "crosslin"),
        ),
        out_specs=P("inline", "crosslin", None),
        check_vma=False,
    )
```

profile of v0, /device:TPU:56, one launch (start us, length us, event | category | flops | bytes accessed | tf_op | source)
XLA Modules:
  0.0 800.4 jit_solution(15141590374692662098)
XLA Ops:
  0.0 1.0 convert_reduce_fusion.1
  1.0 0.7 multiply_add_fusion
  1.9 0.8 copy.27
  2.9 0.7 gather_fusion
  3.6 0.8 broadcast_select_fusion.1
  4.5 10.1 %all-to-all-start = ((s32[128,2,4]{2,1,0:T(2,128)}), s32[128,2,4]{2,1,0:T(2,128)S(1)}, u32[]{:S(2)}, u32[]{:S(2)}) async-start(s32[128,2,4]{2,1,0:T(2,128)} %broadcast_select_fusion.1), calls=%async_computation | async-start | bytes 262144 | tf_op jit(solution)/shard_map/all_to_all | solution.py:84
  14.6 4.8 gather_fusion.1
  19.4 4.1 broadcast_select_fusion
  23.5 10.2 %all-to-all-start.1 = ((f32[128,2,4,1024]{3,2,1,0:T(4,128)}), f32[128,2,4,1024]{3,2,1,0:T(4,128)}, u32[]{:S(2)}, u32[]{:S(2)}) async-start(f32[128,2,4,1024]{3,2,1,0:T(4,128)} %broadcast_select_fusion), calls=%async_computation.1 | async-start | bytes 8388608 | tf_op jit(solution)/shard_map/all_to_all | solution.py:83
  34.4 47.9 %all-to-all-done.1 = f32[128,2,4,1024]{3,2,1,0:T(4,128)} async-done(((f32[128,2,4,1024]{3,2,1,0:T(4,128)}), f32[128,2,4,1024]{3,2,1,0:T(4,128)}, u32[]{:S(2)}, u32[]{:S(2)}) %all-to-all-start.1) | async-done | bytes 4194336 | tf_op jit(solution)/shard_map/all_to_all | solution.py:83
  82.4 5.3 reshape.55
  87.6 9.7 %broadcast_divide_fusion = f32[1024,1024]{1,0:T(8,128)S(1)} fusion(f32[1024]{0:T(1024)S(1)} %broadcast_maximum_fusion, f32[1024,1024]{1,0:T(8,128)} %reshape.55, s32[1024]{0:T(1024)S(1)} %eq.85), kind=kOutput, calls=%fused_computation.1058 | convolution fusion | flops 12886999040 | bytes 8396800 | tf_op jit(solution)/shard_map/dot_general | solution.py:93
  98.0 4.8 collective-permute-start
  102.8 2.4 collective-permute-start.1
  105.2 3.4 pad.10
  108.7 16.1 %collective-permute-done = f32[7,32,1052]{2,1,0:T(8,128)S(1)} collective-permute-done((f32[7,32,1052]{2,1,0:T(8,128)S(1)}, f32[7,32,1052]{2,1,0:T(8,128)S(1)}, u32[]{:S(2)}, u32[]{:S(2)}) %collective-permute-start) | collective-permute-done | bytes 942624 | tf_op jit(solution)/shard_map/ppermute | solution.py:18
  124.7 5.7 collective-permute-done.1
  130.4 177.3 %fusion.219 = f32[32,32,1024]{2,1,0:T(8,128)} fusion(f32[32,32,1052]{2,1,0:T(8,128)} %pad.10, f32[7,32,1052]{2,1,0:T(8,128)S(1)} %collective-permute-done.1, f32[7,32,1052]{2,1,0:T(8,128)S(1)} %collective-permute-done, f32[32,32,1024]{2,1,0:T(8,128)} %bitcast.10, pred[32,32]{1,0:T(8,128)(4,1)S(1)} %get-tuple-element.19, ...), kind=kLoop, calls=%fused_computation.629 | loop fusion | flops 226492416 | bytes 14587904 | tf_op jit(solution)/shard_map/jit(_where)/select_n | solution.py:42
  307.8 2.4 pad_slice_fusion.411
  310.3 1.9 collective-permute-start.2
  312.5 3.6 collective-permute-start.3
  316.2 3.4 pad.11
  319.6 6.7 collective-permute-done.2
  326.9 1.4 collective-permute-done.3
  328.9 251.4 %fusion.430 = f32[32,32,1024]{2,1,0:T(8,128)} fusion(f32[32,32,1052]{2,1,0:T(8,128)} %pad.11, f32[32,7,1052]{2,1,0:T(8,128)S(1)} %copy.31, f32[32,7,1052]{2,1,0:T(8,128)S(1)} %copy.29, f32[32,32,1024]{2,1,0:T(8,128)} %fusion.219, pred[32,32]{1,0:T(8,128)(4,1)S(1)} %get-tuple-element.14, pred[32,32]{1,0:T(8,128)(4,1)S(1)} %get-tuple-element.15, ...), kind=kLoop, calls=%fused_computation.840 | loop fusion | flops 226492416 | bytes 14587904 | tf_op jit(solution)/shard_map/jit(_where)/select_n | solution.py:42
  580.3 2.2 pad_slice_fusion.409
  582.5 1.9 collective-permute-start.4
  584.4 3.9 collective-permute-start.5
  588.4 3.4 pad.12
  591.8 18.2 %collective-permute-done.4 = f32[7,32,1052]{2,1,0:T(8,128)S(1)} collective-permute-done((f32[7,32,1052]{2,1,0:T(8,128)S(1)}, f32[7,32,1052]{2,1,0:T(8,128)S(1)}, u32[]{:S(2)}, u32[]{:S(2)}) %collective-permute-start.4) | collective-permute-done | bytes 942624 | tf_op jit(solution)/shard_map/ppermute | solution.py:18
  609.9 4.1 collective-permute-done.5
  614.1 186.1 %fusion.8 = f32[32,32,1024]{2,1,0:T(8,128)} fusion(f32[32,32,1052]{2,1,0:T(8,128)} %pad.12, f32[7,32,1052]{2,1,0:T(8,128)} %collective-permute-done.5, f32[7,32,1052]{2,1,0:T(8,128)S(1)} %collective-permute-done.4, f32[32,32,1024]{2,1,0:T(8,128)} %fusion.430, pred[32,32]{1,0:T(8,128)(4,1)S(1)} %get-tuple-element.19, ...), kind=kLoop, calls=%fused_computation.418 | loop fusion | flops 226492416 | bytes 14587904 | tf_op jit(solution)/shard_map/jit(_where)/select_n | solution.py:42
  (30 shorter events, 3.4 us)
Async XLA Ops:
  0.0 14.5 %copy-start = (f32[128,4,1024]{2,1,0:T(4,128)S(1)}, f32[128,4,1024]{2,1,0:T(4,128)}, u32[]{:S(2)}) copy-start(f32[128,4,1024]{2,1,0:T(4,128)} %param.5) | copy-start | bytes 6291460
  4.5 19.0 %all-to-all-start = ((s32[128,2,4]{2,1,0:T(2,128)}), s32[128,2,4]{2,1,0:T(2,128)S(1)}, u32[]{:S(2)}, u32[]{:S(2)}) async-start(s32[128,2,4]{2,1,0:T(2,128)} %broadcast_select_fusion.1), calls=%async_computation | async-start | bytes 262144 | tf_op jit(solution)/shard_map/all_to_all | solution.py:84
  23.5 58.9 %all-to-all-start.1 = ((f32[128,2,4,1024]{3,2,1,0:T(4,128)}), f32[128,2,4,1024]{3,2,1,0:T(4,128)}, u32[]{:S(2)}, u32[]{:S(2)}) async-start(f32[128,2,4,1024]{3,2,1,0:T(4,128)} %broadcast_select_fusion), calls=%async_computation.1 | async-start | bytes 8388608 | tf_op jit(solution)/shard_map/all_to_all | solution.py:83
  97.4 11.3 %copy-start.4 = (f32[1024,1024]{1,0:T(8,128)}, f32[1024,1024]{1,0:T(8,128)S(1)}, u32[]{:S(2)}) copy-start(f32[1024,1024]{1,0:T(8,128)S(1)} %broadcast_divide_fusion) | copy-start | bytes 12582916
  97.4 7.9 copy-start.5
  98.0 26.8 %collective-permute-start = (f32[7,32,1052]{2,1,0:T(8,128)S(1)}, f32[7,32,1052]{2,1,0:T(8,128)S(1)}, u32[]{:S(2)}, u32[]{:S(2)}) collective-permute-start(f32[7,32,1052]{2,1,0:T(8,128)S(1)} %get-tuple-element.9), channel_id=1, source_target_pairs={{0,8},{8,16},{16,24},{24,32},{32,40},{40,48},{48,56},{56,64},{64,7... | collective-permute-start | bytes 2827784 | tf_op jit(solution)/shard_map/ppermute | solution.py:18
  102.8 27.6 %collective-permute-start.1 = (f32[7,32,1052]{2,1,0:T(8,128)S(1)}, f32[7,32,1052]{2,1,0:T(8,128)S(1)}, u32[]{:S(2)}, u32[]{:S(2)}) collective-permute-start(f32[7,32,1052]{2,1,0:T(8,128)S(1)} %get-tuple-element.10), channel_id=1, source_target_pairs={{8,0},{16,8},{24,16},{32,24},{40,32},{48,40},{56,48},{64,56},{72,6... | collective-permute-start | bytes 2827784 | tf_op jit(solution)/shard_map/ppermute | solution.py:20
  307.7 8.4 %copy-start.6 = (s32[32,32]{1,0:T(8,128)S(1)}, s32[32,32]{1,0:T(8,128)}, u32[]{:S(2)}) copy-start(s32[32,32]{1,0:T(8,128)} %param.9) | copy-start | bytes 12292
  307.8 8.4 %copy-start.2 = (f32[32,32,1024]{2,1,0:T(8,128)S(1)}, f32[32,32,1024]{2,1,0:T(8,128)}, u32[]{:S(2)}) copy-start(f32[32,32,1024]{2,1,0:T(8,128)} %fusion.219) | copy-start | bytes 12582916
  310.3 15.9 %collective-permute-start.2 = (f32[32,7,1052]{2,0,1:T(8,128)S(1)}, f32[32,7,1052]{2,0,1:T(8,128)S(1)}, u32[]{:S(2)}, u32[]{:S(2)}) collective-permute-start(f32[32,7,1052]{2,0,1:T(8,128)S(1)} %copy.28), channel_id=1, source_target_pairs={{0,1},{1,2},{2,3},{3,4},{4,5},{5,6},{6,7},{8,9},{9,10},{10,11},{11... | collective-permute-start | bytes 2827784 | tf_op jit(solution)/shard_map/ppermute | solution.py:18
  312.5 15.8 %collective-permute-start.3 = (f32[32,7,1052]{2,0,1:T(8,128)S(1)}, f32[32,7,1052]{2,0,1:T(8,128)S(1)}, u32[]{:S(2)}, u32[]{:S(2)}) collective-permute-start(f32[32,7,1052]{2,0,1:T(8,128)S(1)} %copy.30), channel_id=1, source_target_pairs={{1,0},{2,1},{3,2},{4,3},{5,4},{6,5},{7,6},{9,8},{10,9},{11,10},{12... | collective-permute-start | bytes 2827784 | tf_op jit(solution)/shard_map/ppermute | solution.py:20
  580.3 8.1 %copy-start.3 = (f32[32,32,1024]{2,1,0:T(8,128)S(1)}, f32[32,32,1024]{2,1,0:T(8,128)}, u32[]{:S(2)}) copy-start(f32[32,32,1024]{2,1,0:T(8,128)} %fusion.430) | copy-start | bytes 12582916
  582.5 27.5 %collective-permute-start.4 = (f32[7,32,1052]{2,1,0:T(8,128)S(1)}, f32[7,32,1052]{2,1,0:T(8,128)S(1)}, u32[]{:S(2)}, u32[]{:S(2)}) collective-permute-start(f32[7,32,1052]{2,1,0:T(8,128)S(1)} %get-tuple-element.5), channel_id=1, source_target_pairs={{0,8},{8,16},{16,24},{24,32},{32,40},{40,48},{48,56},{56,64},{64,7... | collective-permute-start | bytes 2827784 | tf_op jit(solution)/shard_map/ppermute | solution.py:18
  584.4 29.7 %collective-permute-start.5 = (f32[7,32,1052]{2,1,0:T(8,128)S(1)}, f32[7,32,1052]{2,1,0:T(8,128)}, u32[]{:S(2)}, u32[]{:S(2)}) collective-permute-start(f32[7,32,1052]{2,1,0:T(8,128)S(1)} %get-tuple-element.6), channel_id=1, source_target_pairs={{8,0},{16,8},{24,16},{32,24},{40,32},{48,40},{56,48},{64,56},{72,6... | collective-permute-start | bytes 2827784 | tf_op jit(solution)/shard_map/ppermute | solution.py:20
  588.4 211.8 %copy-start.1 = (f32[128,4,1024]{2,1,0:T(4,128)S(1)}, f32[128,4,1024]{2,1,0:T(4,128)}, u32[]{:S(2)}) copy-start(f32[128,4,1024]{2,1,0:T(4,128)} %param.5) | copy-start | bytes 6291460
where the time goes:
time: 809 us; the launch traced here: 800 us
  other arithmetic  622 us (77%)
  waiting for transfers between devices  100 us (12%)
  starting transfers between devices  38.9 us (5%)
  local copies, waits for them, and re-layouts  29 us (4%)
  matrix products  9.72 us (1%)
    select_n x3, other arithmetic, steer(): result = jnp.where((dip_index == dip_value)[..., None], running, result)  615 us
    all_to_all x1, waiting for transfers between devices, on_device(): lax.all_to_all(outgoing, ('inline', 'crosslin'), split_axis=0, concat_axi...  47.9 us
    ppermute x3, waiting for transfers between devices, padded_2(): lax.ppermute(tail, axis, [(i, (i + 1) % count) for i in range(ends)])  40.9 us
  transfers between devices with their start and end apart: 8, of which 7 were waited for; matrix products, arithmetic and copies ran while one was open for 3% of the time, Pallas kernels for 0%

commit v1 on v0

v1 whole, which is shorter than its diff:
```python
import functools

import jax
import jax.numpy as jnp
from jax import lax
from jax.experimental import pallas as pl
from jax.experimental.pallas import tpu as pltpu
from jax.sharding import PartitionSpec as P

HALF = 7
DMAX = 2
DIPS = 2 * DMAX + 1
TILE = 32
BINS = TILE * TILE
DEV = 128
SUB, LANE = 8, 128
SPAN = 40
GROUP = 8
ROOM = BINS + GROUP
PAY = 72
HALO = HALF * TILE

VM = pl.BlockSpec(memory_space=pltpu.VMEM)
SM = pl.BlockSpec(memory_space=pltpu.SMEM)
HB = pl.BlockSpec(memory_space=pl.ANY)


def params():
    return pltpu.CompilerParams(vmem_limit_bytes=60 << 20)


def pack_kernel(dest, bins, x, out, scr, z, brow, cnt, sem, bsem):
    for tr in range(4):
        for j in range(8):
            z[pl.ds(j * 128, 128), :] = x[pl.ds(j * 4 + tr, 128, stride=32), :].T
        for ti in range(SUB):
            scr[pl.ds(tr * 8 + ti, 128, stride=32), :] = z[pl.ds(ti, 128, stride=8), :].T
    brow[...] = jnp.full((DEV, 1, LANE), float(BINS), jnp.float32)

    def clear(i, _):
        cnt[i] = 0
        return 0

    lax.fori_loop(0, DEV, clear, 0, unroll=8)
    lane = lax.broadcasted_iota(jnp.int32, (1, LANE), 1)

    def place(b, _):
        t = dest[b]
        rank = cnt[t]
        cnt[t] = rank + 1
        pltpu.make_async_copy(
            scr.at[pl.ds(b * 32, 32)], out.at[t, pl.ds(rank * 32, 32)], sem
        ).start()
        row = brow[t]
        for q in range(4):
            row = jnp.where(lane == rank * 4 + q, bins[b * 4 + q].astype(jnp.float32), row)
        brow[t] = row
        return 0

    lax.fori_loop(0, DEV, place, 0)
    copy = pltpu.make_async_copy(brow, out.at[:, pl.ds(64, 1)], bsem)
    copy.start()
    pltpu.make_async_copy(scr, scr, sem).wait()
    copy.wait()


def pack(dest, bins, x):
    return pl.pallas_call(
        pack_kernel,
        out_shape=jax.ShapeDtypeStruct((DEV, PAY, LANE), jnp.float32),
        in_specs=[SM, SM, VM],
        out_specs=HB,
        scratch_shapes=[
            pltpu.VMEM((4096, LANE), jnp.float32),
            pltpu.VMEM((1024, LANE), jnp.float32),
            pltpu.VMEM((DEV, 1, LANE), jnp.float32),
            pltpu.SMEM((DEV,), jnp.int32),
            pltpu.SemaphoreType.DMA,
            pltpu.SemaphoreType.DMA,
        ],
        compiler_params=params(),
        name="pack",
    )(dest, bins, x)


def lists_kernel(dips, table, count):
    for m in range(2):
        for d in range(DIPS):
            count[m * DIPS + d] = 0

        def add(i, _):
            at = m * DIPS + dips[m * BINS + i] + DMAX
            n = count[at]
            table[at * ROOM + n] = i
            count[at] = n + 1
            return 0

        lax.fori_loop(0, BINS, add, 0, unroll=4)
        for d in range(DIPS):
            n = count[m * DIPS + d]
            for u in range(GROUP):
                table[(m * DIPS + d) * ROOM + n + u] = BINS


def make_lists(dips):
    return pl.pallas_call(
        lists_kernel,
        out_shape=(
            jax.ShapeDtypeStruct((2 * DIPS * ROOM,), jnp.int32),
            jax.ShapeDtypeStruct((2 * DIPS,), jnp.int32),
        ),
        in_specs=[SM],
        out_specs=(SM, SM),
        compiler_params=params(),
        cost_estimate=pl.CostEstimate(flops=0, bytes_accessed=60 << 20, transcendentals=0),
        name="lists",
    )(dips)


def bin_kernel(bins, scale, x, out, head, tail, *sums):
    zero = jnp.zeros((SUB, LANE), jnp.float32)

    def clear(i, _):
        for s in sums:
            s[i] = zero
        return 0

    lax.fori_loop(0, BINS, clear, 0, unroll=8)

    def add(i, _):
        for slot in range(2):
            for tr in range(4):
                b = bins[i * 8 + slot * 4 + tr]
                sums[tr][b] += x[i, pl.ds(slot * 32 + tr * 8, 8), :]
        return 0

    lax.fori_loop(0, DEV, add, 0, unroll=2)

    def finish(i, _):
        out[i] = ((sums[0][i] + sums[1][i]) + (sums[2][i] + sums[3][i])) * scale[i]
        return 0

    lax.fori_loop(0, BINS, finish, 0, unroll=8)
    head[...] = out[pl.ds(0, HALO)]
    tail[...] = out[pl.ds(BINS - HALO, HALO)]


FULL = jax.ShapeDtypeStruct((BINS, SUB, LANE), jnp.float32)
EDGE = jax.ShapeDtypeStruct((HALO, SUB, LANE), jnp.float32)


def put_bins(bins, scale, x):
    return pl.pallas_call(
        bin_kernel,
        out_shape=(FULL, EDGE, EDGE),
        in_specs=[SM, SM, VM],
        out_specs=(VM, VM, VM),
        scratch_shapes=[pltpu.VMEM((BINS + 1, SUB, LANE), jnp.float32) for _ in range(4)],
        compiler_params=params(),
        name="put_bins",
    )(bins, scale, x)


def widen(ext, row, x, lane):
    ext[pl.ds(row + 16, 8), :] = x
    ext[pl.ds(row + 24, 8), :] = jnp.where(lane < 127, pltpu.roll(x, 127, 1), 0.0)
    ext[pl.ds(row + 32, 8), :] = jnp.where(lane < 126, pltpu.roll(x, 126, 1), 0.0)
    ext[pl.ds(row + 8, 8), :] = jnp.where(lane >= 1, pltpu.roll(x, 1, 1), 0.0)
    ext[pl.ds(row, 8), :] = jnp.where(lane >= 2, pltpu.roll(x, 2, 1), 0.0)


def row_margins(ext, own, lo, hi):
    lane = lax.broadcasted_iota(jnp.int32, (SUB, LANE), 1)

    def inner(i, _):
        widen(ext, pl.multiple_of((i + HALO) * SPAN, 8), own[i], lane)
        return 0

    lax.fori_loop(0, BINS, inner, 0, unroll=8)

    def outer(i, _):
        widen(ext, pl.multiple_of(i * SPAN, 8), lo[i], lane)
        widen(ext, pl.multiple_of((i + HALO + BINS) * SPAN, 8), hi[i], lane)
        return 0

    lax.fori_loop(0, HALO, outer, 0, unroll=4)


WIDE = TILE + 2 * HALF


def col_margins(ext, own, lo, hi):
    lane = lax.broadcasted_iota(jnp.int32, (SUB, LANE), 1)

    def row(r, _):
        def inner(c, _):
            widen(ext, pl.multiple_of((r * WIDE + HALF + c) * SPAN, 8), own[r * TILE + c], lane)
            return 0

        lax.fori_loop(0, TILE, inner, 0, unroll=8)
        for c in range(HALF):
            widen(ext, pl.multiple_of((r * WIDE + c) * SPAN, 8), lo[r * HALF + c], lane)
            widen(
                ext, pl.multiple_of((r * WIDE + HALF + TILE + c) * SPAN, 8), hi[r * HALF + c], lane
            )
        return 0

    lax.fori_loop(0, TILE, row, 0)


def steer(table, count, which, ext, along_rows, write):
    stride = TILE if along_rows else 1
    for d in range(-DMAX, DMAX + 1):
        at = which * DIPS + d + DMAX
        base0 = 16 - HALF * d

        def group(g, _):
            for u in range(GROUP):
                b = table[at * ROOM + g * GROUP + u]
                first = b if along_rows else b + 2 * HALF * (b >> 5)
                view = ext.at[pl.ds(pl.multiple_of(first * SPAN, 8), 14 * stride * SPAN + SPAN)]

                def tap(k):
                    return view[pl.ds(base0 + (k + HALF) * (stride * SPAN + d), 8), :]

                total = tap(0) * (1.0 / 8.0)
                for k in range(1, HALF + 1):
                    total = total + (tap(k) + tap(-k)) * ((HALF + 1 - k) / 64.0)
                write(b, total)
            return 0

        lax.fori_loop(0, (count[at] + GROUP - 1) // GROUP, group, 0)


def first_kernel(table, count, own, lo, hi, out, left, right, ext, acc):
    row_margins(ext, own, lo, hi)

    def write(b, v):
        acc[b] = v

    steer(table, count, 0, ext, True, write)
    out[...] = acc[pl.ds(0, BINS)]

    def cut(r, _):
        for c in range(HALF):
            left[r * HALF + c] = acc[r * TILE + c]
            right[r * HALF + c] = acc[r * TILE + TILE - HALF + c]
        return 0

    lax.fori_loop(0, TILE, cut, 0)


def second_kernel(table, count, own, lo, hi, out, head, tail, ext, acc):
    col_margins(ext, own, lo, hi)

    def write(b, v):
        acc[b] = v

    steer(table, count, 1, ext, False, write)
    out[...] = acc[pl.ds(0, BINS)]
    head[...] = acc[pl.ds(0, HALO)]
    tail[...] = acc[pl.ds(BINS - HALO, HALO)]


def third_kernel(table, count, own, lo, hi, out, ext, acc, z):
    row_margins(ext, own, lo, hi)

    def write(b, v):
        acc[pl.ds(pl.multiple_of(b * 8, 8), 8), :] = v

    steer(table, count, 0, ext, True, write)

    def natural(i, _):
        for ti in range(SUB):
            z[pl.ds(ti, 128, stride=8), :] = acc[pl.ds(i * 1024 + ti, 128, stride=8), :].T
        for j in range(8):
            out[pl.ds(i * 4, 4), :, pl.ds(j * 128, 128)] = (
                z[pl.ds(j * 128, 128), :].T.reshape(4, 32, 128)
            )
        return 0

    lax.fori_loop(0, 8, natural, 0)


EXT = pltpu.VMEM(((WIDE * TILE + 16) * SPAN, LANE), jnp.float32)
ACC = pltpu.VMEM((BINS + 1, SUB, LANE), jnp.float32)


def middle(kernel, name, table, count, own, lo, hi):
    return pl.pallas_call(
        kernel,
        out_shape=(FULL, EDGE, EDGE),
        in_specs=[SM, SM, VM, VM, VM],
        out_specs=(VM, VM, VM),
        scratch_shapes=[EXT, ACC],
        compiler_params=params(),
        name=name,
    )(table, count, own, lo, hi)


def last(table, count, own, lo, hi):
    return pl.pallas_call(
        third_kernel,
        out_shape=jax.ShapeDtypeStruct((TILE, TILE, SUB * LANE), jnp.float32),
        in_specs=[SM, SM, VM, VM, VM],
        out_specs=VM,
        scratch_shapes=[
            EXT,
            pltpu.VMEM(((BINS + 1) * SUB, LANE), jnp.float32),
            pltpu.VMEM((1024, LANE), jnp.float32),
        ],
        compiler_params=params(),
        name="third",
    )(table, count, own, lo, hi)


def beside(head, tail, axis):
    ends = lax.axis_size(axis) - 1
    lo = lax.ppermute(tail, axis, [(i, i + 1) for i in range(ends)])
    hi = lax.ppermute(head, axis, [(i + 1, i) for i in range(ends)])
    return lo, hi


def on_device(traces, destination, bin_index, dip_inline, dip_cross):
    x = traces.reshape(DEV, 4, 8, 128).transpose(0, 2, 1, 3).reshape(4096, 128)
    outgoing = pack(destination.reshape(-1), bin_index.reshape(-1), x)
    arrived = lax.all_to_all(
        outgoing, ("inline", "crosslin"), split_axis=0, concat_axis=0, tiled=True
    )
    dips = jnp.concatenate([dip_inline.reshape(-1), dip_cross.reshape(-1)])
    table, count = make_lists(dips)
    bins = arrived[:, 64, :8].astype(jnp.int32).reshape(-1)
    fold = jnp.sum(
        (jnp.arange(BINS, dtype=jnp.int32)[:, None] == bins[None, :]).astype(jnp.float32), axis=1
    )
    stacked, head, tail = put_bins(bins, 1.0 / jnp.maximum(fold, 1.0), arrived)
    lo, hi = beside(head, tail, "inline")
    first, left, right = middle(first_kernel, "first", table, count, stacked, lo, hi)
    lo, hi = beside(left, right, "crosslin")
    second, head, tail = middle(second_kernel, "second", table, count, first, lo, hi)
    lo, hi = beside(head, tail, "inline")
    return last(table, count, second, lo, hi)


def solution(mesh):
    return jax.shard_map(
        on_device,
        mesh=mesh,
        in_specs=(
            P(("inline", "crosslin"), None, None),
            P(("inline", "crosslin"), None),
            P(("inline", "crosslin"), None),
            P("inline", "crosslin"),
            P("inline", "crosslin"),
        ),
        out_specs=P("inline", "crosslin", None),
        check_vma=False,
    )
```

time: 809 us -> 257 us (0.32)
  other arithmetic: 622 us -> 1.89 us
  Pallas kernels: 0 us -> 120 us
  blocking collectives: 0 us -> 65.6 us
  waiting for transfers between devices: 100 us -> 44.1 us
  local copies, waits for them, and re-layouts: 29 us -> 6.71 us
  starting transfers between devices: 38.9 us -> 17.2 us
  matrix products: 9.72 us -> 0 us
    select_n x6 -> x0, other arithmetic: 620 us -> none  [the longest x3 615 us: steer(): result = jnp.where((dip_index == dip_value)[..., None], running, result)]
    pallas_call x0 -> x6, Pallas kernels: none -> 120 us  [the longest x2 57.5 us: middle(): pl.pallas_call(kernel, out_shape=(FULL, EDGE, EDGE), in_specs=[SM, SM, VM...]
    all_to_all x0 -> x1, blocking collectives: none -> 65.6 us  [on_device(): lax.all_to_all(outgoing, ('inline', 'crosslin'), split_axis=0, concat_axi...]
    all_to_all x2 -> x0, waiting for transfers between devices: 47.9 us -> none  [the longest x1 47.9 us: on_device(): lax.all_to_all(outgoing, ('inline', 'crosslin'), split_axis=0, concat_axi...]
    all_to_all x2 -> x0, starting transfers between devices: 20.3 us -> none  [the longest x1 10.2 us: on_device(): lax.all_to_all(outgoing, ('inline', 'crosslin'), split_axis=0, concat_axi...]
    pad x3 -> x0, local copies, waits for them, and re-layouts: 10.3 us -> none  [pad_time(): return jnp.pad(gridded, ((0, 0), (0, 0), (margin, margin)))]
    dot_general x1 -> x0, matrix products: 9.72 us -> none  [on_device(): jnp.dot(member, arrived_rows, precision=lax.Precision.HIGHEST, preferred_...]
  transfers between devices with their start and end apart: 8 -> 6, of which waited for: 7 -> 6; matrix products, arithmetic and copies ran while one was open for 3% -> 0% of each run, Pallas kernels for 0% -> 5%
where the time goes in v1:
time: 257 us; the launch traced here: 256 us
  Pallas kernels  120 us (47%)
  blocking collectives  65.6 us (26%)
  waiting for transfers between devices  44.1 us (17%)
  starting transfers between devices  17.2 us (7%)
  local copies, waits for them, and re-layouts  6.71 us (3%)
    all_to_all x1, blocking collectives, on_device(): lax.all_to_all(outgoing, ('inline', 'crosslin'), split_axis=0, concat_axi...  65.6 us
    pallas_call x2, Pallas kernels, middle(): pl.pallas_call(kernel, out_shape=(FULL, EDGE, EDGE), in_specs=[SM, SM, VM...  57.5 us
    ppermute x3, waiting for transfers between devices, beside(): lo = lax.ppermute(tail, axis, [(i, i + 1) for i in range(ends)])  33.1 us
    pallas_call x1, Pallas kernels, last(): pl.pallas_call(third_kernel, out_shape=jax.ShapeDtypeStruct((TILE, TILE,...  33 us
    pallas_call x1, Pallas kernels, make_lists(): pl.pallas_call(lists_kernel, out_shape=(jax.ShapeDtypeStruct((2 * DIPS *...  13.2 us
    ppermute x3, waiting for transfers between devices, beside(): hi = lax.ppermute(head, axis, [(i + 1, i) for i in range(ends)])  11 us
    ppermute x3, starting transfers between devices, beside(): hi = lax.ppermute(head, axis, [(i + 1, i) for i in range(ends)])  9.87 us
    pallas_call x1, Pallas kernels, put_bins(): pl.pallas_call(bin_kernel, out_shape=(FULL, EDGE, EDGE), in_specs=[SM, SM...  9.25 us
  transfers between devices with their start and end apart: 6, of which 6 were waited for; matrix products, arithmetic and copies ran while one was open for 0% of the time, Pallas kernels for 5%

profile of v1, /device:TPU:56, one launch (start us, length us, event | category | flops | bytes accessed | tf_op | source)
XLA Modules:
  0.0 255.8 jit_solution(6840585829705720624)
XLA Ops:
  0.0 0.8 copy.9
  0.8 0.7 reshape.29.bins
  1.5 7.2 %pack.1 = f32[128,72,128]{2,1,0:T(8,128)} custom-call(s32[128]{0:T(128)} %bitcast.7, s32[512]{0:T(512)} %reshape.29.bins, f32[4096,128]{1,0:T(8,128)} %bitcast.6), custom_call_target="tpu_custom_call" | custom-call | tf_op jit(solution)/shard_map/pack/pallas_call | solution.py:68
  8.7 65.6 %all_to_all.5.x = f32[128,72,128]{2,1,0:T(8,128)S(1)} all-to-all(f32[128,72,128]{2,1,0:T(8,128)} %pack.1), channel_id=1, replica_groups=mesh['inline'=16,'crosslin'=8] {'inline','crosslin'}, dimensions={0} | all-to-all | bytes 9437184 | tf_op jit(solution)/shard_map/all_to_all | solution.py:327
  74.3 2.1 copy-done
  76.4 0.2 fusion
  76.6 0.1 convert_element_type.15.bins
  76.7 0.5 convert_reduce_fusion
  77.2 0.6 maximum_divide_fusion.scale
  77.8 9.3 %put_bins.1 = (f32[1024,8,128]{2,1,0:T(8,128)}, f32[224,8,128]{2,1,0:T(8,128)}, f32[224,8,128]{2,1,0:T(8,128)}) custom-call(s32[1024]{0:T(1024)} %copy-done.7, f32[1024]{0:T(1024)} %maximum_divide_fusion.scale, f32[128,72,128]{2,1,0:T(8,128)} %copy-done), custom_call_target="tpu_custom_call" | custom-call | tf_op jit(solution)/shard_map/put_bins/pallas_call | solution.py:153
  87.0 3.5 %collective-permute-start = (f32[224,8,128]{2,1,0:T(8,128)}, f32[224,8,128]{2,1,0:T(8,128)S(1)}, u32[]{:S(2)}, u32[]{:S(2)}) collective-permute-start(f32[224,8,128]{2,1,0:T(8,128)} %get-tuple-element.19), channel_id=1, source_target_pairs={{0,8},{8,16},{16,24},{24,32},{32,40},{40,48},{48,56},{56,64},{64,7... | collective-permute-start | bytes 2752520 | tf_op jit(solution)/shard_map/ppermute | solution.py:319
  90.6 2.3 collective-permute-start.1
  92.9 0.1 reshape.26
  93.0 0.1 reshape.27
  93.0 0.6 pad_add_fusion.dips
  93.7 13.2 %lists.1 = (s32[10320]{0:T(1024)}, s32[10]{0:T(128)}) custom-call(s32[2048]{0:T(1024)} %pad_add_fusion.dips), custom_call_target="tpu_custom_call" | custom-call | bytes 62914560 | tf_op jit(solution)/shard_map/lists/pallas_call | solution.py:106
  106.9 4.7 %collective-permute-done.lo = f32[224,8,128]{2,1,0:T(8,128)S(1)} collective-permute-done((f32[224,8,128]{2,1,0:T(8,128)}, f32[224,8,128]{2,1,0:T(8,128)S(1)}, u32[]{:S(2)}, u32[]{:S(2)}) %collective-permute-start) | collective-permute-done | bytes 917536 | tf_op jit(solution)/shard_map/ppermute | solution.py:319
  111.6 5.1 %collective-permute-done.1.hi = f32[224,8,128]{2,1,0:T(8,128)S(1)} collective-permute-done((f32[224,8,128]{2,1,0:T(8,128)}, f32[224,8,128]{2,1,0:T(8,128)S(1)}, u32[]{:S(2)}, u32[]{:S(2)}) %collective-permute-start.1) | collective-permute-done | bytes 917536 | tf_op jit(solution)/shard_map/ppermute | solution.py:320
  116.7 0.9 copy-done.2
  117.6 31.0 %first.1 = (f32[1024,8,128]{2,1,0:T(8,128)}, f32[224,8,128]{2,1,0:T(8,128)}, f32[224,8,128]{2,1,0:T(8,128)}) custom-call(s32[10320]{0:T(1024)} %get-tuple-element.16.table, s32[10]{0:T(128)} %get-tuple-element.17.count, f32[1024,8,128]{2,1,0:T(8,128)} %get-tuple-element.18.own, f32[224,8,128]{2,1,0:T(8,128)} %copy-done.1, f32[224,8,128]{2,1,0:T(8,128)} %copy-done.2), custom_call_target="tpu_custom_call" | custom-call | tf_op jit(solution)/shard_map/first/pallas_call | solution.py:290
  148.6 1.9 collective-permute-start.2
  150.5 3.6 %collective-permute-start.3 = (f32[224,8,128]{2,1,0:T(8,128)}, f32[224,8,128]{2,1,0:T(8,128)S(1)}, u32[]{:S(2)}, u32[]{:S(2)}) collective-permute-start(f32[224,8,128]{2,1,0:T(8,128)} %get-tuple-element.23), channel_id=1, source_target_pairs={{1,0},{2,1},{3,2},{4,3},{5,4},{6,5},{7,6},{9,8},{10,9},{11,10},{12... | collective-permute-start | bytes 2752520 | tf_op jit(solution)/shard_map/ppermute | solution.py:320
  154.1 9.3 %collective-permute-done.2.lo = f32[224,8,128]{2,1,0:T(8,128)S(1)} collective-permute-done((f32[224,8,128]{2,1,0:T(8,128)}, f32[224,8,128]{2,1,0:T(8,128)S(1)}, u32[]{:S(2)}, u32[]{:S(2)}) %collective-permute-start.2) | collective-permute-done | bytes 917536 | tf_op jit(solution)/shard_map/ppermute | solution.py:319
  163.5 1.9 collective-permute-done.3.hi
  165.3 0.9 copy-done.5
  166.3 26.6 %second.1 = (f32[1024,8,128]{2,1,0:T(8,128)}, f32[224,8,128]{2,1,0:T(8,128)}, f32[224,8,128]{2,1,0:T(8,128)}) custom-call(s32[10320]{0:T(1024)} %get-tuple-element.16.table, s32[10]{0:T(128)} %get-tuple-element.17.count, f32[1024,8,128]{2,1,0:T(8,128)} %get-tuple-element.21.own, f32[224,8,128]{2,1,0:T(8,128)} %copy-done.3, f32[224,8,128]{2,1,0:T(8,128)} %copy-done.5), custom_call_target="tpu_custom_call" | custom-call | tf_op jit(solution)/shard_map/second/pallas_call | solution.py:290
  192.8 1.9 collective-permute-start.4
  194.8 3.9 %collective-permute-start.5 = (f32[224,8,128]{2,1,0:T(8,128)}, f32[224,8,128]{2,1,0:T(8,128)S(1)}, u32[]{:S(2)}, u32[]{:S(2)}) collective-permute-start(f32[224,8,128]{2,1,0:T(8,128)} %get-tuple-element.26), channel_id=1, source_target_pairs={{8,0},{16,8},{24,16},{32,24},{40,32},{48,40},{56,48},{64,56},{72,6... | collective-permute-start | bytes 2752520 | tf_op jit(solution)/shard_map/ppermute | solution.py:320
  198.7 19.0 %collective-permute-done.4.lo = f32[224,8,128]{2,1,0:T(8,128)S(1)} collective-permute-done((f32[224,8,128]{2,1,0:T(8,128)}, f32[224,8,128]{2,1,0:T(8,128)S(1)}, u32[]{:S(2)}, u32[]{:S(2)}) %collective-permute-start.4) | collective-permute-done | bytes 917536 | tf_op jit(solution)/shard_map/ppermute | solution.py:319
  217.7 4.0 %collective-permute-done.5.hi = f32[224,8,128]{2,1,0:T(8,128)S(1)} collective-permute-done((f32[224,8,128]{2,1,0:T(8,128)}, f32[224,8,128]{2,1,0:T(8,128)S(1)}, u32[]{:S(2)}, u32[]{:S(2)}) %collective-permute-start.5) | collective-permute-done | bytes 917536 | tf_op jit(solution)/shard_map/ppermute | solution.py:320
  221.7 1.0 copy-done.6
  222.7 33.0 %third.1 = f32[32,32,1024]{2,1,0:T(8,128)} custom-call(s32[10320]{0:T(1024)} %get-tuple-element.16.table, s32[10]{0:T(128)} %get-tuple-element.17.count, f32[1024,8,128]{2,1,0:T(8,128)} %get-tuple-element.24.own, f32[224,8,128]{2,1,0:T(8,128)} %copy-done.4, f32[224,8,128]{2,1,0:T(8,128)} %copy-done.6), custom_call_target="tpu_custom_call" | custom-call | tf_op jit(solution)/shard_map/third/pallas_call | solution.py:302
  (16 shorter events, 0.0 us)
Async XLA Ops:
  74.3 2.1 copy-start
  76.4 16.5 %copy-start.8 = (s32[32,32]{1,0:T(8,128)S(1)}, s32[32,32]{1,0:T(8,128)}, u32[]{:S(2)}) copy-start(s32[32,32]{1,0:T(8,128)} %param.8) | copy-start | bytes 12292
  76.4 16.6 %copy-start.9 = (s32[32,32]{1,0:T(8,128)S(1)}, s32[32,32]{1,0:T(8,128)}, u32[]{:S(2)}) copy-start(s32[32,32]{1,0:T(8,128)} %param.9) | copy-start | bytes 12292
  76.7 1.1 copy-start.7
  87.0 24.5 %collective-permute-start = (f32[224,8,128]{2,1,0:T(8,128)}, f32[224,8,128]{2,1,0:T(8,128)S(1)}, u32[]{:S(2)}, u32[]{:S(2)}) collective-permute-start(f32[224,8,128]{2,1,0:T(8,128)} %get-tuple-element.19), channel_id=1, source_target_pairs={{0,8},{8,16},{16,24},{24,32},{32,40},{40,48},{48,56},{56,64},{64,7... | collective-permute-start | bytes 2752520 | tf_op jit(solution)/shard_map/ppermute | solution.py:319
  90.6 26.1 %collective-permute-start.1 = (f32[224,8,128]{2,1,0:T(8,128)}, f32[224,8,128]{2,1,0:T(8,128)S(1)}, u32[]{:S(2)}, u32[]{:S(2)}) collective-permute-start(f32[224,8,128]{2,1,0:T(8,128)} %get-tuple-element.20), channel_id=1, source_target_pairs={{8,0},{16,8},{24,16},{32,24},{40,32},{48,40},{56,48},{64,56},{72,6... | collective-permute-start | bytes 2752520 | tf_op jit(solution)/shard_map/ppermute | solution.py:320
  111.6 5.1 %copy-start.1 = (f32[224,8,128]{2,1,0:T(8,128)}, f32[224,8,128]{2,1,0:T(8,128)S(1)}, u32[]{:S(2)}) copy-start(f32[224,8,128]{2,1,0:T(8,128)S(1)} %collective-permute-done.lo) | copy-start | bytes 2752516
  116.7 0.9 copy-start.2
  148.6 14.9 %collective-permute-start.2 = (f32[224,8,128]{2,1,0:T(8,128)}, f32[224,8,128]{2,1,0:T(8,128)S(1)}, u32[]{:S(2)}, u32[]{:S(2)}) collective-permute-start(f32[224,8,128]{2,1,0:T(8,128)} %get-tuple-element.22), channel_id=1, source_target_pairs={{0,1},{1,2},{2,3},{3,4},{4,5},{5,6},{6,7},{8,9},{9,10},{10,11},{11... | collective-permute-start | bytes 2752520 | tf_op jit(solution)/shard_map/ppermute | solution.py:319
  150.5 14.9 %collective-permute-start.3 = (f32[224,8,128]{2,1,0:T(8,128)}, f32[224,8,128]{2,1,0:T(8,128)S(1)}, u32[]{:S(2)}, u32[]{:S(2)}) collective-permute-start(f32[224,8,128]{2,1,0:T(8,128)} %get-tuple-element.23), channel_id=1, source_target_pairs={{1,0},{2,1},{3,2},{4,3},{5,4},{6,5},{7,6},{9,8},{10,9},{11,10},{12... | collective-permute-start | bytes 2752520 | tf_op jit(solution)/shard_map/ppermute | solution.py:320
  163.5 1.9 copy-start.3
  165.3 0.9 copy-start.5
  192.8 24.9 %collective-permute-start.4 = (f32[224,8,128]{2,1,0:T(8,128)}, f32[224,8,128]{2,1,0:T(8,128)S(1)}, u32[]{:S(2)}, u32[]{:S(2)}) collective-permute-start(f32[224,8,128]{2,1,0:T(8,128)} %get-tuple-element.25), channel_id=1, source_target_pairs={{0,8},{8,16},{16,24},{24,32},{32,40},{40,48},{48,56},{56,64},{64,7... | collective-permute-start | bytes 2752520 | tf_op jit(solution)/shard_map/ppermute | solution.py:319
  194.8 27.0 %collective-permute-start.5 = (f32[224,8,128]{2,1,0:T(8,128)}, f32[224,8,128]{2,1,0:T(8,128)S(1)}, u32[]{:S(2)}, u32[]{:S(2)}) collective-permute-start(f32[224,8,128]{2,1,0:T(8,128)} %get-tuple-element.26), channel_id=1, source_target_pairs={{8,0},{16,8},{24,16},{32,24},{40,32},{48,40},{56,48},{64,56},{72,6... | collective-permute-start | bytes 2752520 | tf_op jit(solution)/shard_map/ppermute | solution.py:320
  217.7 4.0 %copy-start.4 = (f32[224,8,128]{2,1,0:T(8,128)}, f32[224,8,128]{2,1,0:T(8,128)S(1)}, u32[]{:S(2)}) copy-start(f32[224,8,128]{2,1,0:T(8,128)S(1)} %collective-permute-done.4.lo) | copy-start | bytes 2752516
  221.7 1.0 copy-start.6

commit v2 on v1

v2 whole, which is shorter than its diff:
```python
import functools

import jax
import jax.numpy as jnp
from jax import lax
from jax.experimental import pallas as pl
from jax.experimental.pallas import tpu as pltpu
from jax.sharding import PartitionSpec as P

HALF = 7
DMAX = 2
DIPS = 2 * DMAX + 1
TILE = 32
BINS = TILE * TILE
DEV = 128
SUB, LANE = 8, 128
SPAN = 40
GROUP = 8
ROOM = 18 * TILE + GROUP
PAY = 72
HALO = HALF * TILE

VM = pl.BlockSpec(memory_space=pltpu.VMEM)
SM = pl.BlockSpec(memory_space=pltpu.SMEM)
HB = pl.BlockSpec(memory_space=pl.ANY)


def params():
    return pltpu.CompilerParams(vmem_limit_bytes=60 << 20)


def pack_kernel(dest, bins, x, out, scr, z, brow, cnt, sem, bsem):
    for tr in range(4):
        for j in range(8):
            z[pl.ds(j * 128, 128), :] = x[pl.ds(j * 4 + tr, 128, stride=32), :].T
        for ti in range(SUB):
            scr[pl.ds(tr * 8 + ti, 128, stride=32), :] = z[pl.ds(ti, 128, stride=8), :].T
    brow[...] = jnp.full((DEV, 1, LANE), float(BINS), jnp.float32)

    def clear(i, _):
        cnt[i] = 0
        return 0

    lax.fori_loop(0, DEV, clear, 0, unroll=8)
    lane = lax.broadcasted_iota(jnp.int32, (1, LANE), 1)

    def place(b, _):
        t = dest[b]
        rank = cnt[t]
        cnt[t] = rank + 1
        pltpu.make_async_copy(
            scr.at[pl.ds(b * 32, 32)], out.at[t, pl.ds(rank * 32, 32)], sem
        ).start()
        row = brow[t]
        for q in range(4):
            row = jnp.where(lane == rank * 4 + q, bins[b * 4 + q].astype(jnp.float32), row)
        brow[t] = row
        return 0

    lax.fori_loop(0, DEV, place, 0)
    copy = pltpu.make_async_copy(brow, out.at[:, pl.ds(64, 1)], bsem)
    copy.start()
    pltpu.make_async_copy(scr, scr, sem).wait()
    copy.wait()


def pack(dest, bins, x):
    return pl.pallas_call(
        pack_kernel,
        out_shape=jax.ShapeDtypeStruct((DEV, PAY, LANE), jnp.float32),
        in_specs=[SM, SM, VM],
        out_specs=HB,
        scratch_shapes=[
            pltpu.VMEM((4096, LANE), jnp.float32),
            pltpu.VMEM((1024, LANE), jnp.float32),
            pltpu.VMEM((DEV, 1, LANE), jnp.float32),
            pltpu.SMEM((DEV,), jnp.int32),
            pltpu.SemaphoreType.DMA,
            pltpu.SemaphoreType.DMA,
        ],
        compiler_params=params(),
        name="pack",
    )(dest, bins, x)


def add_bin(dips, table, count, i, part):
    at = part * DIPS + dips[i] + DMAX
    n = count[at]
    table[at * ROOM + n] = i
    count[at] = n + 1


def lists_kernel(along_rows, dips, table, count):
    for at in range(2 * DIPS):
        count[at] = 0
    inside = range(HALF, TILE - HALF)
    if along_rows:
        for low, high, part in ((0, HALF, 1), (HALF, TILE - HALF, 0), (TILE - HALF, TILE, 1)):

            def add(i, _):
                add_bin(dips, table, count, i, part)
                return 0

            lax.fori_loop(low * TILE, high * TILE, add, 0, unroll=4)
    else:

        def row(r, _):
            for c in range(TILE):
                add_bin(dips, table, count, r * TILE + c, 0 if c in inside else 1)
            return 0

        lax.fori_loop(0, TILE, row, 0)
    for at in range(2 * DIPS):
        n = count[at]
        for u in range(GROUP):
            table[at * ROOM + n + u] = BINS


def make_lists(dips, along_rows):
    return pl.pallas_call(
        functools.partial(lists_kernel, along_rows),
        out_shape=(
            jax.ShapeDtypeStruct((2 * DIPS * ROOM,), jnp.int32),
            jax.ShapeDtypeStruct((2 * DIPS,), jnp.int32),
        ),
        in_specs=[SM],
        out_specs=(SM, SM),
        compiler_params=params(),
        cost_estimate=pl.CostEstimate(flops=0, bytes_accessed=24 << 20, transcendentals=0),
        name="lists_rows" if along_rows else "lists_cols",
    )(dips)


def bin_kernel(bins, scale, x, out, head, tail, *sums):
    zero = jnp.zeros((SUB, LANE), jnp.float32)

    def clear(i, _):
        for s in sums:
            s[i] = zero
        return 0

    lax.fori_loop(0, BINS, clear, 0, unroll=8)

    def add(i, _):
        for slot in range(2):
            for tr in range(4):
                b = bins[i * 8 + slot * 4 + tr]
                sums[tr][b] += x[i, pl.ds(slot * 32 + tr * 8, 8), :]
        return 0

    lax.fori_loop(0, DEV, add, 0, unroll=2)

    def finish(i, _):
        out[i] = ((sums[0][i] + sums[1][i]) + (sums[2][i] + sums[3][i])) * scale[i]
        return 0

    lax.fori_loop(0, BINS, finish, 0, unroll=8)
    head[...] = out[pl.ds(0, HALO)]
    tail[...] = out[pl.ds(BINS - HALO, HALO)]


FULL = jax.ShapeDtypeStruct((BINS, SUB, LANE), jnp.float32)
EDGE = jax.ShapeDtypeStruct((HALO, SUB, LANE), jnp.float32)


def put_bins(bins, scale, x):
    return pl.pallas_call(
        bin_kernel,
        out_shape=(FULL, EDGE, EDGE),
        in_specs=[SM, SM, VM],
        out_specs=(VM, VM, VM),
        scratch_shapes=[pltpu.VMEM((BINS + 1, SUB, LANE), jnp.float32) for _ in range(4)],
        compiler_params=params(),
        name="put_bins",
    )(bins, scale, x)


def widen(ext, row, x, lane):
    ext[pl.ds(row + 16, 8), :] = x
    ext[pl.ds(row + 24, 8), :] = jnp.where(lane < 127, pltpu.roll(x, 127, 1), 0.0)
    ext[pl.ds(row + 32, 8), :] = jnp.where(lane < 126, pltpu.roll(x, 126, 1), 0.0)
    ext[pl.ds(row + 8, 8), :] = jnp.where(lane >= 1, pltpu.roll(x, 1, 1), 0.0)
    ext[pl.ds(row, 8), :] = jnp.where(lane >= 2, pltpu.roll(x, 2, 1), 0.0)


WIDE = TILE + 2 * HALF
ROW_PITCH = TILE * SPAN + 8
COL_PITCH = SPAN
EXT_ROWS = 72000


def start_of(b, along_rows):
    if along_rows:
        return b * SPAN + 8 * (b >> 5)
    return (b + 2 * HALF * (b >> 5)) * SPAN


def inner_margins(ext, own, along_rows):
    lane = lax.broadcasted_iota(jnp.int32, (SUB, LANE), 1)
    shift = HALF * (ROW_PITCH if along_rows else COL_PITCH)

    def row(r, _):
        first = start_of(r * TILE, along_rows) + shift

        def inner(c, _):
            widen(ext, pl.multiple_of(first + c * SPAN, 8), own[r * TILE + c], lane)
            return 0

        lax.fori_loop(0, TILE, inner, 0, unroll=16)
        return 0

    lax.fori_loop(0, TILE, row, 0)


def outer_margins(ext, lo, hi, along_rows):
    lane = lax.broadcasted_iota(jnp.int32, (SUB, LANE), 1)
    if along_rows:

        def row(r, _):
            first = r * ROW_PITCH

            def outer(c, _):
                at = pl.multiple_of(first + c * SPAN, 8)
                widen(ext, at, lo[r * TILE + c], lane)
                widen(
                    ext,
                    pl.multiple_of(at + (TILE + HALF) * ROW_PITCH, 8),
                    hi[r * TILE + c],
                    lane,
                )
                return 0

            lax.fori_loop(0, TILE, outer, 0, unroll=8)
            return 0

        lax.fori_loop(0, HALF, row, 0)
    else:

        def row(r, _):
            first = pl.multiple_of(r * WIDE * SPAN, 8)
            for c in range(HALF):
                widen(ext, first + c * SPAN, lo[r * HALF + c], lane)
                widen(ext, first + (HALF + TILE + c) * SPAN, hi[r * HALF + c], lane)
            return 0

        lax.fori_loop(0, TILE, row, 0)


def steer(table, count, part, ext, along_rows, acc):
    pitch = ROW_PITCH if along_rows else COL_PITCH
    for d in range(-DMAX, DMAX + 1):
        at = part * DIPS + d + DMAX

        def group(g, _):
            for u in range(GROUP):
                b = table[at * ROOM + g * GROUP + u]
                first = pl.multiple_of(start_of(b, along_rows), 8)
                view = ext.at[pl.ds(first, 14 * pitch + SPAN)]

                def tap(k):
                    return view[pl.ds(16 + (k + HALF) * pitch + d * k, 8), :]

                total = tap(0) * (1.0 / 8.0)
                for k in range(1, HALF + 1):
                    total = total + (tap(k) + tap(-k)) * ((HALF + 1 - k) / 64.0)
                acc[b] = total
            return 0

        lax.fori_loop(0, (count[at] + GROUP - 1) // GROUP, group, 0)


def inner_kernel(along_rows, table, count, own, ext, acc):
    inner_margins(ext, own, along_rows)
    steer(table, count, 0, ext, along_rows, acc)


def outer_kernel(along_rows, table, count, lo, hi, ext_in, acc_in, ext, acc, one, two):
    outer_margins(ext, lo, hi, along_rows)
    steer(table, count, 1, ext, along_rows, acc)
    if along_rows:

        def cut(r, _):
            for c in range(HALF):
                one[r * HALF + c] = acc[r * TILE + c]
                two[r * HALF + c] = acc[r * TILE + TILE - HALF + c]
            return 0

        lax.fori_loop(0, TILE, cut, 0)
    else:
        one[...] = acc[pl.ds(0, HALO)]
        two[...] = acc[pl.ds(BINS - HALO, HALO)]


def natural(acc, out, z, i):
    for ti in range(SUB):
        z[pl.ds(ti, 128, stride=8), :] = acc[pl.ds(i * 128, 128), ti, :].T
    for j in range(8):
        out[pl.ds(i * 4, 4), :, pl.ds(j * 128, 128)] = (
            z[pl.ds(j * 128, 128), :].T.reshape(4, 32, 128)
        )


def last_kernel(table, count, lo, hi, ext_in, acc_in, out, ext, acc, z):
    outer_margins(ext, lo, hi, True)
    steer(table, count, 1, ext, True, acc)

    def four(i, _):
        natural(acc, out, z, i)
        return 0

    lax.fori_loop(0, 8, four, 0)


EXT = pltpu.VMEM((EXT_ROWS, LANE), jnp.float32)
ACC = pltpu.VMEM((BINS + 1, SUB, LANE), jnp.float32)


def small():
    return pltpu.CompilerParams(vmem_limit_bytes=16 << 20)


def inner(lists, own, along_rows):
    return pl.pallas_call(
        functools.partial(inner_kernel, along_rows),
        out_shape=(EXT, ACC),
        in_specs=[SM, SM, VM],
        out_specs=(VM, VM),
        compiler_params=small(),
        cost_estimate=pl.CostEstimate(flops=0, bytes_accessed=48 << 20, transcendentals=0),
        name="inner_rows" if along_rows else "inner_cols",
    )(*lists, own)


def outer(lists, lo, hi, kept, along_rows):
    return pl.pallas_call(
        functools.partial(outer_kernel, along_rows),
        out_shape=(EXT, ACC, EDGE, EDGE),
        in_specs=[SM, SM, VM, VM, VM, VM],
        out_specs=(VM, VM, VM, VM),
        input_output_aliases={4: 0, 5: 1},
        compiler_params=small(),
        name="outer_rows" if along_rows else "outer_cols",
    )(*lists, lo, hi, *kept)[1:]


def last(lists, lo, hi, kept):
    return pl.pallas_call(
        last_kernel,
        out_shape=(jax.ShapeDtypeStruct((TILE, TILE, SUB * LANE), jnp.float32), EXT, ACC),
        in_specs=[SM, SM, VM, VM, VM, VM],
        out_specs=(VM, VM, VM),
        input_output_aliases={4: 1, 5: 2},
        scratch_shapes=[pltpu.VMEM((1024, LANE), jnp.float32)],
        compiler_params=small(),
        name="last",
    )(*lists, lo, hi, *kept)[0]


def beside(head, tail, axis):
    ends = lax.axis_size(axis) - 1
    lo = lax.ppermute(tail, axis, [(i, i + 1) for i in range(ends)])
    hi = lax.ppermute(head, axis, [(i + 1, i) for i in range(ends)])
    return lo, hi


def on_device(traces, destination, bin_index, dip_inline, dip_cross):
    x = traces.reshape(DEV, 4, 8, 128).transpose(0, 2, 1, 3).reshape(4096, 128)
    outgoing = pack(destination.reshape(-1), bin_index.reshape(-1), x)
    arrived = lax.all_to_all(
        outgoing, ("inline", "crosslin"), split_axis=0, concat_axis=0, tiled=True
    )
    rows = make_lists(dip_inline.reshape(-1), True)
    cols = make_lists(dip_cross.reshape(-1), False)
    bins = arrived[:, 64, :8].astype(jnp.int32).reshape(-1)
    fold = jnp.sum(
        (jnp.arange(BINS, dtype=jnp.int32)[:, None] == bins[None, :]).astype(jnp.float32), axis=1
    )
    stacked, head, tail = put_bins(bins, 1.0 / jnp.maximum(fold, 1.0), arrived)
    lo, hi = beside(head, tail, "inline")
    kept = inner(rows, stacked, True)
    first, left, right = outer(rows, lo, hi, kept, True)
    lo, hi = beside(left, right, "crosslin")
    kept = inner(cols, first, False)
    second, head, tail = outer(cols, lo, hi, kept, False)
    lo, hi = beside(head, tail, "inline")
    kept = inner(rows, second, True)
    return last(rows, lo, hi, kept)


def solution(mesh):
    return jax.shard_map(
        on_device,
        mesh=mesh,
        in_specs=(
            P(("inline", "crosslin"), None, None),
            P(("inline", "crosslin"), None),
            P(("inline", "crosslin"), None),
            P("inline", "crosslin"),
            P("inline", "crosslin"),
        ),
        out_specs=P("inline", "crosslin", None),
        check_vma=False,
    )
```

time: 257 us -> 214 us (0.83)
  waiting for transfers between devices: 44.1 us -> 11.8 us
  Pallas kernels: 120 us -> 104 us
  local copies, waits for them, and re-layouts: 6.71 us -> 12 us
    ppermute x3, waiting for transfers between devices: 33.1 us -> 4.27 us  [beside(): lo = lax.ppermute(tail, axis, [(i, i + 1) for i in range(ends)])]
    pallas_call x4 -> x8, Pallas kernels: 104 us -> 87.3 us  [the longest x3 41.4 us: inner(): pl.pallas_call(functools.partial(inner_kernel, along_rows), out_shape=(EX...]
    unnamed x21 -> x25, local copies, waits for them, and re-layouts: 5.79 us -> 9.94 us
    ppermute x3, waiting for transfers between devices: 11 us -> 7.49 us  [beside(): hi = lax.ppermute(head, axis, [(i + 1, i) for i in range(ends)])]
  transfers between devices with their start and end apart: 6 -> 6, of which waited for: 6 -> 3; matrix products, arithmetic and copies ran while one was open for 0% -> 1% of each run, Pallas kernels for 5% -> 26%
where the time goes in v2:
time: 214 us; the launch traced here: 212 us
  Pallas kernels  104 us (49%)
  blocking collectives  65.6 us (31%)
  starting transfers between devices  17.2 us (8%)
  local copies, waits for them, and re-layouts  12 us (6%)
  waiting for transfers between devices  11.8 us (6%)
    all_to_all x1, blocking collectives, on_device(): lax.all_to_all(outgoing, ('inline', 'crosslin'), split_axis=0, concat_axi...  65.6 us
    pallas_call x3, Pallas kernels, inner(): pl.pallas_call(functools.partial(inner_kernel, along_rows), out_shape=(EX...  41.4 us
    pallas_call x2, Pallas kernels, outer(): pl.pallas_call(functools.partial(outer_kernel, along_rows), out_shape=(EX...  18.3 us
    pallas_call x1, Pallas kernels, last(): pl.pallas_call(last_kernel, out_shape=(jax.ShapeDtypeStruct((TILE, TILE,...  14.1 us
    pallas_call x2, Pallas kernels, make_lists(): pl.pallas_call(functools.partial(lists_kernel, along_rows), out_shape=(ja...  13.5 us
    unnamed x25, local copies, waits for them, and re-layouts  9.94 us
    ppermute x3, starting transfers between devices, beside(): lo = lax.ppermute(tail, axis, [(i, i + 1) for i in range(ends)])  9.36 us
    pallas_call x1, Pallas kernels, put_bins(): pl.pallas_call(bin_kernel, out_shape=(FULL, EDGE, EDGE), in_specs=[SM, SM...  9.26 us
  transfers between devices with their start and end apart: 6, of which 3 were waited for; matrix products, arithmetic and copies ran while one was open for 1% of the time, Pallas kernels for 26%

profile of v2, /device:TPU:56, one launch (start us, length us, event | category | flops | bytes accessed | tf_op | source)
XLA Modules:
  0.0 211.8 jit_solution(9915282069859815283)
XLA Ops:
  0.0 0.8 copy.15
  0.8 0.7 reshape.29.bins
  1.5 7.2 %pack.1 = f32[128,72,128]{2,1,0:T(8,128)} custom-call(s32[128]{0:T(128)} %bitcast.7, s32[512]{0:T(512)} %reshape.29.bins, f32[4096,128]{1,0:T(8,128)} %bitcast.6), custom_call_target="tpu_custom_call" | custom-call | tf_op jit(solution)/shard_map/pack/pallas_call | solution.py:68
  8.7 65.6 %all_to_all.5.x = f32[128,72,128]{2,1,0:T(8,128)S(1)} all-to-all(f32[128,72,128]{2,1,0:T(8,128)} %pack.1), channel_id=1, replica_groups=mesh['inline'=16,'crosslin'=8] {'inline','crosslin'}, dimensions={0} | all-to-all | bytes 9437184 | tf_op jit(solution)/shard_map/all_to_all | solution.py:369
  74.3 2.1 %copy-done.2 = f32[128,72,128]{2,1,0:T(8,128)} copy-done((f32[128,72,128]{2,1,0:T(8,128)}, f32[128,72,128]{2,1,0:T(8,128)S(1)}, u32[]{:S(2)}) %copy-start.2) | copy-done | bytes 4718616
  76.7 0.5 convert_reduce_fusion
  77.2 0.6 maximum_divide_fusion.scale
  77.8 9.3 %put_bins.1 = (f32[1024,8,128]{2,1,0:T(8,128)}, f32[224,8,128]{2,1,0:T(8,128)}, f32[224,8,128]{2,1,0:T(8,128)}) custom-call(s32[1024]{0:T(1024)} %copy-done.9, f32[1024]{0:T(1024)} %maximum_divide_fusion.scale, f32[128,72,128]{2,1,0:T(8,128)} %copy-done.2), custom_call_target="tpu_custom_call" | custom-call | tf_op jit(solution)/shard_map/put_bins/pallas_call | solution.py:167
  87.1 3.5 %collective-permute-start = (f32[224,8,128]{2,1,0:T(8,128)}, f32[224,8,128]{2,1,0:T(8,128)S(1)}, u32[]{:S(2)}, u32[]{:S(2)}) collective-permute-start(f32[224,8,128]{2,1,0:T(8,128)} %get-tuple-element.29), channel_id=1, source_target_pairs={{0,8},{8,16},{16,24},{24,32},{32,40},{40,48},{48,56},{56,64},{64,7... | collective-permute-start | bytes 2752520 | tf_op jit(solution)/shard_map/ppermute | solution.py:361
  90.6 2.3 %collective-permute-start.1 = (f32[224,8,128]{2,1,0:T(8,128)}, f32[224,8,128]{2,1,0:T(8,128)S(1)}, u32[]{:S(2)}, u32[]{:S(2)}) collective-permute-start(f32[224,8,128]{2,1,0:T(8,128)} %get-tuple-element.30), channel_id=1, source_target_pairs={{8,0},{16,8},{24,16},{32,24},{40,32},{48,40},{56,48},{64,56},{72,6... | collective-permute-start | bytes 2752520 | tf_op jit(solution)/shard_map/ppermute | solution.py:362
  92.9 0.7 reshape.26.dips
  93.6 7.3 %lists_rows.1 = (s32[5840]{0:T(1024)}, s32[10]{0:T(128)}) custom-call(s32[1024]{0:T(1024)} %reshape.26.dips), custom_call_target="tpu_custom_call" | custom-call | bytes 25165824 | tf_op jit(solution)/shard_map/lists_rows/pallas_call | solution.py:120
  100.9 13.8 %inner_rows.2 = (f32[72000,128]{1,0:T(8,128)S(1)}, f32[1025,8,128]{2,1,0:T(8,128)S(1)}) custom-call(s32[5840]{0:T(1024)} %get-tuple-element.25.table, s32[10]{0:T(128)} %get-tuple-element.26.count, f32[1024,8,128]{2,1,0:T(8,128)} %get-tuple-element.31.own), custom_call_target="tpu_custom_call" | custom-call | bytes 50331648 | tf_op jit(solution)/shard_map/inner_rows/pallas_call | solution.py:323
  114.7 2.0 collective-permute-done.1.hi
  116.7 0.9 copy-done.5
  117.6 9.0 %outer_rows.1 = (f32[72000,128]{1,0:T(8,128)S(1)}, f32[1025,8,128]{2,1,0:T(8,128)S(1)}, f32[224,8,128]{2,1,0:T(8,128)}, f32[224,8,128]{2,1,0:T(8,128)}) custom-call(s32[5840]{0:T(1024)} %get-tuple-element.25.table, s32[10]{0:T(128)} %get-tuple-element.26.count, f32[224,8,128]{2,1,0:T(8,128)} %copy-done.3, ...), custom_call_target="tpu_custom_call", output_to_operand_aliasing={{0}: (4, {}), {1}: (5, {})} | custom-call | tf_op jit(solution)/shard_map/outer_rows/pallas_call | solution.py:335
  126.6 1.9 copy-done.1
  128.6 1.9 collective-permute-start.2
  130.5 3.6 %collective-permute-start.3 = (f32[224,8,128]{2,1,0:T(8,128)}, f32[224,8,128]{2,1,0:T(8,128)S(1)}, u32[]{:S(2)}, u32[]{:S(2)}) collective-permute-start(f32[224,8,128]{2,1,0:T(8,128)} %get-tuple-element.35), channel_id=1, source_target_pairs={{1,0},{2,1},{3,2},{4,3},{5,4},{6,5},{7,6},{9,8},{10,9},{11,10},{12... | collective-permute-start | bytes 2752520 | tf_op jit(solution)/shard_map/ppermute | solution.py:362
  134.1 0.7 reshape.27.dips
  134.8 6.2 %lists_cols.1 = (s32[5840]{0:T(1024)}, s32[10]{0:T(128)}) custom-call(s32[1024]{0:T(1024)} %reshape.27.dips), custom_call_target="tpu_custom_call" | custom-call | bytes 25165824 | tf_op jit(solution)/shard_map/lists_cols/pallas_call | solution.py:120
  141.0 13.9 %inner_cols.1 = (f32[72000,128]{1,0:T(8,128)S(1)}, f32[1025,8,128]{2,1,0:T(8,128)S(1)}) custom-call(s32[5840]{0:T(1024)} %get-tuple-element.27.table, s32[10]{0:T(128)} %get-tuple-element.28.count, f32[1025,8,128]{2,1,0:T(8,128)} %copy-done.1), custom_call_target="tpu_custom_call" | custom-call | bytes 50331648 | tf_op jit(solution)/shard_map/inner_cols/pallas_call | solution.py:323
  154.9 0.9 copy-done.4
  156.1 9.2 %outer_cols.1 = (f32[72000,128]{1,0:T(8,128)S(1)}, f32[1025,8,128]{2,1,0:T(8,128)S(1)}, f32[224,8,128]{2,1,0:T(8,128)}, f32[224,8,128]{2,1,0:T(8,128)}) custom-call(s32[5840]{0:T(1024)} %get-tuple-element.27.table, s32[10]{0:T(128)} %get-tuple-element.28.count, f32[224,8,128]{2,1,0:T(8,128)} %copy-done.4, ...), custom_call_target="tpu_custom_call", output_to_operand_aliasing={{0}: (4, {}), {1}: (5, {})} | custom-call | tf_op jit(solution)/shard_map/outer_cols/pallas_call | solution.py:335
  165.4 1.9 copy-done
  167.3 3.9 %collective-permute-start.4 = (f32[224,8,128]{2,1,0:T(8,128)}, f32[224,8,128]{2,1,0:T(8,128)S(1)}, u32[]{:S(2)}, u32[]{:S(2)}) collective-permute-start(f32[224,8,128]{2,1,0:T(8,128)} %get-tuple-element.39), channel_id=1, source_target_pairs={{0,8},{8,16},{16,24},{24,32},{32,40},{40,48},{48,56},{56,64},{64,7... | collective-permute-start | bytes 2752520 | tf_op jit(solution)/shard_map/ppermute | solution.py:361
  171.3 1.9 collective-permute-start.5
  173.2 13.8 %inner_rows.3 = (f32[72000,128]{1,0:T(8,128)S(1)}, f32[1025,8,128]{2,1,0:T(8,128)S(1)}) custom-call(s32[5840]{0:T(1024)} %get-tuple-element.25.table, s32[10]{0:T(128)} %get-tuple-element.26.count, f32[1025,8,128]{2,1,0:T(8,128)} %copy-done), custom_call_target="tpu_custom_call" | custom-call | bytes 50331648 | tf_op jit(solution)/shard_map/inner_rows/pallas_call | solution.py:323
  187.0 4.3 %collective-permute-done.4.lo = f32[224,8,128]{2,1,0:T(8,128)S(1)} collective-permute-done((f32[224,8,128]{2,1,0:T(8,128)}, f32[224,8,128]{2,1,0:T(8,128)S(1)}, u32[]{:S(2)}, u32[]{:S(2)}) %collective-permute-start.4) | collective-permute-done | bytes 917536 | tf_op jit(solution)/shard_map/ppermute | solution.py:361
  191.2 5.5 %collective-permute-done.5.hi = f32[224,8,128]{2,1,0:T(8,128)S(1)} collective-permute-done((f32[224,8,128]{2,1,0:T(8,128)}, f32[224,8,128]{2,1,0:T(8,128)S(1)}, u32[]{:S(2)}, u32[]{:S(2)}) %collective-permute-start.5) | collective-permute-done | bytes 917536 | tf_op jit(solution)/shard_map/ppermute | solution.py:362
  196.7 1.0 copy-done.8
  197.7 14.1 %last.1 = (f32[32,32,1024]{2,1,0:T(8,128)}, f32[72000,128]{1,0:T(8,128)S(1)}, f32[1025,8,128]{2,1,0:T(8,128)S(1)}) custom-call(s32[5840]{0:T(1024)} %get-tuple-element.25.table, s32[10]{0:T(128)} %get-tuple-element.26.count, f32[224,8,128]{2,1,0:T(8,128)} %copy-done.7, f32[224,8,128]{2,1,0:T(8,128)} %copy-done.8, ...), custom_call_target="tpu_custom_call", output_to_operand_aliasing={{1}: (4, {}), {2}: (5, {})} | custom-call | tf_op jit(solution)/shard_map/last/pallas_call | solution.py:347
  (23 shorter events, 0.6 us)
Async XLA Ops:
  74.3 2.1 %copy-start.2 = (f32[128,72,128]{2,1,0:T(8,128)}, f32[128,72,128]{2,1,0:T(8,128)S(1)}, u32[]{:S(2)}) copy-start(f32[128,72,128]{2,1,0:T(8,128)S(1)} %all_to_all.5.x) | copy-start | bytes 14155780
  76.4 16.5 %copy-start.10 = (s32[32,32]{1,0:T(8,128)S(1)}, s32[32,32]{1,0:T(8,128)}, u32[]{:S(2)}) copy-start(s32[32,32]{1,0:T(8,128)} %param.8) | copy-start | bytes 12292
  76.7 1.1 copy-start.9
  87.1 27.6 %collective-permute-start = (f32[224,8,128]{2,1,0:T(8,128)}, f32[224,8,128]{2,1,0:T(8,128)S(1)}, u32[]{:S(2)}, u32[]{:S(2)}) collective-permute-start(f32[224,8,128]{2,1,0:T(8,128)} %get-tuple-element.29), channel_id=1, source_target_pairs={{0,8},{8,16},{16,24},{24,32},{32,40},{40,48},{48,56},{56,64},{64,7... | collective-permute-start | bytes 2752520 | tf_op jit(solution)/shard_map/ppermute | solution.py:361
  90.6 26.1 %collective-permute-start.1 = (f32[224,8,128]{2,1,0:T(8,128)}, f32[224,8,128]{2,1,0:T(8,128)S(1)}, u32[]{:S(2)}, u32[]{:S(2)}) collective-permute-start(f32[224,8,128]{2,1,0:T(8,128)} %get-tuple-element.30), channel_id=1, source_target_pairs={{8,0},{16,8},{24,16},{32,24},{40,32},{48,40},{56,48},{64,56},{72,6... | collective-permute-start | bytes 2752520 | tf_op jit(solution)/shard_map/ppermute | solution.py:362
  114.7 2.0 copy-start.3
  116.7 0.9 copy-start.5
  117.6 16.5 %copy-start.11 = (s32[32,32]{1,0:T(8,128)S(1)}, s32[32,32]{1,0:T(8,128)}, u32[]{:S(2)}) copy-start(s32[32,32]{1,0:T(8,128)} %param.9) | copy-start | bytes 12292
  126.6 1.9 copy-start.1
  128.6 26.3 %collective-permute-start.2 = (f32[224,8,128]{2,1,0:T(8,128)}, f32[224,8,128]{2,1,0:T(8,128)S(1)}, u32[]{:S(2)}, u32[]{:S(2)}) collective-permute-start(f32[224,8,128]{2,1,0:T(8,128)} %get-tuple-element.34), channel_id=1, source_target_pairs={{0,1},{1,2},{2,3},{3,4},{4,5},{5,6},{6,7},{8,9},{9,10},{10,11},{11... | collective-permute-start | bytes 2752520 | tf_op jit(solution)/shard_map/ppermute | solution.py:361
  130.5 24.4 %collective-permute-start.3 = (f32[224,8,128]{2,1,0:T(8,128)}, f32[224,8,128]{2,1,0:T(8,128)S(1)}, u32[]{:S(2)}, u32[]{:S(2)}) collective-permute-start(f32[224,8,128]{2,1,0:T(8,128)} %get-tuple-element.35), channel_id=1, source_target_pairs={{1,0},{2,1},{3,2},{4,3},{5,4},{6,5},{7,6},{9,8},{10,9},{11,10},{12... | collective-permute-start | bytes 2752520 | tf_op jit(solution)/shard_map/ppermute | solution.py:362
  154.9 0.9 copy-start.4
  154.9 1.2 copy-start.6
  165.4 1.9 copy-start
  167.3 23.9 %collective-permute-start.4 = (f32[224,8,128]{2,1,0:T(8,128)}, f32[224,8,128]{2,1,0:T(8,128)S(1)}, u32[]{:S(2)}, u32[]{:S(2)}) collective-permute-start(f32[224,8,128]{2,1,0:T(8,128)} %get-tuple-element.39), channel_id=1, source_target_pairs={{0,8},{8,16},{16,24},{24,32},{32,40},{40,48},{48,56},{56,64},{64,7... | collective-permute-start | bytes 2752520 | tf_op jit(solution)/shard_map/ppermute | solution.py:361
  171.3 25.4 %collective-permute-start.5 = (f32[224,8,128]{2,1,0:T(8,128)}, f32[224,8,128]{2,1,0:T(8,128)S(1)}, u32[]{:S(2)}, u32[]{:S(2)}) collective-permute-start(f32[224,8,128]{2,1,0:T(8,128)} %get-tuple-element.40), channel_id=1, source_target_pairs={{8,0},{16,8},{24,16},{32,24},{40,32},{48,40},{56,48},{64,56},{72,6... | collective-permute-start | bytes 2752520 | tf_op jit(solution)/shard_map/ppermute | solution.py:362
  191.2 5.5 %copy-start.7 = (f32[224,8,128]{2,1,0:T(8,128)}, f32[224,8,128]{2,1,0:T(8,128)S(1)}, u32[]{:S(2)}) copy-start(f32[224,8,128]{2,1,0:T(8,128)S(1)} %collective-permute-done.4.lo) | copy-start | bytes 2752516
  196.7 1.0 copy-start.8

commit v3 on v2

--- a/solution.py
+++ b/solution.py
@@ -15,7 +15,8 @@
 DEV = 128
 SUB, LANE = 8, 128
 SPAN = 40
-GROUP = 8
+GROUP = 16
+MORE = 4
 ROOM = 18 * TILE + GROUP
 PAY = 72
 HALO = HALF * TILE
@@ -116,22 +117,36 @@
             table[at * ROOM + n + u] = BINS
 
 
-def make_lists(dips, along_rows):
-    return pl.pallas_call(
-        functools.partial(lists_kernel, along_rows),
-        out_shape=(
-            jax.ShapeDtypeStruct((2 * DIPS * ROOM,), jnp.int32),
-            jax.ShapeDtypeStruct((2 * DIPS,), jnp.int32),
-        ),
-        in_specs=[SM],
-        out_specs=(SM, SM),
+def both_lists_kernel(dip_rows, dip_cols, table_rows, count_rows, table_cols, count_cols):
+    lists_kernel(True, dip_rows, table_rows, count_rows)
+    lists_kernel(False, dip_cols, table_cols, count_cols)
+
+
+def make_lists(dip_rows, dip_cols):
+    table = jax.ShapeDtypeStruct((2 * DIPS * ROOM,), jnp.int32)
+    count = jax.ShapeDtypeStruct((2 * DIPS,), jnp.int32)
+    table_rows, count_rows, table_cols, count_cols = pl.pallas_call(
+        both_lists_kernel,
+        out_shape=(table, count, table, count),
+        in_specs=[SM, SM],
+        out_specs=(SM,) * 4,
         compiler_params=params(),
         cost_estimate=pl.CostEstimate(flops=0, bytes_accessed=24 << 20, transcendentals=0),
-        name="lists_rows" if along_rows else "lists_cols",
-    )(dips)
-
-
-def bin_kernel(bins, scale, x, out, head, tail, *sums):
+        name="lists",
+    )(dip_rows, dip_cols)
+    return (table_rows, count_rows), (table_cols, count_cols)
+
+
+def bin_kernel(bins, scale, x_hbm, out, head, tail, x, sems, *sums):
+    chunk = DEV // MORE
+    copies = [
+        pltpu.make_async_copy(
+            x_hbm.at[pl.ds(q * chunk, chunk), pl.ds(0, 64)], x.at[pl.ds(q * chunk, chunk)], sems.at[q]
+        )
+        for q in range(MORE)
+    ]
+    for copy in copies:
+        copy.start()
     zero = jnp.zeros((SUB, LANE), jnp.float32)
 
     def clear(i, _):
@@ -148,7 +163,9 @@
                 sums[tr][b] += x[i, pl.ds(slot * 32 + tr * 8, 8), :]
         return 0
 
-    lax.fori_loop(0, DEV, add, 0, unroll=2)
+    for q in range(MORE):
+        copies[q].wait()
+        lax.fori_loop(q * chunk, (q + 1) * chunk, add, 0, unroll=2)
 
     def finish(i, _):
         out[i] = ((sums[0][i] + sums[1][i]) + (sums[2][i] + sums[3][i])) * scale[i]
@@ -167,20 +184,41 @@
     return pl.pallas_call(
         bin_kernel,
         out_shape=(FULL, EDGE, EDGE),
-        in_specs=[SM, SM, VM],
+        in_specs=[SM, SM, HB],
         out_specs=(VM, VM, VM),
-        scratch_shapes=[pltpu.VMEM((BINS + 1, SUB, LANE), jnp.float32) for _ in range(4)],
+        scratch_shapes=[
+            pltpu.VMEM((DEV, 64, LANE), jnp.float32),
+            pltpu.SemaphoreType.DMA((MORE,)),
+            *[pltpu.VMEM((BINS + 1, SUB, LANE), jnp.float32) for _ in range(4)],
+        ],
         compiler_params=params(),
         name="put_bins",
     )(bins, scale, x)
 
 
-def widen(ext, row, x, lane):
-    ext[pl.ds(row + 16, 8), :] = x
-    ext[pl.ds(row + 24, 8), :] = jnp.where(lane < 127, pltpu.roll(x, 127, 1), 0.0)
-    ext[pl.ds(row + 32, 8), :] = jnp.where(lane < 126, pltpu.roll(x, 126, 1), 0.0)
-    ext[pl.ds(row + 8, 8), :] = jnp.where(lane >= 1, pltpu.roll(x, 1, 1), 0.0)
-    ext[pl.ds(row, 8), :] = jnp.where(lane >= 2, pltpu.roll(x, 2, 1), 0.0)
+def shift_matrix():
+    k = lax.broadcasted_iota(jnp.int32, (2 * LANE, 4 * LANE), 0) % LANE
+    n = lax.broadcasted_iota(jnp.int32, (2 * LANE, 4 * LANE), 1)
+    block = n // LANE
+    move = jnp.where(block < 2, block - 2, block - 1)
+    return jnp.where(k == n % LANE + move, 1.0, 0.0).astype(jnp.bfloat16)
+
+
+def widen(ext, starts, x, mat):
+    n = x.shape[0]
+    flat = x.reshape(n * SUB, LANE)
+    high = flat.astype(jnp.bfloat16)
+    low = (flat - high.astype(jnp.float32)).astype(jnp.bfloat16)
+    moved = jnp.dot(
+        jnp.concatenate([high, low], axis=1), mat[...], preferred_element_type=jnp.float32
+    )
+    for u in range(n):
+        at = starts[u]
+        ext[pl.ds(at + 16, 8), :] = flat[u * 8 : u * 8 + 8]
+        for block, offset in enumerate((0, 8, 24, 32)):
+            ext[pl.ds(at + offset, 8), :] = moved[
+                u * 8 : u * 8 + 8, block * LANE : (block + 1) * LANE
+            ]
 
 
 WIDE = TILE + 2 * HALF
@@ -195,55 +233,62 @@
     return (b + 2 * HALF * (b >> 5)) * SPAN
 
 
-def inner_margins(ext, own, along_rows):
-    lane = lax.broadcasted_iota(jnp.int32, (SUB, LANE), 1)
+def inner_margins(ext, own_hbm, own, sems, mat, along_rows):
+    mat[...] = shift_matrix()
     shift = HALF * (ROW_PITCH if along_rows else COL_PITCH)
+    chunk = BINS // MORE
+    copies = [
+        pltpu.make_async_copy(
+            own_hbm.at[pl.ds(q * chunk, chunk)], own.at[pl.ds(q * chunk, chunk)], sems.at[q]
+        )
+        for q in range(MORE)
+    ]
+    for copy in copies:
+        copy.start()
 
     def row(r, _):
         first = start_of(r * TILE, along_rows) + shift
-
-        def inner(c, _):
-            widen(ext, pl.multiple_of(first + c * SPAN, 8), own[r * TILE + c], lane)
-            return 0
-
-        lax.fori_loop(0, TILE, inner, 0, unroll=16)
-        return 0
-
-    lax.fori_loop(0, TILE, row, 0)
-
-
-def outer_margins(ext, lo, hi, along_rows):
-    lane = lax.broadcasted_iota(jnp.int32, (SUB, LANE), 1)
-    if along_rows:
-
-        def row(r, _):
-            first = r * ROW_PITCH
-
-            def outer(c, _):
-                at = pl.multiple_of(first + c * SPAN, 8)
-                widen(ext, at, lo[r * TILE + c], lane)
-                widen(
-                    ext,
-                    pl.multiple_of(at + (TILE + HALF) * ROW_PITCH, 8),
-                    hi[r * TILE + c],
-                    lane,
-                )
+        starts = [pl.multiple_of(first + c * SPAN, 8) for c in range(TILE)]
+        widen(ext, starts, own[pl.ds(r * TILE, TILE)], mat)
+        return 0
+
+    for q in range(MORE):
+        copies[q].wait()
+        lax.fori_loop(q * TILE // MORE, (q + 1) * TILE // MORE, row, 0)
+
+
+def outer_margins(ext, lo_hbm, hi_hbm, lo, hi, sems, mat, along_rows):
+    copies = [
+        pltpu.make_async_copy(lo_hbm, lo, sems.at[0]),
+        pltpu.make_async_copy(hi_hbm, hi, sems.at[1]),
+    ]
+    for copy in copies:
+        copy.start()
+    mat[...] = shift_matrix()
+    for side, ref in enumerate((lo, hi)):
+        copies[side].wait()
+        beyond = side * (TILE + HALF)
+        if along_rows:
+
+            def row(r, _):
+                first = (r + beyond) * ROW_PITCH
+                starts = [pl.multiple_of(first + c * SPAN, 8) for c in range(TILE)]
+                widen(ext, starts, ref[pl.ds(r * TILE, TILE)], mat)
                 return 0
 
-            lax.fori_loop(0, TILE, outer, 0, unroll=8)
-            return 0
-
-        lax.fori_loop(0, HALF, row, 0)
-    else:
-
-        def row(r, _):
-            first = pl.multiple_of(r * WIDE * SPAN, 8)
-            for c in range(HALF):
-                widen(ext, first + c * SPAN, lo[r * HALF + c], lane)
-                widen(ext, first + (HALF + TILE + c) * SPAN, hi[r * HALF + c], lane)
-            return 0
-
-        lax.fori_loop(0, TILE, row, 0)
+            lax.fori_loop(0, HALF, row, 0)
+        else:
+
+            def four_rows(q, _):
+                starts = [
+                    pl.multiple_of(((q * 4 + p) * WIDE + beyond + c) * SPAN, 8)
+                    for p in range(4)
+                    for c in range(HALF)
+                ]
+                widen(ext, starts, ref[pl.ds(q * 4 * HALF, 4 * HALF)], mat)
+                return 0
+
+            lax.fori_loop(0, TILE // 4, four_rows, 0)
 
 
 def steer(table, count, part, ext, along_rows, acc):
@@ -269,13 +314,15 @@
         lax.fori_loop(0, (count[at] + GROUP - 1) // GROUP, group, 0)
 
 
-def inner_kernel(along_rows, table, count, own, ext, acc):
-    inner_margins(ext, own, along_rows)
+def inner_kernel(along_rows, table, count, own_hbm, ext, acc, own, sems, mat):
+    inner_margins(ext, own_hbm, own, sems, mat, along_rows)
     steer(table, count, 0, ext, along_rows, acc)
 
 
-def outer_kernel(along_rows, table, count, lo, hi, ext_in, acc_in, ext, acc, one, two):
-    outer_margins(ext, lo, hi, along_rows)
+def outer_kernel(
+    along_rows, table, count, lo_hbm, hi_hbm, ext_in, acc_in, ext, acc, one, two, lo, hi, sems, mat
+):
+    outer_margins(ext, lo_hbm, hi_hbm, lo, hi, sems, mat, along_rows)
     steer(table, count, 1, ext, along_rows, acc)
     if along_rows:
 
@@ -291,24 +338,34 @@
         two[...] = acc[pl.ds(BINS - HALO, HALO)]
 
 
-def natural(acc, out, z, i):
-    for ti in range(SUB):
-        z[pl.ds(ti, 128, stride=8), :] = acc[pl.ds(i * 128, 128), ti, :].T
-    for j in range(8):
-        out[pl.ds(i * 4, 4), :, pl.ds(j * 128, 128)] = (
-            z[pl.ds(j * 128, 128), :].T.reshape(4, 32, 128)
-        )
-
-
-def last_kernel(table, count, lo, hi, ext_in, acc_in, out, ext, acc, z):
-    outer_margins(ext, lo, hi, True)
+def natural(acc, out_hbm, z, parts, sems, groups):
+    copies = []
+    for slot, i in enumerate(groups):
+        for ti in range(SUB):
+            z[pl.ds(ti, 128, stride=8), :] = acc[pl.ds(i * 128, 128), ti, :].T
+        for j in range(8):
+            parts[slot, :, :, pl.ds(j * 128, 128)] = (
+                z[pl.ds(j * 128, 128), :].T.reshape(4, TILE, 128)
+            )
+        copy = pltpu.make_async_copy(parts.at[slot], out_hbm.at[pl.ds(i * 4, 4)], sems.at[slot])
+        copy.start()
+        copies.append(copy)
+    for copy in copies:
+        copy.wait()
+
+
+def inner_last_kernel(table, count, own_hbm, ext, acc, out_hbm, own, sems, mat, z, parts, outs):
+    inner_kernel(True, table, count, own_hbm, ext, acc, own, sems, mat)
+    natural(acc, out_hbm, z, parts, outs, (2, 3, 4, 5))
+
+
+def last_kernel(
+    table, count, lo_hbm, hi_hbm, ext_in, acc_in, out_in, ext, acc, out_hbm,
+    lo, hi, sems, mat, z, parts, outs,
+):
+    outer_margins(ext, lo_hbm, hi_hbm, lo, hi, sems, mat, True)
     steer(table, count, 1, ext, True, acc)
-
-    def four(i, _):
-        natural(acc, out, z, i)
-        return 0
-
-    lax.fori_loop(0, 8, four, 0)
+    natural(acc, out_hbm, z, parts, outs, (0, 1, 6, 7))
 
 
 EXT = pltpu.VMEM((EXT_ROWS, LANE), jnp.float32)
@@ -319,14 +376,35 @@
     return pltpu.CompilerParams(vmem_limit_bytes=16 << 20)
 
 
+OWN = [
+    pltpu.VMEM((BINS, SUB, LANE), jnp.float32),
+    pltpu.SemaphoreType.DMA((MORE,)),
+    pltpu.VMEM((2 * LANE, 4 * LANE), jnp.bfloat16),
+]
+SIDES = [
+    pltpu.VMEM((HALO, SUB, LANE), jnp.float32),
+    pltpu.VMEM((HALO, SUB, LANE), jnp.float32),
+    pltpu.SemaphoreType.DMA((2,)),
+    pltpu.VMEM((2 * LANE, 4 * LANE), jnp.bfloat16),
+]
+PARTS = [
+    pltpu.VMEM((1024, LANE), jnp.float32),
+    pltpu.VMEM((4, 4, TILE, SUB * LANE), jnp.float32),
+    pltpu.SemaphoreType.DMA((4,)),
+]
+RESULT = jax.ShapeDtypeStruct((TILE, TILE, SUB * LANE), jnp.float32)
+BUSY = pl.CostEstimate(flops=0, bytes_accessed=48 << 20, transcendentals=0)
+
+
 def inner(lists, own, along_rows):
     return pl.pallas_call(
         functools.partial(inner_kernel, along_rows),
         out_shape=(EXT, ACC),
-        in_specs=[SM, SM, VM],
+        in_specs=[SM, SM, HB],
         out_specs=(VM, VM),
+        scratch_shapes=OWN,
         compiler_params=small(),
-        cost_estimate=pl.CostEstimate(flops=0, bytes_accessed=48 << 20, transcendentals=0),
+        cost_estimate=BUSY,
         name="inner_rows" if along_rows else "inner_cols",
     )(*lists, own)
 
@@ -335,25 +413,39 @@
     return pl.pallas_call(
         functools.partial(outer_kernel, along_rows),
         out_shape=(EXT, ACC, EDGE, EDGE),
-        in_specs=[SM, SM, VM, VM, VM, VM],
+        in_specs=[SM, SM, HB, HB, VM, VM],
         out_specs=(VM, VM, VM, VM),
+        scratch_shapes=SIDES,
         input_output_aliases={4: 0, 5: 1},
         compiler_params=small(),
         name="outer_rows" if along_rows else "outer_cols",
     )(*lists, lo, hi, *kept)[1:]
 
 
+def inner_last(lists, own):
+    return pl.pallas_call(
+        inner_last_kernel,
+        out_shape=(EXT, ACC, RESULT),
+        in_specs=[SM, SM, HB],
+        out_specs=(VM, VM, HB),
+        scratch_shapes=OWN + PARTS,
+        compiler_params=small(),
+        cost_estimate=BUSY,
+        name="inner_last",
+    )(*lists, own)
+
+
 def last(lists, lo, hi, kept):
     return pl.pallas_call(
         last_kernel,
-        out_shape=(jax.ShapeDtypeStruct((TILE, TILE, SUB * LANE), jnp.float32), EXT, ACC),
-        in_specs=[SM, SM, VM, VM, VM, VM],
-        out_specs=(VM, VM, VM),
-        input_output_aliases={4: 1, 5: 2},
-        scratch_shapes=[pltpu.VMEM((1024, LANE), jnp.float32)],
+        out_shape=(EXT, ACC, RESULT),
+        in_specs=[SM, SM, HB, HB, VM, VM, HB],
+        out_specs=(VM, VM, HB),
+        scratch_shapes=SIDES + PARTS,
+        input_output_aliases={4: 0, 5: 1, 6: 2},
         compiler_params=small(),
         name="last",
-    )(*lists, lo, hi, *kept)[0]
+    )(*lists, lo, hi, *kept)[2]
 
 
 def beside(head, tail, axis):
@@ -369,8 +461,7 @@
     arrived = lax.all_to_all(
         outgoing, ("inline", "crosslin"), split_axis=0, concat_axis=0, tiled=True
     )
-    rows = make_lists(dip_inline.reshape(-1), True)
-    cols = make_lists(dip_cross.reshape(-1), False)
+    rows, cols = make_lists(dip_inline.reshape(-1), dip_cross.reshape(-1))
     bins = arrived[:, 64, :8].astype(jnp.int32).reshape(-1)
     fold = jnp.sum(
         (jnp.arange(BINS, dtype=jnp.int32)[:, None] == bins[None, :]).astype(jnp.float32), axis=1
@@ -383,7 +474,7 @@
     kept = inner(cols, first, False)
     second, head, tail = outer(cols, lo, hi, kept, False)
     lo, hi = beside(head, tail, "inline")
-    kept = inner(rows, second, True)
+    kept = inner_last(rows, second)
     return last(rows, lo, hi, kept)
 
 

time: 214 us -> 205 us (0.958)
  Pallas kernels: 104 us -> 95.1 us
  waiting for transfers between devices: 11.8 us -> 8.82 us
    pallas_call x3 -> x2, Pallas kernels: 41.4 us -> 24.4 us  [inner(): pl.pallas_call(functools.partial(inner_kernel, along_rows), out_shape=(EX...]
    pallas_call x3, Pallas kernels: 27.6 us -> 37.7 us  [the longest x1 15.2 us: inner_last(): pl.pallas_call(inner_last_kernel, out_shape=(EXT, ACC, RESULT), in_specs=...]
  transfers between devices with their start and end apart: 6 -> 6, of which waited for: 3 -> 2; matrix products, arithmetic and copies ran while one was open for 1% -> 1% of each run, Pallas kernels for 26% -> 26%
where the time goes in v3:
time: 205 us; the launch traced here: 203 us
  Pallas kernels  95.1 us (46%)
  blocking collectives  65.6 us (32%)
  starting transfers between devices  19 us (9%)
  local copies, waits for them, and re-layouts  12.3 us (6%)
  waiting for transfers between devices  8.82 us (4%)
    all_to_all x1, blocking collectives, on_device(): lax.all_to_all(outgoing, ('inline', 'crosslin'), split_axis=0, concat_axi...  65.6 us
    pallas_call x2, Pallas kernels, inner(): pl.pallas_call(functools.partial(inner_kernel, along_rows), out_shape=(EX...  24.4 us
    pallas_call x2, Pallas kernels, outer(): pl.pallas_call(functools.partial(outer_kernel, along_rows), out_shape=(EX...  18.2 us
    pallas_call x1, Pallas kernels, inner_last(): pl.pallas_call(inner_last_kernel, out_shape=(EXT, ACC, RESULT), in_specs=...  15.2 us
    pallas_call x1, Pallas kernels, make_lists(): pl.pallas_call(both_lists_kernel, out_shape=(table, count, table, count),...  12.2 us
    ppermute x3, starting transfers between devices, beside(): lo = lax.ppermute(tail, axis, [(i, i + 1) for i in range(ends)])  11.1 us
    pallas_call x1, Pallas kernels, last(): pl.pallas_call(last_kernel, out_shape=(EXT, ACC, RESULT), in_specs=[SM, S...  10.4 us
    unnamed x25, local copies, waits for them, and re-layouts  10.2 us
  transfers between devices with their start and end apart: 6, of which 2 were waited for; matrix products, arithmetic and copies ran while one was open for 1% of the time, Pallas kernels for 26%

profile of v3, /device:TPU:56, one launch (start us, length us, event | category | flops | bytes accessed | tf_op | source)
XLA Modules:
  0.0 202.5 jit_solution(6233555595798485505)
XLA Ops:
  0.0 0.8 copy.16
  0.8 0.7 reshape.29.bins
  1.5 7.2 %pack.1 = f32[128,72,128]{2,1,0:T(8,128)} custom-call(s32[128]{0:T(128)} %bitcast.7, s32[512]{0:T(512)} %reshape.29.bins, f32[4096,128]{1,0:T(8,128)} %bitcast.6), custom_call_target="tpu_custom_call" | custom-call | tf_op jit(solution)/shard_map/pack/pallas_call | solution.py:69
  8.7 65.6 %all_to_all.5.x_hbm = f32[128,72,128]{2,1,0:T(8,128)S(1)} all-to-all(f32[128,72,128]{2,1,0:T(8,128)} %pack.1), channel_id=1, replica_groups=mesh['inline'=16,'crosslin'=8] {'inline','crosslin'}, dimensions={0} | all-to-all | bytes 9437184 | tf_op jit(solution)/shard_map/all_to_all | solution.py:461
  74.3 2.1 %copy-done.2 = f32[128,72,128]{2,1,0:T(8,128)} copy-done((f32[128,72,128]{2,1,0:T(8,128)}, f32[128,72,128]{2,1,0:T(8,128)S(1)}, u32[]{:S(2)}) %copy-start.2) | copy-done | bytes 4718616
  76.7 0.5 convert_reduce_fusion
  77.2 0.6 maximum_divide_fusion.scale
  77.8 7.7 %put_bins.1 = (f32[1024,8,128]{2,1,0:T(8,128)}, f32[224,8,128]{2,1,0:T(8,128)}, f32[224,8,128]{2,1,0:T(8,128)}) custom-call(s32[1024]{0:T(1024)} %copy-done.9, f32[1024]{0:T(1024)} %maximum_divide_fusion.scale, f32[128,72,128]{2,1,0:T(8,128)} %copy-done.2), custom_call_target="tpu_custom_call" | custom-call | tf_op jit(solution)/shard_map/put_bins/pallas_call | solution.py:184
  85.5 3.5 %collective-permute-start = (f32[224,8,128]{2,1,0:T(8,128)}, f32[224,8,128]{2,1,0:T(8,128)S(1)}, u32[]{:S(2)}, u32[]{:S(2)}) collective-permute-start(f32[224,8,128]{2,1,0:T(8,128)} %get-tuple-element.30), channel_id=1, source_target_pairs={{0,8},{8,16},{16,24},{24,32},{32,40},{40,48},{48,56},{56,64},{64,7... | collective-permute-start | bytes 2752520 | tf_op jit(solution)/shard_map/ppermute | solution.py:453
  89.0 2.3 %collective-permute-start.1 = (f32[224,8,128]{2,1,0:T(8,128)}, f32[224,8,128]{2,1,0:T(8,128)S(1)}, u32[]{:S(2)}, u32[]{:S(2)}) collective-permute-start(f32[224,8,128]{2,1,0:T(8,128)} %get-tuple-element.31), channel_id=1, source_target_pairs={{8,0},{16,8},{24,16},{32,24},{40,32},{48,40},{56,48},{64,56},{72,6... | collective-permute-start | bytes 2752520 | tf_op jit(solution)/shard_map/ppermute | solution.py:454
  91.4 0.7 reshape.26.dip_rows
  92.0 0.7 reshape.27.dip_cols
  92.7 12.2 %lists.1 = (s32[5920]{0:T(1024)}, s32[10]{0:T(128)}, s32[5920]{0:T(1024)}, s32[10]{0:T(128)}) custom-call(s32[1024]{0:T(1024)} %reshape.26.dip_rows, s32[1024]{0:T(1024)} %reshape.27.dip_cols), custom_call_target="tpu_custom_call" | custom-call | bytes 25165824 | tf_op jit(solution)/shard_map/lists/pallas_call | solution.py:128
  104.9 12.2 %inner_rows.1 = (f32[72000,128]{1,0:T(8,128)S(1)}, f32[1025,8,128]{2,1,0:T(8,128)S(1)}) custom-call(s32[5920]{0:T(1024)} %get-tuple-element.26.table, s32[10]{0:T(128)} %get-tuple-element.27.count, f32[1024,8,128]{2,1,0:T(8,128)} %get-tuple-element.32.own_hbm), custom_call_target="tpu_custom_call" | custom-call | bytes 50331648 | tf_op jit(solution)/shard_map/inner_rows/pallas_call | solution.py:400
  117.1 0.9 copy-done.3
  118.0 0.3 copy-done.4
  118.3 9.0 %outer_rows.1 = (f32[72000,128]{1,0:T(8,128)S(1)}, f32[1025,8,128]{2,1,0:T(8,128)S(1)}, f32[224,8,128]{2,1,0:T(8,128)}, f32[224,8,128]{2,1,0:T(8,128)}) custom-call(s32[5920]{0:T(1024)} %get-tuple-element.26.table, s32[10]{0:T(128)} %get-tuple-element.27.count, f32[224,8,128]{2,1,0:T(8,128)} %copy-done.3, ...), custom_call_target="tpu_custom_call", output_to_operand_aliasing={{0}: (4, {}), {1}: (5, {})} | custom-call | tf_op jit(solution)/shard_map/outer_rows/pallas_call | solution.py:413
  127.4 1.9 copy-done.1
  129.3 1.9 collective-permute-start.2
  131.2 3.6 %collective-permute-start.3 = (f32[224,8,128]{2,1,0:T(8,128)}, f32[224,8,128]{2,1,0:T(8,128)S(1)}, u32[]{:S(2)}, u32[]{:S(2)}) collective-permute-start(f32[224,8,128]{2,1,0:T(8,128)} %get-tuple-element.36), channel_id=1, source_target_pairs={{1,0},{2,1},{3,2},{4,3},{5,4},{6,5},{7,6},{9,8},{10,9},{11,10},{12... | collective-permute-start | bytes 2752520 | tf_op jit(solution)/shard_map/ppermute | solution.py:454
  134.9 12.2 %inner_cols.1 = (f32[72000,128]{1,0:T(8,128)S(1)}, f32[1025,8,128]{2,1,0:T(8,128)S(1)}) custom-call(s32[5920]{0:T(1024)} %get-tuple-element.28.table, s32[10]{0:T(128)} %get-tuple-element.29.count, f32[1025,8,128]{2,1,0:T(8,128)} %copy-done.1), custom_call_target="tpu_custom_call" | custom-call | bytes 50331648 | tf_op jit(solution)/shard_map/inner_cols/pallas_call | solution.py:400
  147.1 0.9 copy-done.5
  148.0 0.3 copy-done.7
  148.3 9.1 %outer_cols.1 = (f32[72000,128]{1,0:T(8,128)S(1)}, f32[1025,8,128]{2,1,0:T(8,128)S(1)}, f32[224,8,128]{2,1,0:T(8,128)}, f32[224,8,128]{2,1,0:T(8,128)}) custom-call(s32[5920]{0:T(1024)} %get-tuple-element.28.table, s32[10]{0:T(128)} %get-tuple-element.29.count, f32[224,8,128]{2,1,0:T(8,128)} %copy-done.5, ...), custom_call_target="tpu_custom_call", output_to_operand_aliasing={{0}: (4, {}), {1}: (5, {})} | custom-call | tf_op jit(solution)/shard_map/outer_cols/pallas_call | solution.py:413
  157.5 1.9 copy-done
  159.4 5.7 %collective-permute-start.4 = (f32[224,8,128]{2,1,0:T(8,128)}, f32[224,8,128]{2,1,0:T(8,128)S(1)}, u32[]{:S(2)}, u32[]{:S(2)}) collective-permute-start(f32[224,8,128]{2,1,0:T(8,128)} %get-tuple-element.40), channel_id=1, source_target_pairs={{0,8},{8,16},{16,24},{24,32},{32,40},{40,48},{48,56},{56,64},{64,7... | collective-permute-start | bytes 2752520 | tf_op jit(solution)/shard_map/ppermute | solution.py:453
  165.1 1.9 collective-permute-start.5
  167.0 15.2 %inner_last.1 = (f32[72000,128]{1,0:T(8,128)S(1)}, f32[1025,8,128]{2,1,0:T(8,128)S(1)}, f32[32,32,1024]{2,1,0:T(8,128)}) custom-call(s32[5920]{0:T(1024)} %get-tuple-element.26.table, s32[10]{0:T(128)} %get-tuple-element.27.count, f32[1025,8,128]{2,1,0:T(8,128)} %copy-done), custom_call_target="tpu_custom_call" | custom-call | bytes 50331648 | tf_op jit(solution)/shard_map/inner_last/pallas_call | solution.py:426
  182.2 2.7 %collective-permute-done.4.lo_hbm = f32[224,8,128]{2,1,0:T(8,128)S(1)} collective-permute-done((f32[224,8,128]{2,1,0:T(8,128)}, f32[224,8,128]{2,1,0:T(8,128)S(1)}, u32[]{:S(2)}, u32[]{:S(2)}) %collective-permute-start.4) | collective-permute-done | bytes 917536 | tf_op jit(solution)/shard_map/ppermute | solution.py:453
  184.9 6.1 %collective-permute-done.5.hi_hbm = f32[224,8,128]{2,1,0:T(8,128)S(1)} collective-permute-done((f32[224,8,128]{2,1,0:T(8,128)}, f32[224,8,128]{2,1,0:T(8,128)S(1)}, u32[]{:S(2)}, u32[]{:S(2)}) %collective-permute-start.5) | collective-permute-done | bytes 917536 | tf_op jit(solution)/shard_map/ppermute | solution.py:454
  191.0 1.0 copy-done.8
  192.0 10.4 %last.1 = (f32[72000,128]{1,0:T(8,128)S(1)}, f32[1025,8,128]{2,1,0:T(8,128)S(1)}, f32[32,32,1024]{2,1,0:T(8,128)}) custom-call(s32[5920]{0:T(1024)} %get-tuple-element.26.table, s32[10]{0:T(128)} %get-tuple-element.27.count, f32[224,8,128]{2,1,0:T(8,128)} %copy-done.6, ...), custom_call_target="tpu_custom_call", output_to_operand_aliasing={{0}: (4, {}), {1}: (5, {}), {2}: (6, {})} | custom-call | tf_op jit(solution)/shard_map/last/pallas_call | solution.py:439
  (22 shorter events, 0.3 us)
Async XLA Ops:
  74.3 2.1 %copy-start.2 = (f32[128,72,128]{2,1,0:T(8,128)}, f32[128,72,128]{2,1,0:T(8,128)S(1)}, u32[]{:S(2)}) copy-start(f32[128,72,128]{2,1,0:T(8,128)S(1)} %all_to_all.5.x_hbm) | copy-start | bytes 14155780
  76.4 14.9 %copy-start.10 = (s32[32,32]{1,0:T(8,128)S(1)}, s32[32,32]{1,0:T(8,128)}, u32[]{:S(2)}) copy-start(s32[32,32]{1,0:T(8,128)} %param.8) | copy-start | bytes 12292
  76.4 15.6 %copy-start.11 = (s32[32,32]{1,0:T(8,128)S(1)}, s32[32,32]{1,0:T(8,128)}, u32[]{:S(2)}) copy-start(s32[32,32]{1,0:T(8,128)} %param.9) | copy-start | bytes 12292
  76.7 1.1 copy-start.9
  85.5 31.6 %collective-permute-start = (f32[224,8,128]{2,1,0:T(8,128)}, f32[224,8,128]{2,1,0:T(8,128)S(1)}, u32[]{:S(2)}, u32[]{:S(2)}) collective-permute-start(f32[224,8,128]{2,1,0:T(8,128)} %get-tuple-element.30), channel_id=1, source_target_pairs={{0,8},{8,16},{16,24},{24,32},{32,40},{40,48},{48,56},{56,64},{64,7... | collective-permute-start | bytes 2752520 | tf_op jit(solution)/shard_map/ppermute | solution.py:453
  89.0 28.1 %collective-permute-start.1 = (f32[224,8,128]{2,1,0:T(8,128)}, f32[224,8,128]{2,1,0:T(8,128)S(1)}, u32[]{:S(2)}, u32[]{:S(2)}) collective-permute-start(f32[224,8,128]{2,1,0:T(8,128)} %get-tuple-element.31), channel_id=1, source_target_pairs={{8,0},{16,8},{24,16},{32,24},{40,32},{48,40},{56,48},{64,56},{72,6... | collective-permute-start | bytes 2752520 | tf_op jit(solution)/shard_map/ppermute | solution.py:454
  117.1 0.9 copy-start.3
  117.1 1.2 copy-start.4
  127.4 1.9 copy-start.1
  129.3 17.8 %collective-permute-start.2 = (f32[224,8,128]{2,1,0:T(8,128)}, f32[224,8,128]{2,1,0:T(8,128)S(1)}, u32[]{:S(2)}, u32[]{:S(2)}) collective-permute-start(f32[224,8,128]{2,1,0:T(8,128)} %get-tuple-element.35), channel_id=1, source_target_pairs={{0,1},{1,2},{2,3},{3,4},{4,5},{5,6},{6,7},{8,9},{9,10},{10,11},{11... | collective-permute-start | bytes 2752520 | tf_op jit(solution)/shard_map/ppermute | solution.py:453
  131.2 15.9 %collective-permute-start.3 = (f32[224,8,128]{2,1,0:T(8,128)}, f32[224,8,128]{2,1,0:T(8,128)S(1)}, u32[]{:S(2)}, u32[]{:S(2)}) collective-permute-start(f32[224,8,128]{2,1,0:T(8,128)} %get-tuple-element.36), channel_id=1, source_target_pairs={{1,0},{2,1},{3,2},{4,3},{5,4},{6,5},{7,6},{9,8},{10,9},{11,10},{12... | collective-permute-start | bytes 2752520 | tf_op jit(solution)/shard_map/ppermute | solution.py:454
  147.1 0.9 copy-start.5
  147.1 1.2 copy-start.7
  157.5 1.9 copy-start
  159.4 25.5 %collective-permute-start.4 = (f32[224,8,128]{2,1,0:T(8,128)}, f32[224,8,128]{2,1,0:T(8,128)S(1)}, u32[]{:S(2)}, u32[]{:S(2)}) collective-permute-start(f32[224,8,128]{2,1,0:T(8,128)} %get-tuple-element.40), channel_id=1, source_target_pairs={{0,8},{8,16},{16,24},{24,32},{32,40},{40,48},{48,56},{56,64},{64,7... | collective-permute-start | bytes 2752520 | tf_op jit(solution)/shard_map/ppermute | solution.py:453
  165.1 25.9 %collective-permute-start.5 = (f32[224,8,128]{2,1,0:T(8,128)}, f32[224,8,128]{2,1,0:T(8,128)S(1)}, u32[]{:S(2)}, u32[]{:S(2)}) collective-permute-start(f32[224,8,128]{2,1,0:T(8,128)} %get-tuple-element.41), channel_id=1, source_target_pairs={{8,0},{16,8},{24,16},{32,24},{40,32},{48,40},{56,48},{64,56},{72,6... | collective-permute-start | bytes 2752520 | tf_op jit(solution)/shard_map/ppermute | solution.py:454
  184.9 6.1 %copy-start.6 = (f32[224,8,128]{2,1,0:T(8,128)}, f32[224,8,128]{2,1,0:T(8,128)S(1)}, u32[]{:S(2)}) copy-start(f32[224,8,128]{2,1,0:T(8,128)S(1)} %collective-permute-done.4.lo_hbm) | copy-start | bytes 2752516
  191.0 1.0 copy-start.8

commit v4 on v3

--- a/solution.py
+++ b/solution.py
@@ -84,6 +84,63 @@
     )(dest, bins, x)
 
 
+USED = 65
+
+
+def exchange_kernel(x, out, send, recv, near):
+    inline, crosslin = lax.axis_size("inline"), lax.axis_size("crosslin")
+    i, j = lax.axis_index("inline"), lax.axis_index("crosslin")
+    me = i * crosslin + j
+
+    def peer(s):
+        return lax.rem(i + s // crosslin, inline), lax.rem(j + lax.rem(s, crosslin), crosslin)
+
+    barrier = pltpu.get_barrier_semaphore()
+
+    def greet(s, _):
+        pl.semaphore_signal(
+            barrier, inc=1, device_id=peer(s), device_id_type=pl.DeviceIdType.MESH
+        )
+        return 0
+
+    lax.fori_loop(1, DEV, greet, 0)
+    stay = pltpu.make_async_copy(x.at[me, pl.ds(0, USED)], out.at[me, pl.ds(0, USED)], near)
+    stay.start()
+    pl.semaphore_wait(barrier, DEV - 1)
+
+    def post(s, _):
+        pi, pj = peer(s)
+        pltpu.make_async_remote_copy(
+            src_ref=x.at[pi * crosslin + pj, pl.ds(0, USED)],
+            dst_ref=out.at[me, pl.ds(0, USED)],
+            send_sem=send,
+            recv_sem=recv,
+            device_id=(pi, pj),
+            device_id_type=pl.DeviceIdType.MESH,
+        ).start()
+        return 0
+
+    lax.fori_loop(1, DEV, post, 0)
+    stay.wait()
+    rest = x.at[pl.ds(0, DEV - 1), pl.ds(0, USED)]
+    pltpu.make_async_copy(rest, rest, send).wait()
+    pltpu.make_async_copy(rest, rest, recv).wait()
+
+
+def exchange(x):
+    return pl.pallas_call(
+        exchange_kernel,
+        out_shape=jax.ShapeDtypeStruct((DEV, PAY, LANE), jnp.float32),
+        in_specs=[HB],
+        out_specs=HB,
+        scratch_shapes=[pltpu.SemaphoreType.DMA] * 3,
+        compiler_params=pltpu.CompilerParams(
+            collective_id=0, has_side_effects=True, vmem_limit_bytes=62 << 20
+        ),
+        name="exchange",
+    )(x)
+
+
 def add_bin(dips, table, count, i, part):
     at = part * DIPS + dips[i] + DMAX
     n = count[at]
@@ -372,8 +429,8 @@
 ACC = pltpu.VMEM((BINS + 1, SUB, LANE), jnp.float32)
 
 
-def small():
-    return pltpu.CompilerParams(vmem_limit_bytes=16 << 20)
+def small(mib):
+    return pltpu.CompilerParams(vmem_limit_bytes=mib << 20)
 
 
 OWN = [
@@ -403,7 +460,7 @@
         in_specs=[SM, SM, HB],
         out_specs=(VM, VM),
         scratch_shapes=OWN,
-        compiler_params=small(),
+        compiler_params=small(12),
         cost_estimate=BUSY,
         name="inner_rows" if along_rows else "inner_cols",
     )(*lists, own)
@@ -417,7 +474,7 @@
         out_specs=(VM, VM, VM, VM),
         scratch_shapes=SIDES,
         input_output_aliases={4: 0, 5: 1},
-        compiler_params=small(),
+        compiler_params=small(12),
         name="outer_rows" if along_rows else "outer_cols",
     )(*lists, lo, hi, *kept)[1:]
 
@@ -429,7 +486,7 @@
         in_specs=[SM, SM, HB],
         out_specs=(VM, VM, HB),
         scratch_shapes=OWN + PARTS,
-        compiler_params=small(),
+        compiler_params=small(12),
         cost_estimate=BUSY,
         name="inner_last",
     )(*lists, own)
@@ -443,7 +500,7 @@
         out_specs=(VM, VM, HB),
         scratch_shapes=SIDES + PARTS,
         input_output_aliases={4: 0, 5: 1, 6: 2},
-        compiler_params=small(),
+        compiler_params=small(12),
         name="last",
     )(*lists, lo, hi, *kept)[2]
 
@@ -458,9 +515,7 @@
 def on_device(traces, destination, bin_index, dip_inline, dip_cross):
     x = traces.reshape(DEV, 4, 8, 128).transpose(0, 2, 1, 3).reshape(4096, 128)
     outgoing = pack(destination.reshape(-1), bin_index.reshape(-1), x)
-    arrived = lax.all_to_all(
-        outgoing, ("inline", "crosslin"), split_axis=0, concat_axis=0, tiled=True
-    )
+    arrived = exchange(outgoing)
     rows, cols = make_lists(dip_inline.reshape(-1), dip_cross.reshape(-1))
     bins = arrived[:, 64, :8].astype(jnp.int32).reshape(-1)
     fold = jnp.sum(

time: 205 us -> 239 us (1.17)
  Pallas kernels: 95.1 us -> 184 us
  blocking collectives: 65.6 us -> 0 us
  starting transfers between devices: 19 us -> 30.4 us
    pallas_call x0 -> x1, Pallas kernels: none -> 94.3 us  [exchange(): pl.pallas_call(exchange_kernel, out_shape=jax.ShapeDtypeStruct((DEV, PAY,...]
    all_to_all x1 -> x0, blocking collectives: 65.6 us -> none  [on_device(): lax.all_to_all(outgoing, ('inline', 'crosslin'), split_axis=0, concat_axi...]
    ppermute x3, starting transfers between devices: 7.87 us -> 22.3 us  [beside(): hi = lax.ppermute(head, axis, [(i + 1, i) for i in range(ends)])]
    pallas_call x2, Pallas kernels: 18.2 us -> 13.7 us  [outer(): pl.pallas_call(functools.partial(outer_kernel, along_rows), out_shape=(EX...]
    ppermute x3, starting transfers between devices: 11.1 us -> 8.07 us  [beside(): lo = lax.ppermute(tail, axis, [(i, i + 1) for i in range(ends)])]
    unnamed x25 -> x27, local copies, waits for them, and re-layouts: 10.2 us -> 7.87 us
  transfers between devices with their start and end apart: 6 -> 6, of which waited for: 2 -> 2; matrix products, arithmetic and copies ran while one was open for 1% -> 1% of each run, Pallas kernels for 26% -> 22%
where the time goes in v4:
time: 239 us; the launch traced here: 237 us
  Pallas kernels  184 us (77%)
  starting transfers between devices  30.4 us (13%)
  waiting for transfers between devices  10.2 us (4%)
  local copies, waits for them, and re-layouts  9.97 us (4%)
    pallas_call x1, Pallas kernels, exchange(): pl.pallas_call(exchange_kernel, out_shape=jax.ShapeDtypeStruct((DEV, PAY,...  94.3 us
    pallas_call x2, Pallas kernels, inner(): pl.pallas_call(functools.partial(inner_kernel, along_rows), out_shape=(EX...  24.1 us
    ppermute x3, starting transfers between devices, beside(): hi = lax.ppermute(head, axis, [(i + 1, i) for i in range(ends)])  22.3 us
    pallas_call x1, Pallas kernels, inner_last(): pl.pallas_call(inner_last_kernel, out_shape=(EXT, ACC, RESULT), in_specs=...  14.9 us
    pallas_call x2, Pallas kernels, outer(): pl.pallas_call(functools.partial(outer_kernel, along_rows), out_shape=(EX...  13.7 us
    pallas_call x1, Pallas kernels, make_lists(): pl.pallas_call(both_lists_kernel, out_shape=(table, count, table, count),...  12.2 us
    pallas_call x1, Pallas kernels, last(): pl.pallas_call(last_kernel, out_shape=(EXT, ACC, RESULT), in_specs=[SM, S...  9.57 us
    ppermute x3, starting transfers between devices, beside(): lo = lax.ppermute(tail, axis, [(i, i + 1) for i in range(ends)])  8.07 us
  transfers between devices with their start and end apart: 6, of which 2 were waited for; matrix products, arithmetic and copies ran while one was open for 1% of the time, Pallas kernels for 22%

profile of v4, /device:TPU:56, one launch (start us, length us, event | category | flops | bytes accessed | tf_op | source)
XLA Modules:
  0.0 236.8 jit_solution(13763109832427475589)
XLA Ops:
  0.0 0.8 copy.16
  0.8 0.7 reshape.29.bins
  1.5 7.2 %pack.1.x = f32[128,72,128]{2,1,0:T(8,128)} custom-call(s32[128]{0:T(128)} %bitcast.7, s32[512]{0:T(512)} %reshape.29.bins, f32[4096,128]{1,0:T(8,128)} %bitcast.6), custom_call_target="tpu_custom_call" | custom-call | tf_op jit(solution)/shard_map/pack/pallas_call | solution.py:69
  8.7 94.3 %exchange.1.x_hbm = f32[128,72,128]{2,1,0:T(8,128)} custom-call(f32[128,72,128]{2,1,0:T(8,128)} %pack.1.x), custom_call_target="tpu_custom_call" | custom-call | tf_op jit(solution)/shard_map/exchange/pallas_call | solution.py:131
  103.0 1.2 convert_reduce_fusion.1
  104.2 0.1 convert_element_type.15.bins
  104.3 0.5 convert_reduce_fusion
  104.8 0.6 maximum_divide_fusion.scale
  105.4 7.7 %put_bins.1 = (f32[1024,8,128]{2,1,0:T(8,128)}, f32[224,8,128]{2,1,0:T(8,128)}, f32[224,8,128]{2,1,0:T(8,128)}) custom-call(s32[1024]{0:T(1024)} %copy-done.10, f32[1024]{0:T(1024)} %maximum_divide_fusion.scale, f32[128,72,128]{2,1,0:T(8,128)} %exchange.1.x_hbm), custom_call_target="tpu_custom_call" | custom-call | tf_op jit(solution)/shard_map/put_bins/pallas_call | solution.py:241
  113.1 1.9 collective-permute-start
  115.0 16.3 %collective-permute-start.1 = (f32[224,8,128]{2,1,0:T(8,128)}, f32[224,8,128]{2,1,0:T(8,128)S(1)}, u32[]{:S(2)}, u32[]{:S(2)}) collective-permute-start(f32[224,8,128]{2,1,0:T(8,128)} %get-tuple-element.31), channel_id=1, source_target_pairs={{8,0},{16,8},{24,16},{32,24},{40,32},{48,40},{56,48},{64,56},{72,6... | collective-permute-start | bytes 2752520 | tf_op jit(solution)/shard_map/ppermute | solution.py:511
  131.3 0.7 reshape.26.dip_rows
  132.0 0.7 reshape.27.dip_cols
  132.7 12.2 %lists.1 = (s32[5920]{0:T(1024)}, s32[10]{0:T(128)}, s32[5920]{0:T(1024)}, s32[10]{0:T(128)}) custom-call(s32[1024]{0:T(1024)} %reshape.26.dip_rows, s32[1024]{0:T(1024)} %reshape.27.dip_cols), custom_call_target="tpu_custom_call" | custom-call | bytes 25165824 | tf_op jit(solution)/shard_map/lists/pallas_call | solution.py:185
  144.9 0.7 copy-done.2
  145.6 0.6 copy-done.5
  146.2 12.0 %inner_rows.1 = (f32[72000,128]{1,0:T(8,128)S(1)}, f32[1025,8,128]{2,1,0:T(8,128)S(1)}) custom-call(s32[5920]{0:T(1024)S(1)} %copy-done.2, s32[10]{0:T(128)S(1)} %copy-done.5, f32[1024,8,128]{2,1,0:T(8,128)} %get-tuple-element.32.own_hbm), custom_call_target="tpu_custom_call" | custom-call | bytes 50331648 | tf_op jit(solution)/shard_map/inner_rows/pallas_call | solution.py:457
  158.3 0.9 copy-done.8
  159.2 6.7 %outer_rows.1 = (f32[72000,128]{1,0:T(8,128)S(1)}, f32[1025,8,128]{2,1,0:T(8,128)S(1)}, f32[224,8,128]{2,1,0:T(8,128)S(1)}, f32[224,8,128]{2,1,0:T(8,128)S(1)}) custom-call(s32[5920]{0:T(1024)S(1)} %copy-done.2, s32[10]{0:T(128)S(1)} %copy-done.5, f32[224,8,128]{2,1,0:T(8,128)S(1)} %collective-permute-done.lo_hbm, ...), custom_call_target="tpu_custom_call", output_to_operand_aliasing={{0}: (4, {}), {1}: (5, {})} | custom-call | tf_op jit(solution)/shard_map/outer_rows/pallas_call | solution.py:470
  165.9 1.9 copy-done.1
  167.9 1.9 collective-permute-start.2
  169.8 4.1 %collective-permute-start.3 = (f32[224,8,128]{2,1,0:T(8,128)S(1)}, f32[224,8,128]{2,1,0:T(8,128)S(1)}, u32[]{:S(2)}, u32[]{:S(2)}) collective-permute-start(f32[224,8,128]{2,1,0:T(8,128)S(1)} %get-tuple-element.36), channel_id=1, source_target_pairs={{1,0},{2,1},{3,2},{4,3},{5,4},{6,5},{7,6},{9,8},{10,9},{11,10},{12... | collective-permute-start | bytes 2752520 | tf_op jit(solution)/shard_map/ppermute | solution.py:511
  173.9 12.1 %inner_cols.1 = (f32[72000,128]{1,0:T(8,128)S(1)}, f32[1025,8,128]{2,1,0:T(8,128)S(1)}) custom-call(s32[5920]{0:T(1024)S(1)} %copy-done.4, s32[10]{0:T(128)S(1)} %copy-done.7, f32[1025,8,128]{2,1,0:T(8,128)} %copy-done.1), custom_call_target="tpu_custom_call" | custom-call | bytes 50331648 | tf_op jit(solution)/shard_map/inner_cols/pallas_call | solution.py:457
  186.0 0.9 copy-done.9
  187.0 7.0 %outer_cols.1 = (f32[72000,128]{1,0:T(8,128)S(1)}, f32[1025,8,128]{2,1,0:T(8,128)S(1)}, f32[224,8,128]{2,1,0:T(8,128)S(1)}, f32[224,8,128]{2,1,0:T(8,128)S(1)}) custom-call(s32[5920]{0:T(1024)S(1)} %copy-done.4, s32[10]{0:T(128)S(1)} %copy-done.7, f32[224,8,128]{2,1,0:T(8,128)S(1)} %collective-permute-done.2.lo_hbm, ...), custom_call_target="tpu_custom_call", output_to_operand_aliasing={{0}: (4, {}), {1}: (5, {})} | custom-call | tf_op jit(solution)/shard_map/outer_cols/pallas_call | solution.py:470
  193.9 1.9 copy-done
  195.9 4.2 %collective-permute-start.4 = (f32[224,8,128]{2,1,0:T(8,128)S(1)}, f32[224,8,128]{2,1,0:T(8,128)S(1)}, u32[]{:S(2)}, u32[]{:S(2)}) collective-permute-start(f32[224,8,128]{2,1,0:T(8,128)S(1)} %get-tuple-element.40), channel_id=1, source_target_pairs={{0,8},{8,16},{16,24},{24,32},{32,40},{40,48},{48,56},{56,64},{64,7... | collective-permute-start | bytes 2752520 | tf_op jit(solution)/shard_map/ppermute | solution.py:510
  200.1 1.9 collective-permute-start.5
  202.1 14.9 %inner_last.1 = (f32[72000,128]{1,0:T(8,128)S(1)}, f32[1025,8,128]{2,1,0:T(8,128)S(1)}, f32[32,32,1024]{2,1,0:T(8,128)}) custom-call(s32[5920]{0:T(1024)S(1)} %copy-done.3, s32[10]{0:T(128)S(1)} %copy-done.6, f32[1025,8,128]{2,1,0:T(8,128)} %copy-done), custom_call_target="tpu_custom_call" | custom-call | bytes 50331648 | tf_op jit(solution)/shard_map/inner_last/pallas_call | solution.py:483
  217.0 3.8 %collective-permute-done.4.lo_hbm = f32[224,8,128]{2,1,0:T(8,128)S(1)} collective-permute-done((f32[224,8,128]{2,1,0:T(8,128)S(1)}, f32[224,8,128]{2,1,0:T(8,128)S(1)}, u32[]{:S(2)}, u32[]{:S(2)}) %collective-permute-start.4) | collective-permute-done | bytes 917536 | tf_op jit(solution)/shard_map/ppermute | solution.py:510
  220.7 6.4 %collective-permute-done.5.hi_hbm = f32[224,8,128]{2,1,0:T(8,128)S(1)} collective-permute-done((f32[224,8,128]{2,1,0:T(8,128)S(1)}, f32[224,8,128]{2,1,0:T(8,128)S(1)}, u32[]{:S(2)}, u32[]{:S(2)}) %collective-permute-start.5) | collective-permute-done | bytes 917536 | tf_op jit(solution)/shard_map/ppermute | solution.py:511
  227.2 9.6 %last.1 = (f32[72000,128]{1,0:T(8,128)S(1)}, f32[1025,8,128]{2,1,0:T(8,128)S(1)}, f32[32,32,1024]{2,1,0:T(8,128)}) custom-call(s32[5920]{0:T(1024)S(1)} %copy-done.3, s32[10]{0:T(128)S(1)} %copy-done.6, f32[224,8,128]{2,1,0:T(8,128)S(1)} %collective-permute-done.4.lo_hbm, ...), custom_call_target="tpu_custom_call", output_to_operand_aliasing={{0}: (4, {}), {1}: (5, {}), {2}: (6, {})} | custom-call | tf_op jit(solution)/shard_map/last/pallas_call | solution.py:496
  (24 shorter events, 0.1 us)
Async XLA Ops:
  102.9 28.4 %copy-start.11 = (s32[32,32]{1,0:T(8,128)S(1)}, s32[32,32]{1,0:T(8,128)}, u32[]{:S(2)}) copy-start(s32[32,32]{1,0:T(8,128)} %param.8) | copy-start | bytes 12292
  102.9 29.1 %copy-start.12 = (s32[32,32]{1,0:T(8,128)S(1)}, s32[32,32]{1,0:T(8,128)}, u32[]{:S(2)}) copy-start(s32[32,32]{1,0:T(8,128)} %param.9) | copy-start | bytes 12292
  104.3 1.1 copy-start.10
  113.1 45.2 %collective-permute-start = (f32[224,8,128]{2,1,0:T(8,128)}, f32[224,8,128]{2,1,0:T(8,128)S(1)}, u32[]{:S(2)}, u32[]{:S(2)}) collective-permute-start(f32[224,8,128]{2,1,0:T(8,128)} %get-tuple-element.30), channel_id=1, source_target_pairs={{0,8},{8,16},{16,24},{24,32},{32,40},{40,48},{48,56},{56,64},{64,7... | collective-permute-start | bytes 2752520 | tf_op jit(solution)/shard_map/ppermute | solution.py:510
  115.0 43.3 %collective-permute-start.1 = (f32[224,8,128]{2,1,0:T(8,128)}, f32[224,8,128]{2,1,0:T(8,128)S(1)}, u32[]{:S(2)}, u32[]{:S(2)}) collective-permute-start(f32[224,8,128]{2,1,0:T(8,128)} %get-tuple-element.31), channel_id=1, source_target_pairs={{8,0},{16,8},{24,16},{32,24},{40,32},{48,40},{56,48},{64,56},{72,6... | collective-permute-start | bytes 2752520 | tf_op jit(solution)/shard_map/ppermute | solution.py:511
  144.9 0.7 copy-start.2
  145.6 0.6 copy-start.5
  158.3 0.9 copy-start.8
  159.2 14.7 %copy-start.4 = (s32[5920]{0:T(1024)S(1)}, s32[5920]{0:T(1024)}, u32[]{:S(2)}) copy-start(s32[5920]{0:T(1024)} %get-tuple-element.28.table) | copy-start | bytes 71044
  159.2 14.7 %copy-start.7 = (s32[10]{0:T(128)S(1)}, s32[10]{0:T(128)}, u32[]{:S(2)}) copy-start(s32[10]{0:T(128)} %get-tuple-element.29.count) | copy-start | bytes 124
  165.9 1.9 copy-start.1
  167.9 18.1 %collective-permute-start.2 = (f32[224,8,128]{2,1,0:T(8,128)S(1)}, f32[224,8,128]{2,1,0:T(8,128)S(1)}, u32[]{:S(2)}, u32[]{:S(2)}) collective-permute-start(f32[224,8,128]{2,1,0:T(8,128)S(1)} %get-tuple-element.35), channel_id=1, source_target_pairs={{0,1},{1,2},{2,3},{3,4},{4,5},{5,6},{6,7},{8,9},{9,10},{10,11},{11... | collective-permute-start | bytes 2752520 | tf_op jit(solution)/shard_map/ppermute | solution.py:510
  169.8 16.2 %collective-permute-start.3 = (f32[224,8,128]{2,1,0:T(8,128)S(1)}, f32[224,8,128]{2,1,0:T(8,128)S(1)}, u32[]{:S(2)}, u32[]{:S(2)}) collective-permute-start(f32[224,8,128]{2,1,0:T(8,128)S(1)} %get-tuple-element.36), channel_id=1, source_target_pairs={{1,0},{2,1},{3,2},{4,3},{5,4},{6,5},{7,6},{9,8},{10,9},{11,10},{12... | collective-permute-start | bytes 2752520 | tf_op jit(solution)/shard_map/ppermute | solution.py:511
  186.0 0.9 copy-start.9
  186.9 15.1 %copy-start.3 = (s32[5920]{0:T(1024)S(1)}, s32[5920]{0:T(1024)}, u32[]{:S(2)}) copy-start(s32[5920]{0:T(1024)} %get-tuple-element.26.table) | copy-start | bytes 71044
  186.9 15.1 %copy-start.6 = (s32[10]{0:T(128)S(1)}, s32[10]{0:T(128)}, u32[]{:S(2)}) copy-start(s32[10]{0:T(128)} %get-tuple-element.27.count) | copy-start | bytes 124
  193.9 1.9 copy-start
  195.9 24.9 %collective-permute-start.4 = (f32[224,8,128]{2,1,0:T(8,128)S(1)}, f32[224,8,128]{2,1,0:T(8,128)S(1)}, u32[]{:S(2)}, u32[]{:S(2)}) collective-permute-start(f32[224,8,128]{2,1,0:T(8,128)S(1)} %get-tuple-element.40), channel_id=1, source_target_pairs={{0,8},{8,16},{16,24},{24,32},{32,40},{40,48},{48,56},{56,64},{64,7... | collective-permute-start | bytes 2752520 | tf_op jit(solution)/shard_map/ppermute | solution.py:510
  200.1 27.1 %collective-permute-start.5 = (f32[224,8,128]{2,1,0:T(8,128)S(1)}, f32[224,8,128]{2,1,0:T(8,128)S(1)}, u32[]{:S(2)}, u32[]{:S(2)}) collective-permute-start(f32[224,8,128]{2,1,0:T(8,128)S(1)} %get-tuple-element.41), channel_id=1, source_target_pairs={{8,0},{16,8},{24,16},{32,24},{40,32},{48,40},{56,48},{64,56},{72,6... | collective-permute-start | bytes 2752520 | tf_op jit(solution)/shard_map/ppermute | solution.py:511

commit v5 on v3

--- a/solution.py
+++ b/solution.py
@@ -18,7 +18,7 @@
 GROUP = 16
 MORE = 4
 ROOM = 18 * TILE + GROUP
-PAY = 72
+PAY = 65
 HALO = HALF * TILE
 
 VM = pl.BlockSpec(memory_space=pltpu.VMEM)
@@ -50,16 +50,16 @@
         rank = cnt[t]
         cnt[t] = rank + 1
         pltpu.make_async_copy(
-            scr.at[pl.ds(b * 32, 32)], out.at[t, pl.ds(rank * 32, 32)], sem
+            scr.at[pl.ds(b * 32, 32)], out.at[t, pl.ds(rank * 32, 32), 0], sem
         ).start()
         row = brow[t]
         for q in range(4):
-            row = jnp.where(lane == rank * 4 + q, bins[b * 4 + q].astype(jnp.float32), row)
+            row = jnp.where(lane == rank * 4 + q, bins[q, b].astype(jnp.float32), row)
         brow[t] = row
         return 0
 
     lax.fori_loop(0, DEV, place, 0)
-    copy = pltpu.make_async_copy(brow, out.at[:, pl.ds(64, 1)], bsem)
+    copy = pltpu.make_async_copy(brow, out.at[:, 64], bsem)
     copy.start()
     pltpu.make_async_copy(scr, scr, sem).wait()
     copy.wait()
@@ -68,7 +68,7 @@
 def pack(dest, bins, x):
     return pl.pallas_call(
         pack_kernel,
-        out_shape=jax.ShapeDtypeStruct((DEV, PAY, LANE), jnp.float32),
+        out_shape=jax.ShapeDtypeStruct((DEV, PAY, 1, LANE), jnp.float32),
         in_specs=[SM, SM, VM],
         out_specs=HB,
         scratch_shapes=[
@@ -141,7 +141,7 @@
     chunk = DEV // MORE
     copies = [
         pltpu.make_async_copy(
-            x_hbm.at[pl.ds(q * chunk, chunk), pl.ds(0, 64)], x.at[pl.ds(q * chunk, chunk)], sems.at[q]
+            x_hbm.at[pl.ds(q * chunk, chunk), pl.ds(0, 64), 0], x.at[pl.ds(q * chunk, chunk)], sems.at[q]
         )
         for q in range(MORE)
     ]
@@ -191,7 +191,7 @@
             pltpu.SemaphoreType.DMA((MORE,)),
             *[pltpu.VMEM((BINS + 1, SUB, LANE), jnp.float32) for _ in range(4)],
         ],
-        compiler_params=params(),
+        compiler_params=small(58),
         name="put_bins",
     )(bins, scale, x)
 
@@ -320,10 +320,13 @@
 
 
 def outer_kernel(
-    along_rows, table, count, lo_hbm, hi_hbm, ext_in, acc_in, ext, acc, one, two, lo, hi, sems, mat
+    along_rows, table, count, lo_hbm, hi_hbm, ext_in, acc_in,
+    ext, acc, one, two, whole, lo, hi, sems, mat, away,
 ):
     outer_margins(ext, lo_hbm, hi_hbm, lo, hi, sems, mat, along_rows)
     steer(table, count, 1, ext, along_rows, acc)
+    keep = pltpu.make_async_copy(acc.at[pl.ds(0, BINS)], whole, away)
+    keep.start()
     if along_rows:
 
         def cut(r, _):
@@ -336,6 +339,7 @@
     else:
         one[...] = acc[pl.ds(0, HALO)]
         two[...] = acc[pl.ds(BINS - HALO, HALO)]
+    keep.wait()
 
 
 def natural(acc, out_hbm, z, parts, sems, groups):
@@ -372,8 +376,8 @@
 ACC = pltpu.VMEM((BINS + 1, SUB, LANE), jnp.float32)
 
 
-def small():
-    return pltpu.CompilerParams(vmem_limit_bytes=16 << 20)
+def small(mib):
+    return pltpu.CompilerParams(vmem_limit_bytes=mib << 20)
 
 
 OWN = [
@@ -403,23 +407,24 @@
         in_specs=[SM, SM, HB],
         out_specs=(VM, VM),
         scratch_shapes=OWN,
-        compiler_params=small(),
+        compiler_params=small(12),
         cost_estimate=BUSY,
         name="inner_rows" if along_rows else "inner_cols",
     )(*lists, own)
 
 
 def outer(lists, lo, hi, kept, along_rows):
-    return pl.pallas_call(
+    _, _, one, two, whole = pl.pallas_call(
         functools.partial(outer_kernel, along_rows),
-        out_shape=(EXT, ACC, EDGE, EDGE),
+        out_shape=(EXT, ACC, EDGE, EDGE, FULL),
         in_specs=[SM, SM, HB, HB, VM, VM],
-        out_specs=(VM, VM, VM, VM),
-        scratch_shapes=SIDES,
+        out_specs=(VM, VM, VM, VM, HB),
+        scratch_shapes=SIDES + [pltpu.SemaphoreType.DMA],
         input_output_aliases={4: 0, 5: 1},
-        compiler_params=small(),
+        compiler_params=small(12),
         name="outer_rows" if along_rows else "outer_cols",
-    )(*lists, lo, hi, *kept)[1:]
+    )(*lists, lo, hi, *kept)
+    return whole, one, two
 
 
 def inner_last(lists, own):
@@ -429,7 +434,7 @@
         in_specs=[SM, SM, HB],
         out_specs=(VM, VM, HB),
         scratch_shapes=OWN + PARTS,
-        compiler_params=small(),
+        compiler_params=small(12),
         cost_estimate=BUSY,
         name="inner_last",
     )(*lists, own)
@@ -443,7 +448,7 @@
         out_specs=(VM, VM, HB),
         scratch_shapes=SIDES + PARTS,
         input_output_aliases={4: 0, 5: 1, 6: 2},
-        compiler_params=small(),
+        compiler_params=small(12),
         name="last",
     )(*lists, lo, hi, *kept)[2]
 
@@ -457,12 +462,12 @@
 
 def on_device(traces, destination, bin_index, dip_inline, dip_cross):
     x = traces.reshape(DEV, 4, 8, 128).transpose(0, 2, 1, 3).reshape(4096, 128)
-    outgoing = pack(destination.reshape(-1), bin_index.reshape(-1), x)
+    outgoing = pack(destination.reshape(-1), bin_index.T, x)
     arrived = lax.all_to_all(
         outgoing, ("inline", "crosslin"), split_axis=0, concat_axis=0, tiled=True
     )
     rows, cols = make_lists(dip_inline.reshape(-1), dip_cross.reshape(-1))
-    bins = arrived[:, 64, :8].astype(jnp.int32).reshape(-1)
+    bins = arrived[:, 64, 0, :8].astype(jnp.int32).reshape(-1)
     fold = jnp.sum(
         (jnp.arange(BINS, dtype=jnp.int32)[:, None] == bins[None, :]).astype(jnp.float32), axis=1
     )

time: 205 us -> 192 us (0.937)
  local copies, waits for them, and re-layouts: 12.3 us -> 6.59 us
  blocking collectives: 65.6 us -> 61.8 us
    unnamed x25 -> x24, local copies, waits for them, and re-layouts: 10.2 us -> 5.18 us
    all_to_all x1, blocking collectives: 65.6 us -> 61.8 us  [on_device(): lax.all_to_all(outgoing, ('inline', 'crosslin'), split_axis=0, concat_axi...]
  transfers between devices with their start and end apart: 6 -> 6, of which waited for: 2 -> 2; matrix products, arithmetic and copies ran while one was open for 1% -> 1% of each run, Pallas kernels for 26% -> 27%
where the time goes in v5:
time: 192 us; the launch traced here: 191 us
  Pallas kernels  93.4 us (49%)
  blocking collectives  61.8 us (32%)
  starting transfers between devices  19.3 us (10%)
  waiting for transfers between devices  8.5 us (4%)
  local copies, waits for them, and re-layouts  6.59 us (3%)
    all_to_all x1, blocking collectives, on_device(): lax.all_to_all(outgoing, ('inline', 'crosslin'), split_axis=0, concat_axi...  61.8 us
    pallas_call x2, Pallas kernels, inner(): pl.pallas_call(functools.partial(inner_kernel, along_rows), out_shape=(EX...  24.1 us
    pallas_call x2, Pallas kernels, outer(): pl.pallas_call(functools.partial(outer_kernel, along_rows), out_shape=(EX...  17.3 us
    pallas_call x1, Pallas kernels, inner_last(): pl.pallas_call(inner_last_kernel, out_shape=(EXT, ACC, RESULT), in_specs=...  15.1 us
    pallas_call x1, Pallas kernels, make_lists(): pl.pallas_call(both_lists_kernel, out_shape=(table, count, table, count),...  12.2 us
    ppermute x3, starting transfers between devices, beside(): lo = lax.ppermute(tail, axis, [(i, i + 1) for i in range(ends)])  11.8 us
    pallas_call x1, Pallas kernels, last(): pl.pallas_call(last_kernel, out_shape=(EXT, ACC, RESULT), in_specs=[SM, S...  9.57 us
    pallas_call x1, Pallas kernels, put_bins(): pl.pallas_call(bin_kernel, out_shape=(FULL, EDGE, EDGE), in_specs=[SM, SM...  7.67 us
  transfers between devices with their start and end apart: 6, of which 2 were waited for; matrix products, arithmetic and copies ran while one was open for 1% of the time, Pallas kernels for 27%

profile of v5, /device:TPU:56, one launch (start us, length us, event | category | flops | bytes accessed | tf_op | source)
XLA Modules:
  0.0 191.2 jit_solution(866075022442776451)
XLA Ops:
  0.0 7.4 %pack.1 = f32[128,65,1,128]{3,2,1,0:T(1,128)} custom-call(s32[128]{0:T(128)} %bitcast.9, s32[4,128]{1,0:T(4,128)} %bitcast.8, f32[4096,128]{1,0:T(8,128)} %bitcast.7), custom_call_target="tpu_custom_call" | custom-call | tf_op jit(solution)/shard_map/pack/pallas_call | solution.py:69
  7.4 61.8 %all_to_all.5.x_hbm = f32[128,65,1,128]{3,2,1,0:T(1,128)S(1)} all-to-all(f32[128,65,1,128]{3,2,1,0:T(1,128)} %pack.1), channel_id=1, replica_groups=mesh['inline'=16,'crosslin'=8] {'inline','crosslin'}, dimensions={0} | all-to-all | bytes 8519680 | tf_op jit(solution)/shard_map/all_to_all | solution.py:466
  69.2 2.0 %copy-done.6 = f32[128,65,1,128]{3,2,1,0:T(1,128)} copy-done((f32[128,65,1,128]{3,2,1,0:T(1,128)}, f32[128,65,1,128]{3,2,1,0:T(1,128)S(1)}, u32[]{:S(2)}) %copy-start.6) | copy-done | bytes 4259864
  71.1 0.2 fusion
  71.3 0.1 convert_element_type.15.bins
  71.4 0.5 convert_reduce_fusion
  71.9 0.6 maximum_divide_fusion.scale
  72.5 7.7 %put_bins.1 = (f32[1024,8,128]{2,1,0:T(8,128)}, f32[224,8,128]{2,1,0:T(8,128)}, f32[224,8,128]{2,1,0:T(8,128)}) custom-call(s32[1024]{0:T(1024)} %copy-done.11, f32[1024]{0:T(1024)} %maximum_divide_fusion.scale, f32[128,65,1,128]{3,2,1,0:T(1,128)} %copy-done.6), custom_call_target="tpu_custom_call" | custom-call | tf_op jit(solution)/shard_map/put_bins/pallas_call | solution.py:184
  80.2 3.9 %collective-permute-start = (f32[224,8,128]{2,1,0:T(8,128)}, f32[224,8,128]{2,1,0:T(8,128)S(1)}, u32[]{:S(2)}, u32[]{:S(2)}) collective-permute-start(f32[224,8,128]{2,1,0:T(8,128)} %get-tuple-element.30), channel_id=1, source_target_pairs={{0,8},{8,16},{16,24},{24,32},{32,40},{40,48},{48,56},{56,64},{64,7... | collective-permute-start | bytes 2752520 | tf_op jit(solution)/shard_map/ppermute | solution.py:458
  84.1 2.0 %collective-permute-start.1 = (f32[224,8,128]{2,1,0:T(8,128)}, f32[224,8,128]{2,1,0:T(8,128)S(1)}, u32[]{:S(2)}, u32[]{:S(2)}) collective-permute-start(f32[224,8,128]{2,1,0:T(8,128)} %get-tuple-element.31), channel_id=1, source_target_pairs={{8,0},{16,8},{24,16},{32,24},{40,32},{48,40},{56,48},{64,56},{72,6... | collective-permute-start | bytes 2752520 | tf_op jit(solution)/shard_map/ppermute | solution.py:459
  86.1 0.7 reshape.23.dip_rows
  86.7 0.7 reshape.24.dip_cols
  87.4 12.2 %lists.1 = (s32[5920]{0:T(1024)}, s32[10]{0:T(128)}, s32[5920]{0:T(1024)}, s32[10]{0:T(128)}) custom-call(s32[1024]{0:T(1024)} %reshape.23.dip_rows, s32[1024]{0:T(1024)} %reshape.24.dip_cols), custom_call_target="tpu_custom_call" | custom-call | bytes 25165824 | tf_op jit(solution)/shard_map/lists/pallas_call | solution.py:128
  99.6 0.7 copy-done
  100.3 0.6 copy-done.3
  100.9 12.0 %inner_rows.1 = (f32[72000,128]{1,0:T(8,128)S(1)}, f32[1025,8,128]{2,1,0:T(8,128)S(1)}) custom-call(s32[5920]{0:T(1024)S(1)} %copy-done, s32[10]{0:T(128)S(1)} %copy-done.3, f32[1024,8,128]{2,1,0:T(8,128)} %get-tuple-element.32.own_hbm), custom_call_target="tpu_custom_call" | custom-call | bytes 50331648 | tf_op jit(solution)/shard_map/inner_rows/pallas_call | solution.py:404
  113.0 0.0 collective-permute-done.lo_hbm
  113.0 0.9 copy-done.7
  114.0 8.5 %outer_rows.1 = (f32[72000,128]{1,0:T(8,128)S(1)}, f32[1025,8,128]{2,1,0:T(8,128)S(1)}, f32[224,8,128]{2,1,0:T(8,128)S(1)}, f32[224,8,128]{2,1,0:T(8,128)S(1)}, f32[1024,8,128]{2,1,0:T(8,128)}) custom-call(s32[5920]{0:T(1024)S(1)} %copy-done, s32[10]{0:T(128)S(1)} %copy-done.3, ...), custom_call_target="tpu_custom_call", output_to_operand_aliasing={{0}: (4, {}), {1}: (5, {})} | custom-call | tf_op jit(solution)/shard_map/outer_rows/pallas_call | solution.py:417
  122.5 1.9 %collective-permute-start.2 = (f32[224,8,128]{2,1,0:T(8,128)S(1)}, f32[224,8,128]{2,1,0:T(8,128)S(1)}, u32[]{:S(2)}, u32[]{:S(2)}) collective-permute-start(f32[224,8,128]{2,1,0:T(8,128)S(1)} %get-tuple-element.35), channel_id=1, source_target_pairs={{0,1},{1,2},{2,3},{3,4},{4,5},{5,6},{6,7},{8,9},{9,10},{10,11},{11... | collective-permute-start | bytes 2752520 | tf_op jit(solution)/shard_map/ppermute | solution.py:458
  124.4 3.6 %collective-permute-start.3 = (f32[224,8,128]{2,1,0:T(8,128)S(1)}, f32[224,8,128]{2,1,0:T(8,128)S(1)}, u32[]{:S(2)}, u32[]{:S(2)}) collective-permute-start(f32[224,8,128]{2,1,0:T(8,128)S(1)} %get-tuple-element.36), channel_id=1, source_target_pairs={{1,0},{2,1},{3,2},{4,3},{5,4},{6,5},{7,6},{9,8},{10,9},{11,10},{12... | collective-permute-start | bytes 2752520 | tf_op jit(solution)/shard_map/ppermute | solution.py:459
  128.1 12.1 %inner_cols.1 = (f32[72000,128]{1,0:T(8,128)S(1)}, f32[1025,8,128]{2,1,0:T(8,128)S(1)}) custom-call(s32[5920]{0:T(1024)S(1)} %copy-done.2, s32[10]{0:T(128)S(1)} %copy-done.5, f32[1024,8,128]{2,1,0:T(8,128)} %get-tuple-element.37.own_hbm), custom_call_target="tpu_custom_call" | custom-call | bytes 50331648 | tf_op jit(solution)/shard_map/inner_cols/pallas_call | solution.py:404
  140.2 0.0 collective-permute-done.2.lo_hbm
  140.2 0.0 copy-start.8
  140.2 0.9 copy-done.8
  141.1 8.8 %outer_cols.1 = (f32[72000,128]{1,0:T(8,128)S(1)}, f32[1025,8,128]{2,1,0:T(8,128)S(1)}, f32[224,8,128]{2,1,0:T(8,128)S(1)}, f32[224,8,128]{2,1,0:T(8,128)S(1)}, f32[1024,8,128]{2,1,0:T(8,128)}) custom-call(s32[5920]{0:T(1024)S(1)} %copy-done.2, s32[10]{0:T(128)S(1)} %copy-done.5, ...), custom_call_target="tpu_custom_call", output_to_operand_aliasing={{0}: (4, {}), {1}: (5, {})} | custom-call | tf_op jit(solution)/shard_map/outer_cols/pallas_call | solution.py:417
  150.0 6.0 %collective-permute-start.4 = (f32[224,8,128]{2,1,0:T(8,128)S(1)}, f32[224,8,128]{2,1,0:T(8,128)S(1)}, u32[]{:S(2)}, u32[]{:S(2)}) collective-permute-start(f32[224,8,128]{2,1,0:T(8,128)S(1)} %get-tuple-element.40), channel_id=1, source_target_pairs={{0,8},{8,16},{16,24},{24,32},{32,40},{40,48},{48,56},{56,64},{64,7... | collective-permute-start | bytes 2752520 | tf_op jit(solution)/shard_map/ppermute | solution.py:458
  156.0 1.9 %collective-permute-start.5 = (f32[224,8,128]{2,1,0:T(8,128)S(1)}, f32[224,8,128]{2,1,0:T(8,128)S(1)}, u32[]{:S(2)}, u32[]{:S(2)}) collective-permute-start(f32[224,8,128]{2,1,0:T(8,128)S(1)} %get-tuple-element.41), channel_id=1, source_target_pairs={{8,0},{16,8},{24,16},{32,24},{40,32},{48,40},{56,48},{64,56},{72,6... | collective-permute-start | bytes 2752520 | tf_op jit(solution)/shard_map/ppermute | solution.py:459
  157.9 15.1 %inner_last.1 = (f32[72000,128]{1,0:T(8,128)S(1)}, f32[1025,8,128]{2,1,0:T(8,128)S(1)}, f32[32,32,1024]{2,1,0:T(8,128)}) custom-call(s32[5920]{0:T(1024)S(1)} %copy-done.1, s32[10]{0:T(128)S(1)} %copy-done.4, f32[1024,8,128]{2,1,0:T(8,128)} %get-tuple-element.42.own_hbm), custom_call_target="tpu_custom_call" | custom-call | bytes 50331648 | tf_op jit(solution)/shard_map/inner_last/pallas_call | solution.py:431
  173.0 2.3 %collective-permute-done.4.lo_hbm = f32[224,8,128]{2,1,0:T(8,128)S(1)} collective-permute-done((f32[224,8,128]{2,1,0:T(8,128)S(1)}, f32[224,8,128]{2,1,0:T(8,128)S(1)}, u32[]{:S(2)}, u32[]{:S(2)}) %collective-permute-start.4) | collective-permute-done | bytes 917536 | tf_op jit(solution)/shard_map/ppermute | solution.py:458
  175.3 6.2 %collective-permute-done.5.hi_hbm = f32[224,8,128]{2,1,0:T(8,128)S(1)} collective-permute-done((f32[224,8,128]{2,1,0:T(8,128)S(1)}, f32[224,8,128]{2,1,0:T(8,128)S(1)}, u32[]{:S(2)}, u32[]{:S(2)}) %collective-permute-start.5) | collective-permute-done | bytes 917536 | tf_op jit(solution)/shard_map/ppermute | solution.py:459
  181.5 9.6 %last.1 = (f32[72000,128]{1,0:T(8,128)S(1)}, f32[1025,8,128]{2,1,0:T(8,128)S(1)}, f32[32,32,1024]{2,1,0:T(8,128)}) custom-call(s32[5920]{0:T(1024)S(1)} %copy-done.1, s32[10]{0:T(128)S(1)} %copy-done.4, f32[224,8,128]{2,1,0:T(8,128)S(1)} %collective-permute-done.4.lo_hbm, ...), custom_call_target="tpu_custom_call", output_to_operand_aliasing={{0}: (4, {}), {1}: (5, {}), {2}: (6, {})} | custom-call | tf_op jit(solution)/shard_map/last/pallas_call | solution.py:444
  (20 shorter events, 0.0 us)
Async XLA Ops:
  69.2 2.0 %copy-start.6 = (f32[128,65,1,128]{3,2,1,0:T(1,128)}, f32[128,65,1,128]{3,2,1,0:T(1,128)S(1)}, u32[]{:S(2)}) copy-start(f32[128,65,1,128]{3,2,1,0:T(1,128)S(1)} %all_to_all.5.x_hbm) | copy-start | bytes 12779524
  71.1 14.9 %copy-start.9 = (s32[32,32]{1,0:T(8,128)S(1)}, s32[32,32]{1,0:T(8,128)}, u32[]{:S(2)}) copy-start(s32[32,32]{1,0:T(8,128)} %param.8) | copy-start | bytes 12292
  71.1 15.6 %copy-start.10 = (s32[32,32]{1,0:T(8,128)S(1)}, s32[32,32]{1,0:T(8,128)}, u32[]{:S(2)}) copy-start(s32[32,32]{1,0:T(8,128)} %param.9) | copy-start | bytes 12292
  71.4 1.1 copy-start.11
  80.2 32.8 %collective-permute-start = (f32[224,8,128]{2,1,0:T(8,128)}, f32[224,8,128]{2,1,0:T(8,128)S(1)}, u32[]{:S(2)}, u32[]{:S(2)}) collective-permute-start(f32[224,8,128]{2,1,0:T(8,128)} %get-tuple-element.30), channel_id=1, source_target_pairs={{0,8},{8,16},{16,24},{24,32},{32,40},{40,48},{48,56},{56,64},{64,7... | collective-permute-start | bytes 2752520 | tf_op jit(solution)/shard_map/ppermute | solution.py:458
  84.1 28.9 %collective-permute-start.1 = (f32[224,8,128]{2,1,0:T(8,128)}, f32[224,8,128]{2,1,0:T(8,128)S(1)}, u32[]{:S(2)}, u32[]{:S(2)}) collective-permute-start(f32[224,8,128]{2,1,0:T(8,128)} %get-tuple-element.31), channel_id=1, source_target_pairs={{8,0},{16,8},{24,16},{32,24},{40,32},{48,40},{56,48},{64,56},{72,6... | collective-permute-start | bytes 2752520 | tf_op jit(solution)/shard_map/ppermute | solution.py:459
  99.6 0.7 copy-start
  100.3 0.6 copy-start.3
  113.0 0.9 copy-start.7
  114.0 14.1 %copy-start.2 = (s32[5920]{0:T(1024)S(1)}, s32[5920]{0:T(1024)}, u32[]{:S(2)}) copy-start(s32[5920]{0:T(1024)} %get-tuple-element.28.table) | copy-start | bytes 71044
  114.0 14.1 %copy-start.5 = (s32[10]{0:T(128)S(1)}, s32[10]{0:T(128)}, u32[]{:S(2)}) copy-start(s32[10]{0:T(128)} %get-tuple-element.29.count) | copy-start | bytes 124
  122.5 17.7 %collective-permute-start.2 = (f32[224,8,128]{2,1,0:T(8,128)S(1)}, f32[224,8,128]{2,1,0:T(8,128)S(1)}, u32[]{:S(2)}, u32[]{:S(2)}) collective-permute-start(f32[224,8,128]{2,1,0:T(8,128)S(1)} %get-tuple-element.35), channel_id=1, source_target_pairs={{0,1},{1,2},{2,3},{3,4},{4,5},{5,6},{6,7},{8,9},{9,10},{10,11},{11... | collective-permute-start | bytes 2752520 | tf_op jit(solution)/shard_map/ppermute | solution.py:458
  124.4 15.8 %collective-permute-start.3 = (f32[224,8,128]{2,1,0:T(8,128)S(1)}, f32[224,8,128]{2,1,0:T(8,128)S(1)}, u32[]{:S(2)}, u32[]{:S(2)}) collective-permute-start(f32[224,8,128]{2,1,0:T(8,128)S(1)} %get-tuple-element.36), channel_id=1, source_target_pairs={{1,0},{2,1},{3,2},{4,3},{5,4},{6,5},{7,6},{9,8},{10,9},{11,10},{12... | collective-permute-start | bytes 2752520 | tf_op jit(solution)/shard_map/ppermute | solution.py:459
  140.2 0.9 copy-start.8
  141.1 16.8 %copy-start.1 = (s32[5920]{0:T(1024)S(1)}, s32[5920]{0:T(1024)}, u32[]{:S(2)}) copy-start(s32[5920]{0:T(1024)} %get-tuple-element.26.table) | copy-start | bytes 71044
  141.1 16.8 %copy-start.4 = (s32[10]{0:T(128)S(1)}, s32[10]{0:T(128)}, u32[]{:S(2)}) copy-start(s32[10]{0:T(128)} %get-tuple-element.27.count) | copy-start | bytes 124
  150.0 25.3 %collective-permute-start.4 = (f32[224,8,128]{2,1,0:T(8,128)S(1)}, f32[224,8,128]{2,1,0:T(8,128)S(1)}, u32[]{:S(2)}, u32[]{:S(2)}) collective-permute-start(f32[224,8,128]{2,1,0:T(8,128)S(1)} %get-tuple-element.40), channel_id=1, source_target_pairs={{0,8},{8,16},{16,24},{24,32},{32,40},{40,48},{48,56},{56,64},{64,7... | collective-permute-start | bytes 2752520 | tf_op jit(solution)/shard_map/ppermute | solution.py:458
  156.0 25.5 %collective-permute-start.5 = (f32[224,8,128]{2,1,0:T(8,128)S(1)}, f32[224,8,128]{2,1,0:T(8,128)S(1)}, u32[]{:S(2)}, u32[]{:S(2)}) collective-permute-start(f32[224,8,128]{2,1,0:T(8,128)S(1)} %get-tuple-element.41), channel_id=1, source_target_pairs={{8,0},{16,8},{24,16},{32,24},{40,32},{48,40},{56,48},{64,56},{72,6... | collective-permute-start | bytes 2752520 | tf_op jit(solution)/shard_map/ppermute | solution.py:459

commit v6 on v5

--- a/solution.py
+++ b/solution.py
@@ -85,15 +85,15 @@
 
 
 def add_bin(dips, table, count, i, part):
-    at = part * DIPS + dips[i] + DMAX
+    at = dips[i] + (part * DIPS + DMAX)
     n = count[at]
-    table[at * ROOM + n] = i
+    table[n] = i
     count[at] = n + 1
 
 
 def lists_kernel(along_rows, dips, table, count):
     for at in range(2 * DIPS):
-        count[at] = 0
+        count[at] = at * ROOM
     inside = range(HALF, TILE - HALF)
     if along_rows:
         for low, high, part in ((0, HALF, 1), (HALF, TILE - HALF, 0), (TILE - HALF, TILE, 1)):
@@ -102,7 +102,7 @@
                 add_bin(dips, table, count, i, part)
                 return 0
 
-            lax.fori_loop(low * TILE, high * TILE, add, 0, unroll=4)
+            lax.fori_loop(low * TILE, high * TILE, add, 0, unroll=16)
     else:
 
         def row(r, _):
@@ -114,7 +114,8 @@
     for at in range(2 * DIPS):
         n = count[at]
         for u in range(GROUP):
-            table[at * ROOM + n + u] = BINS
+            table[n + u] = BINS
+        count[at] = n - at * ROOM
 
 
 def both_lists_kernel(dip_rows, dip_cols, table_rows, count_rows, table_cols, count_cols):
@@ -137,7 +138,7 @@
     return (table_rows, count_rows), (table_cols, count_cols)
 
 
-def bin_kernel(bins, scale, x_hbm, out, head, tail, x, sems, *sums):
+def bin_kernel(bins, scale, after, x_hbm, out, head, tail, x, sems, *sums):
     chunk = DEV // MORE
     copies = [
         pltpu.make_async_copy(
@@ -180,11 +181,11 @@
 EDGE = jax.ShapeDtypeStruct((HALO, SUB, LANE), jnp.float32)
 
 
-def put_bins(bins, scale, x):
+def put_bins(bins, scale, after, x):
     return pl.pallas_call(
         bin_kernel,
         out_shape=(FULL, EDGE, EDGE),
-        in_specs=[SM, SM, HB],
+        in_specs=[SM, SM, SM, HB],
         out_specs=(VM, VM, VM),
         scratch_shapes=[
             pltpu.VMEM((DEV, 64, LANE), jnp.float32),
@@ -193,7 +194,7 @@
         ],
         compiler_params=small(58),
         name="put_bins",
-    )(bins, scale, x)
+    )(bins, scale, after, x)
 
 
 def shift_matrix():
@@ -246,15 +247,19 @@
     for copy in copies:
         copy.start()
 
-    def row(r, _):
-        first = start_of(r * TILE, along_rows) + shift
-        starts = [pl.multiple_of(first + c * SPAN, 8) for c in range(TILE)]
-        widen(ext, starts, own[pl.ds(r * TILE, TILE)], mat)
+    below = ROW_PITCH if along_rows else WIDE * SPAN
+
+    def two_rows(r, _):
+        first = start_of(r * 2 * TILE, along_rows) + shift
+        starts = [
+            pl.multiple_of(first + p * below + c * SPAN, 8) for p in range(2) for c in range(TILE)
+        ]
+        widen(ext, starts, own[pl.ds(r * 2 * TILE, 2 * TILE)], mat)
         return 0
 
     for q in range(MORE):
         copies[q].wait()
-        lax.fori_loop(q * TILE // MORE, (q + 1) * TILE // MORE, row, 0)
+        lax.fori_loop(q * TILE // MORE // 2, (q + 1) * TILE // MORE // 2, two_rows, 0)
 
 
 def outer_margins(ext, lo_hbm, hi_hbm, lo, hi, sems, mat, along_rows):
@@ -471,7 +476,7 @@
     fold = jnp.sum(
         (jnp.arange(BINS, dtype=jnp.int32)[:, None] == bins[None, :]).astype(jnp.float32), axis=1
     )
-    stacked, head, tail = put_bins(bins, 1.0 / jnp.maximum(fold, 1.0), arrived)
+    stacked, head, tail = put_bins(bins, 1.0 / jnp.maximum(fold, 1.0), rows[1], arrived)
     lo, hi = beside(head, tail, "inline")
     kept = inner(rows, stacked, True)
     first, left, right = outer(rows, lo, hi, kept, True)

time: 192 us -> 182 us (0.948)
  blocking collectives: 61.8 us -> 0 us
  waiting for transfers between devices: 8.5 us -> 61 us
  starting transfers between devices: 19.3 us -> 28.7 us
  Pallas kernels: 93.4 us -> 86.1 us
  local copies, waits for them, and re-layouts: 6.59 us -> 3.3 us
    all_to_all x1 -> x0, blocking collectives: 61.8 us -> none  [on_device(): lax.all_to_all(outgoing, ('inline', 'crosslin'), split_axis=0, concat_axi...]
    all_to_all x0 -> x1, waiting for transfers between devices: none -> 35.8 us  [on_device(): lax.all_to_all(outgoing, ('inline', 'crosslin'), split_axis=0, concat_axi...]
    ppermute x3, waiting for transfers between devices: 2.27 us -> 14.3 us  [beside(): lo = lax.ppermute(tail, axis, [(i, i + 1) for i in range(ends)])]
    all_to_all x0 -> x1, starting transfers between devices: none -> 10.5 us  [on_device(): lax.all_to_all(outgoing, ('inline', 'crosslin'), split_axis=0, concat_axi...]
    pallas_call x2, Pallas kernels: 24.1 us -> 19.3 us  [inner(): pl.pallas_call(functools.partial(inner_kernel, along_rows), out_shape=(EX...]
    ppermute x3, waiting for transfers between devices: 6.23 us -> 10.9 us  [beside(): hi = lax.ppermute(head, axis, [(i + 1, i) for i in range(ends)])]
    unnamed x24 -> x18, local copies, waits for them, and re-layouts: 5.18 us -> 1.88 us
    ppermute x3, starting transfers between devices: 11.8 us -> 8.69 us  [beside(): lo = lax.ppermute(tail, axis, [(i, i + 1) for i in range(ends)])]
  transfers between devices with their start and end apart: 6 -> 7, of which waited for: 2 -> 6; matrix products, arithmetic and copies ran while one was open for 1% -> 1% of each run, Pallas kernels for 27% -> 24%
where the time goes in v6:
time: 182 us
  Pallas kernels  86.1 us (47%)
  waiting for transfers between devices  61 us (34%)
  starting transfers between devices  28.7 us (16%)
  local copies, waits for them, and re-layouts  3.3 us (2%)
  other arithmetic  2.13 us (1%)
    all_to_all x1, waiting for transfers between devices, on_device(): lax.all_to_all(outgoing, ('inline', 'crosslin'), split_axis=0, concat_axi...  35.8 us
    pallas_call x2, Pallas kernels, inner(): pl.pallas_call(functools.partial(inner_kernel, along_rows), out_shape=(EX...  19.3 us
    pallas_call x2, Pallas kernels, outer(): pl.pallas_call(functools.partial(outer_kernel, along_rows), out_shape=(EX...  17.3 us
    ppermute x3, waiting for transfers between devices, beside(): lo = lax.ppermute(tail, axis, [(i, i + 1) for i in range(ends)])  14.3 us
    pallas_call x1, Pallas kernels, inner_last(): pl.pallas_call(inner_last_kernel, out_shape=(EXT, ACC, RESULT), in_specs=...  12.7 us
    pallas_call x1, Pallas kernels, make_lists(): pl.pallas_call(both_lists_kernel, out_shape=(table, count, table, count),...  12.3 us
    ppermute x3, waiting for transfers between devices, beside(): hi = lax.ppermute(head, axis, [(i + 1, i) for i in range(ends)])  10.9 us
    all_to_all x1, starting transfers between devices, on_device(): lax.all_to_all(outgoing, ('inline', 'crosslin'), split_axis=0, concat_axi...  10.5 us
  transfers between devices with their start and end apart: 7, of which 6 were waited for; matrix products, arithmetic and copies ran while one was open for 1% of the time, Pallas kernels for 24%

profile of v6, /device:TPU:56, one launch (start us, length us, event | category | flops | bytes accessed | tf_op | source)
XLA Modules:
  0.0 181.5 jit_solution(56244322319276653)
XLA Ops:
  0.0 7.4 %pack.1 = f32[128,65,1,128]{3,2,1,0:T(1,128)} custom-call(s32[128]{0:T(128)} %bitcast.9, s32[4,128]{1,0:T(4,128)} %bitcast.8, f32[4096,128]{1,0:T(8,128)} %bitcast.7), custom_call_target="tpu_custom_call" | custom-call | tf_op jit(solution)/shard_map/pack/pallas_call | solution.py:69
  7.4 0.0 copy-start.7
  7.4 0.0 copy-start.8
  7.4 10.5 %all-to-all-start = ((f32[128,65,1,128]{3,2,1,0:T(1,128)}), f32[128,65,1,128]{3,2,1,0:T(1,128)}, u32[]{:S(2)}, u32[]{:S(2)}) async-start(f32[128,65,1,128]{3,2,1,0:T(1,128)} %pack.1), calls=%async_computation | async-start | bytes 8519680 | tf_op jit(solution)/shard_map/all_to_all | solution.py:471
  17.9 0.7 reshape.23.dip_rows
  18.6 0.7 reshape.24.dip_cols
  19.3 12.3 %lists.1 = (s32[5920]{0:T(1024)}, s32[10]{0:T(128)}, s32[5920]{0:T(1024)}, s32[10]{0:T(128)}) custom-call(s32[1024]{0:T(1024)} %reshape.23.dip_rows, s32[1024]{0:T(1024)} %reshape.24.dip_cols), custom_call_target="tpu_custom_call" | custom-call | bytes 25165824 | tf_op jit(solution)/shard_map/lists/pallas_call | solution.py:129
  31.6 35.8 %all-to-all-done.x_hbm = f32[128,65,1,128]{3,2,1,0:T(1,128)} async-done(((f32[128,65,1,128]{3,2,1,0:T(1,128)}), f32[128,65,1,128]{3,2,1,0:T(1,128)}, u32[]{:S(2)}, u32[]{:S(2)}) %all-to-all-start) | async-done | bytes 4259872 | tf_op jit(solution)/shard_map/all_to_all | solution.py:471
  67.3 1.0 fusion
  68.4 0.1 convert_element_type.15.bins
  68.5 0.5 convert_reduce_fusion
  69.0 0.6 maximum_divide_fusion.scale
  69.6 7.7 %put_bins.1 = (f32[1024,8,128]{2,1,0:T(8,128)}, f32[224,8,128]{2,1,0:T(8,128)}, f32[224,8,128]{2,1,0:T(8,128)}) custom-call(s32[1024]{0:T(1024)} %copy-done.6, f32[1024]{0:T(1024)} %maximum_divide_fusion.scale, s32[10]{0:T(128)} %get-tuple-element.27.after.count, f32[128,65,1,128]{3,2,1,0:T(1,128)} %all-to-all-done.x_hbm), custom_call_target="tpu_custom_call" | custom-call | tf_op jit(solution)/shard_map/put_bins/pallas_call | solution.py:185
  77.3 4.8 %collective-permute-start = (f32[224,8,128]{2,1,0:T(8,128)}, f32[224,8,128]{2,1,0:T(8,128)S(1)}, u32[]{:S(2)}, u32[]{:S(2)}) collective-permute-start(f32[224,8,128]{2,1,0:T(8,128)} %get-tuple-element.30), channel_id=1, source_target_pairs={{0,8},{8,16},{16,24},{24,32},{32,40},{40,48},{48,56},{56,64},{64,7... | collective-permute-start | bytes 2752520 | tf_op jit(solution)/shard_map/ppermute | solution.py:463
  82.1 1.9 %collective-permute-start.1 = (f32[224,8,128]{2,1,0:T(8,128)}, f32[224,8,128]{2,1,0:T(8,128)S(1)}, u32[]{:S(2)}, u32[]{:S(2)}) collective-permute-start(f32[224,8,128]{2,1,0:T(8,128)} %get-tuple-element.31), channel_id=1, source_target_pairs={{8,0},{16,8},{24,16},{32,24},{40,32},{48,40},{56,48},{64,56},{72,6... | collective-permute-start | bytes 2752520 | tf_op jit(solution)/shard_map/ppermute | solution.py:464
  84.1 9.6 %inner_rows.1 = (f32[72000,128]{1,0:T(8,128)S(1)}, f32[1025,8,128]{2,1,0:T(8,128)S(1)}) custom-call(s32[5920]{0:T(1024)S(1)} %copy-done, s32[10]{0:T(128)S(1)} %copy-done.2, f32[1024,8,128]{2,1,0:T(8,128)} %get-tuple-element.32.own_hbm), custom_call_target="tpu_custom_call" | custom-call | bytes 50331648 | tf_op jit(solution)/shard_map/inner_rows/pallas_call | solution.py:409
  93.7 8.0 %collective-permute-done.lo_hbm = f32[224,8,128]{2,1,0:T(8,128)S(1)} collective-permute-done((f32[224,8,128]{2,1,0:T(8,128)}, f32[224,8,128]{2,1,0:T(8,128)S(1)}, u32[]{:S(2)}, u32[]{:S(2)}) %collective-permute-start) | collective-permute-done | bytes 917536 | tf_op jit(solution)/shard_map/ppermute | solution.py:463
  101.7 5.7 %collective-permute-done.1.hi_hbm = f32[224,8,128]{2,1,0:T(8,128)S(1)} collective-permute-done((f32[224,8,128]{2,1,0:T(8,128)}, f32[224,8,128]{2,1,0:T(8,128)S(1)}, u32[]{:S(2)}, u32[]{:S(2)}) %collective-permute-start.1) | collective-permute-done | bytes 917536 | tf_op jit(solution)/shard_map/ppermute | solution.py:464
  107.4 0.9 copy-done.5
  108.4 8.5 %outer_rows.1 = (f32[72000,128]{1,0:T(8,128)S(1)}, f32[1025,8,128]{2,1,0:T(8,128)S(1)}, f32[224,8,128]{2,1,0:T(8,128)S(1)}, f32[224,8,128]{2,1,0:T(8,128)S(1)}, f32[1024,8,128]{2,1,0:T(8,128)}) custom-call(s32[5920]{0:T(1024)S(1)} %copy-done, s32[10]{0:T(128)S(1)} %copy-done.2, ...), custom_call_target="tpu_custom_call", output_to_operand_aliasing={{0}: (4, {}), {1}: (5, {})} | custom-call | tf_op jit(solution)/shard_map/outer_rows/pallas_call | solution.py:422
  116.8 1.9 %collective-permute-start.2 = (f32[224,8,128]{2,1,0:T(8,128)S(1)}, f32[224,8,128]{2,1,0:T(8,128)S(1)}, u32[]{:S(2)}, u32[]{:S(2)}) collective-permute-start(f32[224,8,128]{2,1,0:T(8,128)S(1)} %get-tuple-element.35), channel_id=1, source_target_pairs={{0,1},{1,2},{2,3},{3,4},{4,5},{5,6},{6,7},{8,9},{9,10},{10,11},{11... | collective-permute-start | bytes 2752520 | tf_op jit(solution)/shard_map/ppermute | solution.py:463
  118.7 3.6 %collective-permute-start.3 = (f32[224,8,128]{2,1,0:T(8,128)S(1)}, f32[224,8,128]{2,1,0:T(8,128)S(1)}, u32[]{:S(2)}, u32[]{:S(2)}) collective-permute-start(f32[224,8,128]{2,1,0:T(8,128)S(1)} %get-tuple-element.36), channel_id=1, source_target_pairs={{1,0},{2,1},{3,2},{4,3},{5,4},{6,5},{7,6},{9,8},{10,9},{11,10},{12... | collective-permute-start | bytes 2752520 | tf_op jit(solution)/shard_map/ppermute | solution.py:464
  122.4 9.7 %inner_cols.1 = (f32[72000,128]{1,0:T(8,128)S(1)}, f32[1025,8,128]{2,1,0:T(8,128)S(1)}) custom-call(s32[5920]{0:T(1024)S(1)} %copy-done.1, s32[10]{0:T(128)S(1)} %copy-done.3, f32[1024,8,128]{2,1,0:T(8,128)} %get-tuple-element.37.own_hbm), custom_call_target="tpu_custom_call" | custom-call | bytes 50331648 | tf_op jit(solution)/shard_map/inner_cols/pallas_call | solution.py:409
  132.1 1.2 collective-permute-done.3.hi_hbm
  133.3 0.9 copy-done.4
  134.2 8.8 %outer_cols.1 = (f32[72000,128]{1,0:T(8,128)S(1)}, f32[1025,8,128]{2,1,0:T(8,128)S(1)}, f32[224,8,128]{2,1,0:T(8,128)S(1)}, f32[224,8,128]{2,1,0:T(8,128)S(1)}, f32[1024,8,128]{2,1,0:T(8,128)}) custom-call(s32[5920]{0:T(1024)S(1)} %copy-done.1, s32[10]{0:T(128)S(1)} %copy-done.3, ...), custom_call_target="tpu_custom_call", output_to_operand_aliasing={{0}: (4, {}), {1}: (5, {})} | custom-call | tf_op jit(solution)/shard_map/outer_cols/pallas_call | solution.py:422
  143.1 1.9 %collective-permute-start.4 = (f32[224,8,128]{2,1,0:T(8,128)S(1)}, f32[224,8,128]{2,1,0:T(8,128)S(1)}, u32[]{:S(2)}, u32[]{:S(2)}) collective-permute-start(f32[224,8,128]{2,1,0:T(8,128)S(1)} %get-tuple-element.40), channel_id=1, source_target_pairs={{0,8},{8,16},{16,24},{24,32},{32,40},{40,48},{48,56},{56,64},{64,7... | collective-permute-start | bytes 2752520 | tf_op jit(solution)/shard_map/ppermute | solution.py:463
  145.0 3.9 %collective-permute-start.5 = (f32[224,8,128]{2,1,0:T(8,128)S(1)}, f32[224,8,128]{2,1,0:T(8,128)S(1)}, u32[]{:S(2)}, u32[]{:S(2)}) collective-permute-start(f32[224,8,128]{2,1,0:T(8,128)S(1)} %get-tuple-element.41), channel_id=1, source_target_pairs={{8,0},{16,8},{24,16},{32,24},{40,32},{48,40},{56,48},{64,56},{72,6... | collective-permute-start | bytes 2752520 | tf_op jit(solution)/shard_map/ppermute | solution.py:464
  148.9 12.7 %inner_last.1 = (f32[72000,128]{1,0:T(8,128)S(1)}, f32[1025,8,128]{2,1,0:T(8,128)S(1)}, f32[32,32,1024]{2,1,0:T(8,128)}) custom-call(s32[5920]{0:T(1024)S(1)} %copy-done, s32[10]{0:T(128)S(1)} %copy-done.2, f32[1024,8,128]{2,1,0:T(8,128)} %get-tuple-element.42.own_hbm), custom_call_target="tpu_custom_call" | custom-call | bytes 50331648 | tf_op jit(solution)/shard_map/inner_last/pallas_call | solution.py:436
  161.6 6.3 %collective-permute-done.4.lo_hbm = f32[224,8,128]{2,1,0:T(8,128)S(1)} collective-permute-done((f32[224,8,128]{2,1,0:T(8,128)S(1)}, f32[224,8,128]{2,1,0:T(8,128)S(1)}, u32[]{:S(2)}, u32[]{:S(2)}) %collective-permute-start.4) | collective-permute-done | bytes 917536 | tf_op jit(solution)/shard_map/ppermute | solution.py:463
  167.8 4.0 %collective-permute-done.5.hi_hbm = f32[224,8,128]{2,1,0:T(8,128)S(1)} collective-permute-done((f32[224,8,128]{2,1,0:T(8,128)S(1)}, f32[224,8,128]{2,1,0:T(8,128)S(1)}, u32[]{:S(2)}, u32[]{:S(2)}) %collective-permute-start.5) | collective-permute-done | bytes 917536 | tf_op jit(solution)/shard_map/ppermute | solution.py:464
  171.9 9.5 %last.1 = (f32[72000,128]{1,0:T(8,128)S(1)}, f32[1025,8,128]{2,1,0:T(8,128)S(1)}, f32[32,32,1024]{2,1,0:T(8,128)}) custom-call(s32[5920]{0:T(1024)S(1)} %copy-done, s32[10]{0:T(128)S(1)} %copy-done.2, f32[224,8,128]{2,1,0:T(8,128)S(1)} %collective-permute-done.4.lo_hbm, ...), custom_call_target="tpu_custom_call", output_to_operand_aliasing={{0}: (4, {}), {1}: (5, {}), {2}: (6, {})} | custom-call | tf_op jit(solution)/shard_map/last/pallas_call | solution.py:449
  (15 shorter events, 0.0 us)
Async XLA Ops:
  7.4 10.5 %copy-start.7 = (s32[32,32]{1,0:T(8,128)S(1)}, s32[32,32]{1,0:T(8,128)}, u32[]{:S(2)}) copy-start(s32[32,32]{1,0:T(8,128)} %param.8) | copy-start | bytes 12292
  7.4 11.2 %copy-start.8 = (s32[32,32]{1,0:T(8,128)S(1)}, s32[32,32]{1,0:T(8,128)}, u32[]{:S(2)}) copy-start(s32[32,32]{1,0:T(8,128)} %param.9) | copy-start | bytes 12292
  7.4 59.9 %all-to-all-start = ((f32[128,65,1,128]{3,2,1,0:T(1,128)}), f32[128,65,1,128]{3,2,1,0:T(1,128)}, u32[]{:S(2)}, u32[]{:S(2)}) async-start(f32[128,65,1,128]{3,2,1,0:T(1,128)} %pack.1), calls=%async_computation | async-start | bytes 8519680 | tf_op jit(solution)/shard_map/all_to_all | solution.py:471
  31.5 52.5 %copy-start = (s32[5920]{0:T(1024)S(1)}, s32[5920]{0:T(1024)}, u32[]{:S(2)}) copy-start(s32[5920]{0:T(1024)} %get-tuple-element.26.table) | copy-start | bytes 71044
  31.6 52.5 %copy-start.2 = (s32[10]{0:T(128)S(1)}, s32[10]{0:T(128)}, u32[]{:S(2)}) copy-start(s32[10]{0:T(128)} %get-tuple-element.27.after.count) | copy-start | bytes 124
  68.5 1.1 copy-start.6
  77.3 24.5 %collective-permute-start = (f32[224,8,128]{2,1,0:T(8,128)}, f32[224,8,128]{2,1,0:T(8,128)S(1)}, u32[]{:S(2)}, u32[]{:S(2)}) collective-permute-start(f32[224,8,128]{2,1,0:T(8,128)} %get-tuple-element.30), channel_id=1, source_target_pairs={{0,8},{8,16},{16,24},{24,32},{32,40},{40,48},{48,56},{56,64},{64,7... | collective-permute-start | bytes 2752520 | tf_op jit(solution)/shard_map/ppermute | solution.py:463
  82.1 25.3 %collective-permute-start.1 = (f32[224,8,128]{2,1,0:T(8,128)}, f32[224,8,128]{2,1,0:T(8,128)S(1)}, u32[]{:S(2)}, u32[]{:S(2)}) collective-permute-start(f32[224,8,128]{2,1,0:T(8,128)} %get-tuple-element.31), channel_id=1, source_target_pairs={{8,0},{16,8},{24,16},{32,24},{40,32},{48,40},{56,48},{64,56},{72,6... | collective-permute-start | bytes 2752520 | tf_op jit(solution)/shard_map/ppermute | solution.py:464
  107.4 0.9 copy-start.5
  108.4 14.0 %copy-start.1 = (s32[5920]{0:T(1024)S(1)}, s32[5920]{0:T(1024)}, u32[]{:S(2)}) copy-start(s32[5920]{0:T(1024)} %get-tuple-element.28.table) | copy-start | bytes 71044
  108.4 14.1 %copy-start.3 = (s32[10]{0:T(128)S(1)}, s32[10]{0:T(128)}, u32[]{:S(2)}) copy-start(s32[10]{0:T(128)} %get-tuple-element.29.count) | copy-start | bytes 124
  116.8 15.3 %collective-permute-start.2 = (f32[224,8,128]{2,1,0:T(8,128)S(1)}, f32[224,8,128]{2,1,0:T(8,128)S(1)}, u32[]{:S(2)}, u32[]{:S(2)}) collective-permute-start(f32[224,8,128]{2,1,0:T(8,128)S(1)} %get-tuple-element.35), channel_id=1, source_target_pairs={{0,1},{1,2},{2,3},{3,4},{4,5},{5,6},{6,7},{8,9},{9,10},{10,11},{11... | collective-permute-start | bytes 2752520 | tf_op jit(solution)/shard_map/ppermute | solution.py:463
  118.7 14.5 %collective-permute-start.3 = (f32[224,8,128]{2,1,0:T(8,128)S(1)}, f32[224,8,128]{2,1,0:T(8,128)S(1)}, u32[]{:S(2)}, u32[]{:S(2)}) collective-permute-start(f32[224,8,128]{2,1,0:T(8,128)S(1)} %get-tuple-element.36), channel_id=1, source_target_pairs={{1,0},{2,1},{3,2},{4,3},{5,4},{6,5},{7,6},{9,8},{10,9},{11,10},{12... | collective-permute-start | bytes 2752520 | tf_op jit(solution)/shard_map/ppermute | solution.py:464
  133.3 0.9 copy-start.4
  143.1 24.8 %collective-permute-start.4 = (f32[224,8,128]{2,1,0:T(8,128)S(1)}, f32[224,8,128]{2,1,0:T(8,128)S(1)}, u32[]{:S(2)}, u32[]{:S(2)}) collective-permute-start(f32[224,8,128]{2,1,0:T(8,128)S(1)} %get-tuple-element.40), channel_id=1, source_target_pairs={{0,8},{8,16},{16,24},{24,32},{32,40},{40,48},{48,56},{56,64},{64,7... | collective-permute-start | bytes 2752520 | tf_op jit(solution)/shard_map/ppermute | solution.py:463
  145.0 26.9 %collective-permute-start.5 = (f32[224,8,128]{2,1,0:T(8,128)S(1)}, f32[224,8,128]{2,1,0:T(8,128)S(1)}, u32[]{:S(2)}, u32[]{:S(2)}) collective-permute-start(f32[224,8,128]{2,1,0:T(8,128)S(1)} %get-tuple-element.41), channel_id=1, source_target_pairs={{8,0},{16,8},{24,16},{32,24},{40,32},{48,40},{56,48},{64,56},{72,6... | collective-permute-start | bytes 2752520 | tf_op jit(solution)/shard_map/ppermute | solution.py:464

commit v7 on v6

--- a/solution.py
+++ b/solution.py
@@ -270,30 +270,36 @@
     for copy in copies:
         copy.start()
     mat[...] = shift_matrix()
-    for side, ref in enumerate((lo, hi)):
-        copies[side].wait()
-        beyond = side * (TILE + HALF)
-        if along_rows:
-
-            def row(r, _):
-                first = (r + beyond) * ROW_PITCH
-                starts = [pl.multiple_of(first + c * SPAN, 8) for c in range(TILE)]
-                widen(ext, starts, ref[pl.ds(r * TILE, TILE)], mat)
-                return 0
-
-            lax.fori_loop(0, HALF, row, 0)
-        else:
-
-            def four_rows(q, _):
-                starts = [
-                    pl.multiple_of(((q * 4 + p) * WIDE + beyond + c) * SPAN, 8)
-                    for p in range(4)
-                    for c in range(HALF)
-                ]
-                widen(ext, starts, ref[pl.ds(q * 4 * HALF, 4 * HALF)], mat)
-                return 0
-
-            lax.fori_loop(0, TILE // 4, four_rows, 0)
+    for copy in copies:
+        copy.wait()
+    far = TILE + HALF
+    if along_rows:
+
+        def row(r, _):
+            starts = [
+                pl.multiple_of((r + beyond) * ROW_PITCH + c * SPAN, 8)
+                for beyond in (0, far)
+                for c in range(TILE)
+            ]
+            here = pl.ds(r * TILE, TILE)
+            widen(ext, starts, jnp.concatenate([lo[here], hi[here]], axis=0), mat)
+            return 0
+
+        lax.fori_loop(0, HALF, row, 0)
+    else:
+
+        def four_rows(q, _):
+            starts = [
+                pl.multiple_of(((q * 4 + p) * WIDE + beyond + c) * SPAN, 8)
+                for beyond in (0, far)
+                for p in range(4)
+                for c in range(HALF)
+            ]
+            here = pl.ds(q * 4 * HALF, 4 * HALF)
+            widen(ext, starts, jnp.concatenate([lo[here], hi[here]], axis=0), mat)
+            return 0
+
+        lax.fori_loop(0, TILE // 4, four_rows, 0)
 
 
 def steer(table, count, part, ext, along_rows, acc):

time: 182 us -> 181 us (level)
  no operation moved by 1% of the time
where the time goes in v7:
time: 181 us; the launch traced here: 180 us
  Pallas kernels  84.9 us (47%)
  waiting for transfers between devices  61 us (34%)
  starting transfers between devices  28.7 us (16%)
  local copies, waits for them, and re-layouts  3.3 us (2%)
  other arithmetic  2.13 us (1%)
    all_to_all x1, waiting for transfers between devices, on_device(): lax.all_to_all(outgoing, ('inline', 'crosslin'), split_axis=0, concat_axi...  35.8 us
    pallas_call x2, Pallas kernels, inner(): pl.pallas_call(functools.partial(inner_kernel, along_rows), out_shape=(EX...  19.3 us
    pallas_call x2, Pallas kernels, outer(): pl.pallas_call(functools.partial(outer_kernel, along_rows), out_shape=(EX...  17.2 us
    ppermute x3, waiting for transfers between devices, beside(): lo = lax.ppermute(tail, axis, [(i, i + 1) for i in range(ends)])  14.3 us
    pallas_call x1, Pallas kernels, inner_last(): pl.pallas_call(inner_last_kernel, out_shape=(EXT, ACC, RESULT), in_specs=...  12.6 us
    pallas_call x1, Pallas kernels, make_lists(): pl.pallas_call(both_lists_kernel, out_shape=(table, count, table, count),...  12.3 us
    ppermute x3, waiting for transfers between devices, beside(): hi = lax.ppermute(head, axis, [(i + 1, i) for i in range(ends)])  10.9 us
    all_to_all x1, starting transfers between devices, on_device(): lax.all_to_all(outgoing, ('inline', 'crosslin'), split_axis=0, concat_axi...  10.5 us
  transfers between devices with their start and end apart: 7, of which 6 were waited for; matrix products, arithmetic and copies ran while one was open for 1% of the time, Pallas kernels for 24%

profile of v7, /device:TPU:56, one launch (start us, length us, event | category | flops | bytes accessed | tf_op | source)
XLA Modules:
  0.0 180.4 jit_solution(5411601103863881077)
XLA Ops:
  0.0 7.4 %pack.1 = f32[128,65,1,128]{3,2,1,0:T(1,128)} custom-call(s32[128]{0:T(128)} %bitcast.9, s32[4,128]{1,0:T(4,128)} %bitcast.8, f32[4096,128]{1,0:T(8,128)} %bitcast.7), custom_call_target="tpu_custom_call" | custom-call | tf_op jit(solution)/shard_map/pack/pallas_call | solution.py:69
  7.4 0.0 copy-start.7
  7.4 0.0 copy-start.8
  7.4 10.5 %all-to-all-start = ((f32[128,65,1,128]{3,2,1,0:T(1,128)}), f32[128,65,1,128]{3,2,1,0:T(1,128)}, u32[]{:S(2)}, u32[]{:S(2)}) async-start(f32[128,65,1,128]{3,2,1,0:T(1,128)} %pack.1), calls=%async_computation | async-start | bytes 8519680 | tf_op jit(solution)/shard_map/all_to_all | solution.py:477
  17.9 0.7 reshape.23.dip_rows
  18.6 0.7 reshape.24.dip_cols
  19.3 12.3 %lists.1 = (s32[5920]{0:T(1024)}, s32[10]{0:T(128)}, s32[5920]{0:T(1024)}, s32[10]{0:T(128)}) custom-call(s32[1024]{0:T(1024)} %reshape.23.dip_rows, s32[1024]{0:T(1024)} %reshape.24.dip_cols), custom_call_target="tpu_custom_call" | custom-call | bytes 25165824 | tf_op jit(solution)/shard_map/lists/pallas_call | solution.py:129
  31.6 35.8 %all-to-all-done.x_hbm = f32[128,65,1,128]{3,2,1,0:T(1,128)} async-done(((f32[128,65,1,128]{3,2,1,0:T(1,128)}), f32[128,65,1,128]{3,2,1,0:T(1,128)}, u32[]{:S(2)}, u32[]{:S(2)}) %all-to-all-start) | async-done | bytes 4259872 | tf_op jit(solution)/shard_map/all_to_all | solution.py:477
  67.3 1.0 fusion
  68.4 0.1 convert_element_type.15.bins
  68.5 0.5 convert_reduce_fusion
  69.0 0.6 maximum_divide_fusion.scale
  69.6 7.7 %put_bins.1 = (f32[1024,8,128]{2,1,0:T(8,128)}, f32[224,8,128]{2,1,0:T(8,128)}, f32[224,8,128]{2,1,0:T(8,128)}) custom-call(s32[1024]{0:T(1024)} %copy-done.6, f32[1024]{0:T(1024)} %maximum_divide_fusion.scale, s32[10]{0:T(128)} %get-tuple-element.27.after.count, f32[128,65,1,128]{3,2,1,0:T(1,128)} %all-to-all-done.x_hbm), custom_call_target="tpu_custom_call" | custom-call | tf_op jit(solution)/shard_map/put_bins/pallas_call | solution.py:185
  77.3 4.8 %collective-permute-start = (f32[224,8,128]{2,1,0:T(8,128)}, f32[224,8,128]{2,1,0:T(8,128)S(1)}, u32[]{:S(2)}, u32[]{:S(2)}) collective-permute-start(f32[224,8,128]{2,1,0:T(8,128)} %get-tuple-element.30), channel_id=1, source_target_pairs={{0,8},{8,16},{16,24},{24,32},{32,40},{40,48},{48,56},{56,64},{64,7... | collective-permute-start | bytes 2752520 | tf_op jit(solution)/shard_map/ppermute | solution.py:469
  82.1 1.9 %collective-permute-start.1 = (f32[224,8,128]{2,1,0:T(8,128)}, f32[224,8,128]{2,1,0:T(8,128)S(1)}, u32[]{:S(2)}, u32[]{:S(2)}) collective-permute-start(f32[224,8,128]{2,1,0:T(8,128)} %get-tuple-element.31), channel_id=1, source_target_pairs={{8,0},{16,8},{24,16},{32,24},{40,32},{48,40},{56,48},{64,56},{72,6... | collective-permute-start | bytes 2752520 | tf_op jit(solution)/shard_map/ppermute | solution.py:470
  84.1 9.6 %inner_rows.1 = (f32[72000,128]{1,0:T(8,128)S(1)}, f32[1025,8,128]{2,1,0:T(8,128)S(1)}) custom-call(s32[5920]{0:T(1024)S(1)} %copy-done, s32[10]{0:T(128)S(1)} %copy-done.2, f32[1024,8,128]{2,1,0:T(8,128)} %get-tuple-element.32.own_hbm), custom_call_target="tpu_custom_call" | custom-call | bytes 50331648 | tf_op jit(solution)/shard_map/inner_rows/pallas_call | solution.py:415
  93.7 8.1 %collective-permute-done.lo_hbm = f32[224,8,128]{2,1,0:T(8,128)S(1)} collective-permute-done((f32[224,8,128]{2,1,0:T(8,128)}, f32[224,8,128]{2,1,0:T(8,128)S(1)}, u32[]{:S(2)}, u32[]{:S(2)}) %collective-permute-start) | collective-permute-done | bytes 917536 | tf_op jit(solution)/shard_map/ppermute | solution.py:469
  101.7 5.7 %collective-permute-done.1.hi_hbm = f32[224,8,128]{2,1,0:T(8,128)S(1)} collective-permute-done((f32[224,8,128]{2,1,0:T(8,128)}, f32[224,8,128]{2,1,0:T(8,128)S(1)}, u32[]{:S(2)}, u32[]{:S(2)}) %collective-permute-start.1) | collective-permute-done | bytes 917536 | tf_op jit(solution)/shard_map/ppermute | solution.py:470
  107.4 0.9 copy-done.5
  108.4 8.5 %outer_rows.1 = (f32[72000,128]{1,0:T(8,128)S(1)}, f32[1025,8,128]{2,1,0:T(8,128)S(1)}, f32[224,8,128]{2,1,0:T(8,128)S(1)}, f32[224,8,128]{2,1,0:T(8,128)S(1)}, f32[1024,8,128]{2,1,0:T(8,128)}) custom-call(s32[5920]{0:T(1024)S(1)} %copy-done, s32[10]{0:T(128)S(1)} %copy-done.2, ...), custom_call_target="tpu_custom_call", output_to_operand_aliasing={{0}: (4, {}), {1}: (5, {})} | custom-call | tf_op jit(solution)/shard_map/outer_rows/pallas_call | solution.py:428
  116.9 1.9 %collective-permute-start.2 = (f32[224,8,128]{2,1,0:T(8,128)S(1)}, f32[224,8,128]{2,1,0:T(8,128)S(1)}, u32[]{:S(2)}, u32[]{:S(2)}) collective-permute-start(f32[224,8,128]{2,1,0:T(8,128)S(1)} %get-tuple-element.35), channel_id=1, source_target_pairs={{0,1},{1,2},{2,3},{3,4},{4,5},{5,6},{6,7},{8,9},{9,10},{10,11},{11... | collective-permute-start | bytes 2752520 | tf_op jit(solution)/shard_map/ppermute | solution.py:469
  118.8 3.6 %collective-permute-start.3 = (f32[224,8,128]{2,1,0:T(8,128)S(1)}, f32[224,8,128]{2,1,0:T(8,128)S(1)}, u32[]{:S(2)}, u32[]{:S(2)}) collective-permute-start(f32[224,8,128]{2,1,0:T(8,128)S(1)} %get-tuple-element.36), channel_id=1, source_target_pairs={{1,0},{2,1},{3,2},{4,3},{5,4},{6,5},{7,6},{9,8},{10,9},{11,10},{12... | collective-permute-start | bytes 2752520 | tf_op jit(solution)/shard_map/ppermute | solution.py:470
  122.5 9.7 %inner_cols.1 = (f32[72000,128]{1,0:T(8,128)S(1)}, f32[1025,8,128]{2,1,0:T(8,128)S(1)}) custom-call(s32[5920]{0:T(1024)S(1)} %copy-done.1, s32[10]{0:T(128)S(1)} %copy-done.3, f32[1024,8,128]{2,1,0:T(8,128)} %get-tuple-element.37.own_hbm), custom_call_target="tpu_custom_call" | custom-call | bytes 50331648 | tf_op jit(solution)/shard_map/inner_cols/pallas_call | solution.py:415
  132.1 1.2 collective-permute-done.3.hi_hbm
  133.3 0.9 copy-done.4
  134.2 8.8 %outer_cols.1 = (f32[72000,128]{1,0:T(8,128)S(1)}, f32[1025,8,128]{2,1,0:T(8,128)S(1)}, f32[224,8,128]{2,1,0:T(8,128)S(1)}, f32[224,8,128]{2,1,0:T(8,128)S(1)}, f32[1024,8,128]{2,1,0:T(8,128)}) custom-call(s32[5920]{0:T(1024)S(1)} %copy-done.1, s32[10]{0:T(128)S(1)} %copy-done.3, ...), custom_call_target="tpu_custom_call", output_to_operand_aliasing={{0}: (4, {}), {1}: (5, {})} | custom-call | tf_op jit(solution)/shard_map/outer_cols/pallas_call | solution.py:428
  143.0 1.9 %collective-permute-start.4 = (f32[224,8,128]{2,1,0:T(8,128)S(1)}, f32[224,8,128]{2,1,0:T(8,128)S(1)}, u32[]{:S(2)}, u32[]{:S(2)}) collective-permute-start(f32[224,8,128]{2,1,0:T(8,128)S(1)} %get-tuple-element.40), channel_id=1, source_target_pairs={{0,8},{8,16},{16,24},{24,32},{32,40},{40,48},{48,56},{56,64},{64,7... | collective-permute-start | bytes 2752520 | tf_op jit(solution)/shard_map/ppermute | solution.py:469
  144.9 3.9 %collective-permute-start.5 = (f32[224,8,128]{2,1,0:T(8,128)S(1)}, f32[224,8,128]{2,1,0:T(8,128)S(1)}, u32[]{:S(2)}, u32[]{:S(2)}) collective-permute-start(f32[224,8,128]{2,1,0:T(8,128)S(1)} %get-tuple-element.41), channel_id=1, source_target_pairs={{8,0},{16,8},{24,16},{32,24},{40,32},{48,40},{56,48},{64,56},{72,6... | collective-permute-start | bytes 2752520 | tf_op jit(solution)/shard_map/ppermute | solution.py:470
  148.9 12.6 %inner_last.1 = (f32[72000,128]{1,0:T(8,128)S(1)}, f32[1025,8,128]{2,1,0:T(8,128)S(1)}, f32[32,32,1024]{2,1,0:T(8,128)}) custom-call(s32[5920]{0:T(1024)S(1)} %copy-done, s32[10]{0:T(128)S(1)} %copy-done.2, f32[1024,8,128]{2,1,0:T(8,128)} %get-tuple-element.42.own_hbm), custom_call_target="tpu_custom_call" | custom-call | bytes 50331648 | tf_op jit(solution)/shard_map/inner_last/pallas_call | solution.py:442
  161.5 6.3 %collective-permute-done.4.lo_hbm = f32[224,8,128]{2,1,0:T(8,128)S(1)} collective-permute-done((f32[224,8,128]{2,1,0:T(8,128)S(1)}, f32[224,8,128]{2,1,0:T(8,128)S(1)}, u32[]{:S(2)}, u32[]{:S(2)}) %collective-permute-start.4) | collective-permute-done | bytes 917536 | tf_op jit(solution)/shard_map/ppermute | solution.py:469
  167.8 4.0 %collective-permute-done.5.hi_hbm = f32[224,8,128]{2,1,0:T(8,128)S(1)} collective-permute-done((f32[224,8,128]{2,1,0:T(8,128)S(1)}, f32[224,8,128]{2,1,0:T(8,128)S(1)}, u32[]{:S(2)}, u32[]{:S(2)}) %collective-permute-start.5) | collective-permute-done | bytes 917536 | tf_op jit(solution)/shard_map/ppermute | solution.py:470
  171.8 8.4 %last.1 = (f32[72000,128]{1,0:T(8,128)S(1)}, f32[1025,8,128]{2,1,0:T(8,128)S(1)}, f32[32,32,1024]{2,1,0:T(8,128)}) custom-call(s32[5920]{0:T(1024)S(1)} %copy-done, s32[10]{0:T(128)S(1)} %copy-done.2, f32[224,8,128]{2,1,0:T(8,128)S(1)} %collective-permute-done.4.lo_hbm, ...), custom_call_target="tpu_custom_call", output_to_operand_aliasing={{0}: (4, {}), {1}: (5, {}), {2}: (6, {})} | custom-call | tf_op jit(solution)/shard_map/last/pallas_call | solution.py:455
  (15 shorter events, 0.0 us)
Async XLA Ops:
  7.4 10.5 %copy-start.7 = (s32[32,32]{1,0:T(8,128)S(1)}, s32[32,32]{1,0:T(8,128)}, u32[]{:S(2)}) copy-start(s32[32,32]{1,0:T(8,128)} %param.8) | copy-start | bytes 12292
  7.4 11.2 %copy-start.8 = (s32[32,32]{1,0:T(8,128)S(1)}, s32[32,32]{1,0:T(8,128)}, u32[]{:S(2)}) copy-start(s32[32,32]{1,0:T(8,128)} %param.9) | copy-start | bytes 12292
  7.4 59.9 %all-to-all-start = ((f32[128,65,1,128]{3,2,1,0:T(1,128)}), f32[128,65,1,128]{3,2,1,0:T(1,128)}, u32[]{:S(2)}, u32[]{:S(2)}) async-start(f32[128,65,1,128]{3,2,1,0:T(1,128)} %pack.1), calls=%async_computation | async-start | bytes 8519680 | tf_op jit(solution)/shard_map/all_to_all | solution.py:477
  31.6 52.5 %copy-start = (s32[5920]{0:T(1024)S(1)}, s32[5920]{0:T(1024)}, u32[]{:S(2)}) copy-start(s32[5920]{0:T(1024)} %get-tuple-element.26.table) | copy-start | bytes 71044
  31.6 52.5 %copy-start.2 = (s32[10]{0:T(128)S(1)}, s32[10]{0:T(128)}, u32[]{:S(2)}) copy-start(s32[10]{0:T(128)} %get-tuple-element.27.after.count) | copy-start | bytes 124
  68.5 1.1 copy-start.6
  77.3 24.5 %collective-permute-start = (f32[224,8,128]{2,1,0:T(8,128)}, f32[224,8,128]{2,1,0:T(8,128)S(1)}, u32[]{:S(2)}, u32[]{:S(2)}) collective-permute-start(f32[224,8,128]{2,1,0:T(8,128)} %get-tuple-element.30), channel_id=1, source_target_pairs={{0,8},{8,16},{16,24},{24,32},{32,40},{40,48},{48,56},{56,64},{64,7... | collective-permute-start | bytes 2752520 | tf_op jit(solution)/shard_map/ppermute | solution.py:469
  82.1 25.3 %collective-permute-start.1 = (f32[224,8,128]{2,1,0:T(8,128)}, f32[224,8,128]{2,1,0:T(8,128)S(1)}, u32[]{:S(2)}, u32[]{:S(2)}) collective-permute-start(f32[224,8,128]{2,1,0:T(8,128)} %get-tuple-element.31), channel_id=1, source_target_pairs={{8,0},{16,8},{24,16},{32,24},{40,32},{48,40},{56,48},{64,56},{72,6... | collective-permute-start | bytes 2752520 | tf_op jit(solution)/shard_map/ppermute | solution.py:470
  107.4 0.9 copy-start.5
  108.4 14.1 %copy-start.1 = (s32[5920]{0:T(1024)S(1)}, s32[5920]{0:T(1024)}, u32[]{:S(2)}) copy-start(s32[5920]{0:T(1024)} %get-tuple-element.28.table) | copy-start | bytes 71044
  108.4 14.1 %copy-start.3 = (s32[10]{0:T(128)S(1)}, s32[10]{0:T(128)}, u32[]{:S(2)}) copy-start(s32[10]{0:T(128)} %get-tuple-element.29.count) | copy-start | bytes 124
  116.9 15.3 %collective-permute-start.2 = (f32[224,8,128]{2,1,0:T(8,128)S(1)}, f32[224,8,128]{2,1,0:T(8,128)S(1)}, u32[]{:S(2)}, u32[]{:S(2)}) collective-permute-start(f32[224,8,128]{2,1,0:T(8,128)S(1)} %get-tuple-element.35), channel_id=1, source_target_pairs={{0,1},{1,2},{2,3},{3,4},{4,5},{5,6},{6,7},{8,9},{9,10},{10,11},{11... | collective-permute-start | bytes 2752520 | tf_op jit(solution)/shard_map/ppermute | solution.py:469
  118.8 14.5 %collective-permute-start.3 = (f32[224,8,128]{2,1,0:T(8,128)S(1)}, f32[224,8,128]{2,1,0:T(8,128)S(1)}, u32[]{:S(2)}, u32[]{:S(2)}) collective-permute-start(f32[224,8,128]{2,1,0:T(8,128)S(1)} %get-tuple-element.36), channel_id=1, source_target_pairs={{1,0},{2,1},{3,2},{4,3},{5,4},{6,5},{7,6},{9,8},{10,9},{11,10},{12... | collective-permute-start | bytes 2752520 | tf_op jit(solution)/shard_map/ppermute | solution.py:470
  133.3 0.9 copy-start.4
  143.0 24.8 %collective-permute-start.4 = (f32[224,8,128]{2,1,0:T(8,128)S(1)}, f32[224,8,128]{2,1,0:T(8,128)S(1)}, u32[]{:S(2)}, u32[]{:S(2)}) collective-permute-start(f32[224,8,128]{2,1,0:T(8,128)S(1)} %get-tuple-element.40), channel_id=1, source_target_pairs={{0,8},{8,16},{16,24},{24,32},{32,40},{40,48},{48,56},{56,64},{64,7... | collective-permute-start | bytes 2752520 | tf_op jit(solution)/shard_map/ppermute | solution.py:469
  144.9 26.9 %collective-permute-start.5 = (f32[224,8,128]{2,1,0:T(8,128)S(1)}, f32[224,8,128]{2,1,0:T(8,128)S(1)}, u32[]{:S(2)}, u32[]{:S(2)}) collective-permute-start(f32[224,8,128]{2,1,0:T(8,128)S(1)} %get-tuple-element.41), channel_id=1, source_target_pairs={{8,0},{16,8},{24,16},{32,24},{40,32},{48,40},{56,48},{64,56},{72,6... | collective-permute-start | bytes 2752520 | tf_op jit(solution)/shard_map/ppermute | solution.py:470

commit v8 on v7

--- a/solution.py
+++ b/solution.py
@@ -225,7 +225,7 @@
 WIDE = TILE + 2 * HALF
 ROW_PITCH = TILE * SPAN + 8
 COL_PITCH = SPAN
-EXT_ROWS = 72000
+EXT_ROWS = 70000
 
 
 def start_of(b, along_rows):

time: 181 us -> 178 us (0.983)
  local copies, waits for them, and re-layouts: 3.3 us -> 1.45 us
    unnamed x18 -> x14, local copies, waits for them, and re-layouts: 1.88 us -> 0.03 us
  transfers between devices with their start and end apart: 7 -> 7, of which waited for: 6 -> 6; matrix products, arithmetic and copies ran while one was open for 1% -> 1% of each run, Pallas kernels for 24% -> 25%
where the time goes in v8:
time: 178 us; the launch traced here: 177 us
  Pallas kernels  83.1 us (47%)
  waiting for transfers between devices  61.1 us (34%)
  starting transfers between devices  28.7 us (16%)
  other arithmetic  2.12 us (1%)
    all_to_all x1, waiting for transfers between devices, on_device(): lax.all_to_all(outgoing, ('inline', 'crosslin'), split_axis=0, concat_axi...  35.8 us
    pallas_call x2, Pallas kernels, inner(): pl.pallas_call(functools.partial(inner_kernel, along_rows), out_shape=(EX...  19.3 us
    pallas_call x2, Pallas kernels, outer(): pl.pallas_call(functools.partial(outer_kernel, along_rows), out_shape=(EX...  15.4 us
    ppermute x3, waiting for transfers between devices, beside(): lo = lax.ppermute(tail, axis, [(i, i + 1) for i in range(ends)])  14.5 us
    pallas_call x1, Pallas kernels, inner_last(): pl.pallas_call(inner_last_kernel, out_shape=(EXT, ACC, RESULT), in_specs=...  12.6 us
    pallas_call x1, Pallas kernels, make_lists(): pl.pallas_call(both_lists_kernel, out_shape=(table, count, table, count),...  12.3 us
    ppermute x3, waiting for transfers between devices, beside(): hi = lax.ppermute(head, axis, [(i + 1, i) for i in range(ends)])  10.9 us
    all_to_all x1, starting transfers between devices, on_device(): lax.all_to_all(outgoing, ('inline', 'crosslin'), split_axis=0, concat_axi...  10.5 us
  transfers between devices with their start and end apart: 7, of which 6 were waited for; matrix products, arithmetic and copies ran while one was open for 1% of the time, Pallas kernels for 25%

profile of v8, /device:TPU:56, one launch (start us, length us, event | category | flops | bytes accessed | tf_op | source)
XLA Modules:
  0.0 176.8 jit_solution(5784395891821553690)
XLA Ops:
  0.0 7.4 %pack.1 = f32[128,65,1,128]{3,2,1,0:T(1,128)} custom-call(s32[128]{0:T(128)} %bitcast.9, s32[4,128]{1,0:T(4,128)} %bitcast.8, f32[4096,128]{1,0:T(8,128)} %bitcast.7), custom_call_target="tpu_custom_call" | custom-call | tf_op jit(solution)/shard_map/pack/pallas_call | solution.py:69
  7.4 0.0 copy-start.5
  7.4 0.0 copy-start.6
  7.4 10.5 %all-to-all-start = ((f32[128,65,1,128]{3,2,1,0:T(1,128)}), f32[128,65,1,128]{3,2,1,0:T(1,128)}, u32[]{:S(2)}, u32[]{:S(2)}) async-start(f32[128,65,1,128]{3,2,1,0:T(1,128)} %pack.1), calls=%async_computation | async-start | bytes 8519680 | tf_op jit(solution)/shard_map/all_to_all | solution.py:477
  17.9 0.0 copy-done.5
  17.9 0.7 reshape.23.dip_rows
  18.6 0.7 reshape.24.dip_cols
  19.2 12.3 %lists.1 = (s32[5920]{0:T(1024)}, s32[10]{0:T(128)}, s32[5920]{0:T(1024)}, s32[10]{0:T(128)}) custom-call(s32[1024]{0:T(1024)} %reshape.23.dip_rows, s32[1024]{0:T(1024)} %reshape.24.dip_cols), custom_call_target="tpu_custom_call" | custom-call | bytes 25165824 | tf_op jit(solution)/shard_map/lists/pallas_call | solution.py:129
  31.6 35.8 %all-to-all-done.x_hbm = f32[128,65,1,128]{3,2,1,0:T(1,128)} async-done(((f32[128,65,1,128]{3,2,1,0:T(1,128)}), f32[128,65,1,128]{3,2,1,0:T(1,128)}, u32[]{:S(2)}, u32[]{:S(2)}) %all-to-all-start) | async-done | bytes 4259872 | tf_op jit(solution)/shard_map/all_to_all | solution.py:477
  67.3 1.0 fusion
  68.4 0.1 convert_element_type.15.bins
  68.5 0.5 convert_reduce_fusion
  69.0 0.6 maximum_divide_fusion.scale
  69.5 7.7 %put_bins.1 = (f32[1024,8,128]{2,1,0:T(8,128)}, f32[224,8,128]{2,1,0:T(8,128)}, f32[224,8,128]{2,1,0:T(8,128)}) custom-call(s32[1024]{0:T(1024)} %copy-done.4, f32[1024]{0:T(1024)} %maximum_divide_fusion.scale, s32[10]{0:T(128)} %get-tuple-element.27.after.count, f32[128,65,1,128]{3,2,1,0:T(1,128)} %all-to-all-done.x_hbm), custom_call_target="tpu_custom_call" | custom-call | tf_op jit(solution)/shard_map/put_bins/pallas_call | solution.py:185
  77.2 4.8 %collective-permute-start = (f32[224,8,128]{2,1,0:T(8,128)}, f32[224,8,128]{2,1,0:T(8,128)S(1)}, u32[]{:S(2)}, u32[]{:S(2)}) collective-permute-start(f32[224,8,128]{2,1,0:T(8,128)} %get-tuple-element.30), channel_id=1, source_target_pairs={{0,8},{8,16},{16,24},{24,32},{32,40},{40,48},{48,56},{56,64},{64,7... | collective-permute-start | bytes 2752520 | tf_op jit(solution)/shard_map/ppermute | solution.py:469
  82.1 1.9 %collective-permute-start.1 = (f32[224,8,128]{2,1,0:T(8,128)}, f32[224,8,128]{2,1,0:T(8,128)S(1)}, u32[]{:S(2)}, u32[]{:S(2)}) collective-permute-start(f32[224,8,128]{2,1,0:T(8,128)} %get-tuple-element.31), channel_id=1, source_target_pairs={{8,0},{16,8},{24,16},{32,24},{40,32},{48,40},{56,48},{64,56},{72,6... | collective-permute-start | bytes 2752520 | tf_op jit(solution)/shard_map/ppermute | solution.py:470
  84.0 9.6 %inner_rows.1 = (f32[70000,128]{1,0:T(8,128)S(1)}, f32[1025,8,128]{2,1,0:T(8,128)S(1)}) custom-call(s32[5920]{0:T(1024)S(1)} %copy-done, s32[10]{0:T(128)S(1)} %copy-done.2, f32[1024,8,128]{2,1,0:T(8,128)} %get-tuple-element.32.own_hbm), custom_call_target="tpu_custom_call" | custom-call | bytes 50331648 | tf_op jit(solution)/shard_map/inner_rows/pallas_call | solution.py:415
  93.6 8.1 %collective-permute-done.lo_hbm = f32[224,8,128]{2,1,0:T(8,128)S(1)} collective-permute-done((f32[224,8,128]{2,1,0:T(8,128)}, f32[224,8,128]{2,1,0:T(8,128)S(1)}, u32[]{:S(2)}, u32[]{:S(2)}) %collective-permute-start) | collective-permute-done | bytes 917536 | tf_op jit(solution)/shard_map/ppermute | solution.py:469
  101.7 5.7 %collective-permute-done.1.hi_hbm = f32[224,8,128]{2,1,0:T(8,128)S(1)} collective-permute-done((f32[224,8,128]{2,1,0:T(8,128)}, f32[224,8,128]{2,1,0:T(8,128)S(1)}, u32[]{:S(2)}, u32[]{:S(2)}) %collective-permute-start.1) | collective-permute-done | bytes 917536 | tf_op jit(solution)/shard_map/ppermute | solution.py:470
  107.4 7.6 %outer_rows.1 = (f32[70000,128]{1,0:T(8,128)S(1)}, f32[1025,8,128]{2,1,0:T(8,128)S(1)}, f32[224,8,128]{2,1,0:T(8,128)S(1)}, f32[224,8,128]{2,1,0:T(8,128)S(1)}, f32[1024,8,128]{2,1,0:T(8,128)}) custom-call(s32[5920]{0:T(1024)S(1)} %copy-done, s32[10]{0:T(128)S(1)} %copy-done.2, ...), custom_call_target="tpu_custom_call", output_to_operand_aliasing={{0}: (4, {}), {1}: (5, {})} | custom-call | tf_op jit(solution)/shard_map/outer_rows/pallas_call | solution.py:428
  115.0 1.9 %collective-permute-start.2 = (f32[224,8,128]{2,1,0:T(8,128)S(1)}, f32[224,8,128]{2,1,0:T(8,128)S(1)}, u32[]{:S(2)}, u32[]{:S(2)}) collective-permute-start(f32[224,8,128]{2,1,0:T(8,128)S(1)} %get-tuple-element.35), channel_id=1, source_target_pairs={{0,1},{1,2},{2,3},{3,4},{4,5},{5,6},{6,7},{8,9},{9,10},{10,11},{11... | collective-permute-start | bytes 2752520 | tf_op jit(solution)/shard_map/ppermute | solution.py:469
  116.9 3.6 %collective-permute-start.3 = (f32[224,8,128]{2,1,0:T(8,128)S(1)}, f32[224,8,128]{2,1,0:T(8,128)S(1)}, u32[]{:S(2)}, u32[]{:S(2)}) collective-permute-start(f32[224,8,128]{2,1,0:T(8,128)S(1)} %get-tuple-element.36), channel_id=1, source_target_pairs={{1,0},{2,1},{3,2},{4,3},{5,4},{6,5},{7,6},{9,8},{10,9},{11,10},{12... | collective-permute-start | bytes 2752520 | tf_op jit(solution)/shard_map/ppermute | solution.py:470
  120.6 9.7 %inner_cols.1 = (f32[70000,128]{1,0:T(8,128)S(1)}, f32[1025,8,128]{2,1,0:T(8,128)S(1)}) custom-call(s32[5920]{0:T(1024)S(1)} %copy-done.1, s32[10]{0:T(128)S(1)} %copy-done.3, f32[1024,8,128]{2,1,0:T(8,128)} %get-tuple-element.37.own_hbm), custom_call_target="tpu_custom_call" | custom-call | bytes 50331648 | tf_op jit(solution)/shard_map/inner_cols/pallas_call | solution.py:415
  130.3 0.0 collective-permute-done.2.lo_hbm
  130.3 1.1 collective-permute-done.3.hi_hbm
  131.5 7.8 %outer_cols.1 = (f32[70000,128]{1,0:T(8,128)S(1)}, f32[1025,8,128]{2,1,0:T(8,128)S(1)}, f32[224,8,128]{2,1,0:T(8,128)S(1)}, f32[224,8,128]{2,1,0:T(8,128)S(1)}, f32[1024,8,128]{2,1,0:T(8,128)}) custom-call(s32[5920]{0:T(1024)S(1)} %copy-done.1, s32[10]{0:T(128)S(1)} %copy-done.3, ...), custom_call_target="tpu_custom_call", output_to_operand_aliasing={{0}: (4, {}), {1}: (5, {})} | custom-call | tf_op jit(solution)/shard_map/outer_cols/pallas_call | solution.py:428
  139.3 1.9 %collective-permute-start.4 = (f32[224,8,128]{2,1,0:T(8,128)S(1)}, f32[224,8,128]{2,1,0:T(8,128)S(1)}, u32[]{:S(2)}, u32[]{:S(2)}) collective-permute-start(f32[224,8,128]{2,1,0:T(8,128)S(1)} %get-tuple-element.40), channel_id=1, source_target_pairs={{0,8},{8,16},{16,24},{24,32},{32,40},{40,48},{48,56},{56,64},{64,7... | collective-permute-start | bytes 2752520 | tf_op jit(solution)/shard_map/ppermute | solution.py:469
  141.3 3.9 %collective-permute-start.5 = (f32[224,8,128]{2,1,0:T(8,128)S(1)}, f32[224,8,128]{2,1,0:T(8,128)S(1)}, u32[]{:S(2)}, u32[]{:S(2)}) collective-permute-start(f32[224,8,128]{2,1,0:T(8,128)S(1)} %get-tuple-element.41), channel_id=1, source_target_pairs={{8,0},{16,8},{24,16},{32,24},{40,32},{48,40},{56,48},{64,56},{72,6... | collective-permute-start | bytes 2752520 | tf_op jit(solution)/shard_map/ppermute | solution.py:470
  145.2 12.6 %inner_last.1 = (f32[70000,128]{1,0:T(8,128)S(1)}, f32[1025,8,128]{2,1,0:T(8,128)S(1)}, f32[32,32,1024]{2,1,0:T(8,128)}) custom-call(s32[5920]{0:T(1024)S(1)} %copy-done, s32[10]{0:T(128)S(1)} %copy-done.2, f32[1024,8,128]{2,1,0:T(8,128)} %get-tuple-element.42.own_hbm), custom_call_target="tpu_custom_call" | custom-call | bytes 50331648 | tf_op jit(solution)/shard_map/inner_last/pallas_call | solution.py:442
  157.8 6.4 %collective-permute-done.4.lo_hbm = f32[224,8,128]{2,1,0:T(8,128)S(1)} collective-permute-done((f32[224,8,128]{2,1,0:T(8,128)S(1)}, f32[224,8,128]{2,1,0:T(8,128)S(1)}, u32[]{:S(2)}, u32[]{:S(2)}) %collective-permute-start.4) | collective-permute-done | bytes 917536 | tf_op jit(solution)/shard_map/ppermute | solution.py:469
  164.2 4.0 %collective-permute-done.5.hi_hbm = f32[224,8,128]{2,1,0:T(8,128)S(1)} collective-permute-done((f32[224,8,128]{2,1,0:T(8,128)S(1)}, f32[224,8,128]{2,1,0:T(8,128)S(1)}, u32[]{:S(2)}, u32[]{:S(2)}) %collective-permute-start.5) | collective-permute-done | bytes 917536 | tf_op jit(solution)/shard_map/ppermute | solution.py:470
  168.2 8.4 %last.1 = (f32[70000,128]{1,0:T(8,128)S(1)}, f32[1025,8,128]{2,1,0:T(8,128)S(1)}, f32[32,32,1024]{2,1,0:T(8,128)}) custom-call(s32[5920]{0:T(1024)S(1)} %copy-done, s32[10]{0:T(128)S(1)} %copy-done.2, f32[224,8,128]{2,1,0:T(8,128)S(1)} %collective-permute-done.4.lo_hbm, ...), custom_call_target="tpu_custom_call", output_to_operand_aliasing={{0}: (4, {}), {1}: (5, {}), {2}: (6, {})} | custom-call | tf_op jit(solution)/shard_map/last/pallas_call | solution.py:455
  (11 shorter events, 0.0 us)
Async XLA Ops:
  7.4 10.5 %copy-start.5 = (s32[32,32]{1,0:T(8,128)S(1)}, s32[32,32]{1,0:T(8,128)}, u32[]{:S(2)}) copy-start(s32[32,32]{1,0:T(8,128)} %param.8) | copy-start | bytes 12292
  7.4 11.2 %copy-start.6 = (s32[32,32]{1,0:T(8,128)S(1)}, s32[32,32]{1,0:T(8,128)}, u32[]{:S(2)}) copy-start(s32[32,32]{1,0:T(8,128)} %param.9) | copy-start | bytes 12292
  7.4 59.9 %all-to-all-start = ((f32[128,65,1,128]{3,2,1,0:T(1,128)}), f32[128,65,1,128]{3,2,1,0:T(1,128)}, u32[]{:S(2)}, u32[]{:S(2)}) async-start(f32[128,65,1,128]{3,2,1,0:T(1,128)} %pack.1), calls=%async_computation | async-start | bytes 8519680 | tf_op jit(solution)/shard_map/all_to_all | solution.py:477
  31.5 52.5 %copy-start = (s32[5920]{0:T(1024)S(1)}, s32[5920]{0:T(1024)}, u32[]{:S(2)}) copy-start(s32[5920]{0:T(1024)} %get-tuple-element.26.table) | copy-start | bytes 71044
  31.5 52.5 %copy-start.2 = (s32[10]{0:T(128)S(1)}, s32[10]{0:T(128)}, u32[]{:S(2)}) copy-start(s32[10]{0:T(128)} %get-tuple-element.27.after.count) | copy-start | bytes 124
  68.4 1.1 copy-start.4
  77.2 24.5 %collective-permute-start = (f32[224,8,128]{2,1,0:T(8,128)}, f32[224,8,128]{2,1,0:T(8,128)S(1)}, u32[]{:S(2)}, u32[]{:S(2)}) collective-permute-start(f32[224,8,128]{2,1,0:T(8,128)} %get-tuple-element.30), channel_id=1, source_target_pairs={{0,8},{8,16},{16,24},{24,32},{32,40},{40,48},{48,56},{56,64},{64,7... | collective-permute-start | bytes 2752520 | tf_op jit(solution)/shard_map/ppermute | solution.py:469
  82.1 25.3 %collective-permute-start.1 = (f32[224,8,128]{2,1,0:T(8,128)}, f32[224,8,128]{2,1,0:T(8,128)S(1)}, u32[]{:S(2)}, u32[]{:S(2)}) collective-permute-start(f32[224,8,128]{2,1,0:T(8,128)} %get-tuple-element.31), channel_id=1, source_target_pairs={{8,0},{16,8},{24,16},{32,24},{40,32},{48,40},{56,48},{64,56},{72,6... | collective-permute-start | bytes 2752520 | tf_op jit(solution)/shard_map/ppermute | solution.py:470
  107.4 13.2 %copy-start.1 = (s32[5920]{0:T(1024)S(1)}, s32[5920]{0:T(1024)}, u32[]{:S(2)}) copy-start(s32[5920]{0:T(1024)} %get-tuple-element.28.table) | copy-start | bytes 71044
  107.4 13.2 %copy-start.3 = (s32[10]{0:T(128)S(1)}, s32[10]{0:T(128)}, u32[]{:S(2)}) copy-start(s32[10]{0:T(128)} %get-tuple-element.29.count) | copy-start | bytes 124
  115.0 15.3 %collective-permute-start.2 = (f32[224,8,128]{2,1,0:T(8,128)S(1)}, f32[224,8,128]{2,1,0:T(8,128)S(1)}, u32[]{:S(2)}, u32[]{:S(2)}) collective-permute-start(f32[224,8,128]{2,1,0:T(8,128)S(1)} %get-tuple-element.35), channel_id=1, source_target_pairs={{0,1},{1,2},{2,3},{3,4},{4,5},{5,6},{6,7},{8,9},{9,10},{10,11},{11... | collective-permute-start | bytes 2752520 | tf_op jit(solution)/shard_map/ppermute | solution.py:469
  116.9 14.5 %collective-permute-start.3 = (f32[224,8,128]{2,1,0:T(8,128)S(1)}, f32[224,8,128]{2,1,0:T(8,128)S(1)}, u32[]{:S(2)}, u32[]{:S(2)}) collective-permute-start(f32[224,8,128]{2,1,0:T(8,128)S(1)} %get-tuple-element.36), channel_id=1, source_target_pairs={{1,0},{2,1},{3,2},{4,3},{5,4},{6,5},{7,6},{9,8},{10,9},{11,10},{12... | collective-permute-start | bytes 2752520 | tf_op jit(solution)/shard_map/ppermute | solution.py:470
  139.3 24.9 %collective-permute-start.4 = (f32[224,8,128]{2,1,0:T(8,128)S(1)}, f32[224,8,128]{2,1,0:T(8,128)S(1)}, u32[]{:S(2)}, u32[]{:S(2)}) collective-permute-start(f32[224,8,128]{2,1,0:T(8,128)S(1)} %get-tuple-element.40), channel_id=1, source_target_pairs={{0,8},{8,16},{16,24},{24,32},{32,40},{40,48},{48,56},{56,64},{64,7... | collective-permute-start | bytes 2752520 | tf_op jit(solution)/shard_map/ppermute | solution.py:469
  141.3 27.0 %collective-permute-start.5 = (f32[224,8,128]{2,1,0:T(8,128)S(1)}, f32[224,8,128]{2,1,0:T(8,128)S(1)}, u32[]{:S(2)}, u32[]{:S(2)}) collective-permute-start(f32[224,8,128]{2,1,0:T(8,128)S(1)} %get-tuple-element.41), channel_id=1, source_target_pairs={{8,0},{16,8},{24,16},{32,24},{40,32},{48,40},{56,48},{64,56},{72,6... | collective-permute-start | bytes 2752520 | tf_op jit(solution)/shard_map/ppermute | solution.py:470
